TPU v7x, 32 devices: a whole 2x2x4 slice. The times are simulated.
32 devices in a mesh: batch: 8 (over z, y), fsdp: 4 (over x, core).
Axes of the slice: x: 2, y: 2, z: 4, core: 2. Of those that a mesh axis runs over, the one named last changes fastest.
Arguments:
- tokens: bfloat16 [128, 256, 768], P(('batch', 'fsdp')), may hold values from -6 to 6
- cotangent: bfloat16 [128, 256, 768], P(('batch', 'fsdp')), may hold values from -6 to 6
- mask_pos: int32 [128, 128], P(('batch', 'fsdp')), may hold values from 0 to 255, as said below
- mask_count: int32 [128], P(('batch', 'fsdp')), may hold values from 8 to 128, as said below
- w_qkv: float32 [768, 2304], P('fsdp'), may hold values from -0.21875 to 0.21875
- m_qkv: float32 [768, 2304], P(('fsdp', 'batch')), may hold values from -217.2232 to 217.2232
- v_qkv: float32 [768, 2304], P(('fsdp', 'batch')), may hold values from 1474.56 to 23592.96
- w_out: float32 [768, 768], P('fsdp'), may hold values from -0.875 to 0.875
- m_out: float32 [768, 768], P(('fsdp', 'batch')), may hold values from -50.685413 to 50.685413
- v_out: float32 [768, 768], P(('fsdp', 'batch')), may hold values from 80.2816 to 1284.5056
- w_fc1: float32 [768, 3072], P('fsdp'), may hold values from -0.21875 to 0.21875
- m_fc1: float32 [768, 3072], P(('fsdp', 'batch')), may hold values from -86.88928 to 86.88928
- v_fc1: float32 [768, 3072], P(('fsdp', 'batch')), may hold values from 235.9296 to 3774.8735
- w_fc2: float32 [3072, 768], P('fsdp'), may hold values from -0.109375 to 0.109375
- m_fc2: float32 [3072, 768], P(('fsdp', 'batch')), may hold values from -181.01933 to 181.01933
- v_fc2: float32 [3072, 768], P(('fsdp', 'batch')), may hold values from 1024 to 16384
- vectors: float32 [14, 768], P(None, 'fsdp'), may hold values from -1.2 to 1.6
- m_vec: float32 [14, 768], P(None, ('fsdp', 'batch')), may hold values from -217.2232 to 217.2232
- v_vec: float32 [14, 768], P(None, ('fsdp', 'batch')), may hold values from 1474.56 to 23592.96
Outputs:
- layer_out: bfloat16 [128, 256, 768], P(('batch', 'fsdp'))
- grad_tokens: float32 [128, 256, 768], P(('batch', 'fsdp'))
- new_w_qkv: float32 [768, 2304], P('fsdp')
- new_m_qkv: float32 [768, 2304], P(('fsdp', 'batch'))
- new_v_qkv: float32 [768, 2304], P(('fsdp', 'batch'))
- new_w_out: float32 [768, 768], P('fsdp')
- new_m_out: float32 [768, 768], P(('fsdp', 'batch'))
- new_v_out: float32 [768, 768], P(('fsdp', 'batch'))
- new_w_fc1: float32 [768, 3072], P('fsdp')
- new_m_fc1: float32 [768, 3072], P(('fsdp', 'batch'))
- new_v_fc1: float32 [768, 3072], P(('fsdp', 'batch'))
- new_w_fc2: float32 [3072, 768], P('fsdp')
- new_m_fc2: float32 [3072, 768], P(('fsdp', 'batch'))
- new_v_fc2: float32 [3072, 768], P(('fsdp', 'batch'))
- new_vectors: float32 [14, 768], P(None, 'fsdp')
- new_m_vec: float32 [14, 768], P(None, ('fsdp', 'batch'))
- new_v_vec: float32 [14, 768], P(None, ('fsdp', 'batch'))
Inputs may be any that keep to these rules, and one draw needn't show every extreme that they name: `mask_pos`: each row holds 128 different positions of the pair; its first mask_count entries are the masked tokens. `mask_count`: some pair has 128 masked tokens.
All inputs are finite; a program needn't handle non-finite values.
Results may differ from a plain program's by a relative error of at most 0.015.
Values may be sent and summed in bfloat16 or wider, within the bound.
No kernel may reach another device: no remote copies, remote signals or barrier semaphores. Data moves between devices by JAX's collectives and lax.ppermute only.
A program may use at most 192 MiB of HBM per device.

v0:
```python
import math

import jax
import jax.numpy as jnp
from jax import lax
from jax.sharding import PartitionSpec as P

D = 768
HEADS = 12
HDIM = 64
FF = 3072
TEXT = 40
STEP = 3
MAXM = 128


BETA_ONE = 0.5
BETA_TWO = 0.5
EPS_ADAM = 1e-08
STEP_RATES = (0.03, 0.1, 0.03, 0.015, 0.3)
DECAY_RATES = (0.01, 0.01, 0.01, 0.01, 0.0)
INV_ROOT_TWO = 1.0 / math.sqrt(2.0)
INV_ROOT_TWOPI = 1.0 / math.sqrt(2.0 * math.pi)


def dot_first(left_mat, right_mat):
    return lax.dot_general(
        left_mat, right_mat, (((0,), (0,)), ((), ())), preferred_element_type=jnp.float32
    )


def dot_last(left_mat, right_mat):
    return lax.dot_general(
        left_mat, right_mat, (((1,), (1,)), ((), ())), preferred_element_type=jnp.float32
    )


def normalize(hidden):
    row_mean = jnp.mean(hidden, axis=-1, keepdims=True)
    centred = hidden - row_mean
    inv_scale = lax.rsqrt(jnp.mean(centred * centred, axis=-1, keepdims=True) + 1e-06)
    return (centred * inv_scale, inv_scale)


def norm_back(gradient, normed, inv_scale, gain_row):
    scaled = gradient * gain_row
    return inv_scale * (
        scaled
        - jnp.mean(scaled, axis=-1, keepdims=True)
        - normed * jnp.mean(scaled * normed, axis=-1, keepdims=True)
    )


def adamw(weight, gradient, moment_one, moment_two, step_rate, decay_rate):
    new_first = BETA_ONE * moment_one + (1.0 - BETA_ONE) * gradient
    new_second = BETA_TWO * moment_two + (1.0 - BETA_TWO) * gradient * gradient
    correct_one = 1.0 - BETA_ONE**STEP
    correct_two = 1.0 - BETA_TWO**STEP
    update = (
        new_first / correct_one / (jnp.sqrt(new_second / correct_two) + EPS_ADAM)
        + decay_rate * weight
    )
    return (weight - step_rate * update, new_first, new_second)


def shards(
    tokens,
    cotangent,
    mask_pos,
    mask_count,
    w_qkv,
    m_qkv,
    v_qkv,
    w_out,
    m_out,
    v_out,
    w_fc1,
    m_fc1,
    v_fc1,
    w_fc2,
    m_fc2,
    v_fc2,
    vectors,
    m_vec,
    v_vec,
):
    pair_count, length, model_width = tokens.shape
    token_rows = pair_count * length
    fc1_parts = FF // D
    attn_scale = HDIM ** (-0.5)
    shard_qkv = w_qkv.astype(jnp.bfloat16)
    shard_out = w_out.astype(jnp.bfloat16)
    shard_fc1 = w_fc1.astype(jnp.bfloat16)
    shard_fc2 = w_fc2.astype(jnp.bfloat16)
    shard_vec = vectors.astype(jnp.bfloat16)
    qkv_w, out_w, fc1_w, fc2_w, vec_low = (
        lax.all_gather(shard_qkv, "fsdp", axis=0, tiled=True),
        lax.all_gather(shard_out, "fsdp", axis=0, tiled=True),
        lax.all_gather(shard_fc1, "fsdp", axis=0, tiled=True),
        lax.all_gather(shard_fc2, "fsdp", axis=0, tiled=True),
        lax.all_gather(shard_vec, "fsdp", axis=1, tiled=True),
    )
    vector_rows = vec_low.astype(jnp.float32)
    is_image = lax.broadcasted_iota(jnp.int32, (length, 1), 0) >= TEXT
    stream_zero = tokens.astype(jnp.float32) + jnp.where(is_image, vector_rows[1], vector_rows[0])
    stream_zero = stream_zero.reshape(token_rows, model_width)
    normed_one, scale_one = normalize(stream_zero)
    input_one = (normed_one * vector_rows[2] + vector_rows[3]).astype(jnp.bfloat16)
    qkv_bias = jnp.concatenate(
        [vector_rows[4], jnp.zeros((model_width,), jnp.float32), vector_rows[5]]
    )
    qkv_all = (jnp.dot(input_one, qkv_w, preferred_element_type=jnp.float32) + qkv_bias).astype(
        jnp.bfloat16
    )
    head_view = qkv_all.reshape(pair_count, length, 3, HEADS, HDIM)
    queries = head_view[:, :, 0]
    keys_all = head_view[:, :, 1]
    values_all = head_view[:, :, 2]
    scores = (
        jnp.einsum("pqhe,pkhe->pqhk", queries, keys_all, preferred_element_type=jnp.float32)
        * attn_scale
    )
    row_max = jnp.max(scores, axis=-1, keepdims=True)
    log_total = row_max + jnp.log(jnp.sum(jnp.exp(scores - row_max), axis=-1, keepdims=True))
    attn_low = jnp.exp(scores - log_total).astype(jnp.bfloat16)
    mixed_heads = jnp.einsum(
        "pqhk,pkhe->pqhe", attn_low, values_all, preferred_element_type=jnp.float32
    )
    mixed_heads = mixed_heads.astype(jnp.bfloat16).reshape(token_rows, model_width)
    stream_one = (
        stream_zero
        + jnp.dot(mixed_heads, out_w, preferred_element_type=jnp.float32)
        + vector_rows[6]
    )
    normed_two, scale_two = normalize(stream_one)
    input_two = (normed_two * vector_rows[7] + vector_rows[8]).astype(jnp.bfloat16)
    preact = jnp.dot(input_two, fc1_w, preferred_element_type=jnp.float32) + vector_rows[
        9 : 9 + fc1_parts
    ].reshape(FF)
    activated = jax.nn.gelu(preact, approximate=False).astype(jnp.bfloat16)
    result = (
        stream_one
        + jnp.dot(activated, fc2_w, preferred_element_type=jnp.float32)
        + vector_rows[9 + fc1_parts]
    )
    layer_out = result.astype(jnp.bfloat16).reshape(pair_count, length, model_width)
    qkv_w, out_w, fc1_w, fc2_w, vec_low = (
        lax.all_gather(shard_qkv, "fsdp", axis=0, tiled=True),
        lax.all_gather(shard_out, "fsdp", axis=0, tiled=True),
        lax.all_gather(shard_fc1, "fsdp", axis=0, tiled=True),
        lax.all_gather(shard_fc2, "fsdp", axis=0, tiled=True),
        lax.all_gather(shard_vec, "fsdp", axis=1, tiled=True),
    )
    vector_rows = vec_low.astype(jnp.float32)
    slot_index = lax.broadcasted_iota(jnp.int32, (pair_count, MAXM), 1)
    slot_live = slot_index < mask_count[:, None]
    positions = lax.broadcasted_iota(jnp.int32, (pair_count, MAXM, length), 2)
    keep_rows = jnp.any((mask_pos[:, :, None] == positions) & slot_live[:, :, None], axis=1)
    chosen = keep_rows.shape[1]
    picked = pair_count * chosen

    def select(values):
        shaped = values.reshape((pair_count, length) + values.shape[1:])
        return shaped.reshape((picked,) + values.shape[1:])

    def spread_back(values):
        shaped = values.reshape((pair_count, chosen) + values.shape[1:])
        return shaped.reshape((token_rows,) + values.shape[1:])

    grad_out = select(
        cotangent.reshape(token_rows, model_width).astype(jnp.float32)
    ) * keep_rows.reshape(picked, 1).astype(jnp.float32)
    grad_low = grad_out.astype(jnp.bfloat16)
    grad_fc2 = dot_first(select(activated), grad_low)
    bias_fc2 = jnp.sum(grad_out, axis=0)
    grad_act = dot_last(grad_low, fc2_w)
    preact_sel = select(preact)
    gelu_slope = (
        0.5 * (1.0 + lax.erf(preact_sel * INV_ROOT_TWO))
        + preact_sel * jnp.exp(-0.5 * preact_sel * preact_sel) * INV_ROOT_TWOPI
    )
    grad_pre = grad_act * gelu_slope
    bias_fc1 = jnp.sum(grad_pre, axis=0)
    pre_low = grad_pre.astype(jnp.bfloat16)
    grad_fc1 = dot_first(select(input_two), pre_low)
    grad_norm_two = dot_last(pre_low, fc1_w)
    normed_two_sel = select(normed_two)
    gain_two = jnp.sum(grad_norm_two * normed_two_sel, axis=0)
    shift_two = jnp.sum(grad_norm_two, axis=0)
    grad_stream = grad_out + norm_back(
        grad_norm_two, normed_two_sel, select(scale_two), vector_rows[7]
    )
    bias_out = jnp.sum(grad_stream, axis=0)
    stream_low = grad_stream.astype(jnp.bfloat16)
    grad_outw = dot_first(select(mixed_heads), stream_low)
    grad_mixed = (
        dot_last(stream_low, out_w).astype(jnp.bfloat16).reshape(pair_count, chosen, HEADS, HDIM)
    )
    queries_sel = select(queries.reshape(token_rows, HEADS, HDIM)).reshape(
        pair_count, chosen, HEADS, HDIM
    )
    total_sel = select(log_total.reshape(token_rows, HEADS, 1)).reshape(
        pair_count, chosen, HEADS, 1
    )
    scores_again = (
        jnp.einsum("pqhe,pkhe->pqhk", queries_sel, keys_all, preferred_element_type=jnp.float32)
        * attn_scale
    )
    attn_again = jnp.exp(scores_again - total_sel)
    grad_values = jnp.einsum(
        "pqhk,pqhe->pkhe",
        attn_again.astype(jnp.bfloat16),
        grad_mixed,
        preferred_element_type=jnp.float32,
    )
    grad_attn = jnp.einsum(
        "pqhe,pkhe->pqhk", grad_mixed, values_all, preferred_element_type=jnp.float32
    )
    grad_scores = attn_again * (grad_attn - jnp.sum(attn_again * grad_attn, axis=-1, keepdims=True))
    grad_scores = grad_scores.astype(jnp.bfloat16)
    grad_queries = (
        jnp.einsum("pqhk,pkhe->pqhe", grad_scores, keys_all, preferred_element_type=jnp.float32)
        * attn_scale
    )
    grad_keys = (
        jnp.einsum("pqhk,pqhe->pkhe", grad_scores, queries_sel, preferred_element_type=jnp.float32)
        * attn_scale
    )
    grad_queries = spread_back(grad_queries.reshape(picked, model_width))
    grad_values = grad_values.reshape(token_rows, model_width)
    grad_qkv = jnp.concatenate(
        [grad_queries, grad_keys.reshape(token_rows, model_width), grad_values], axis=1
    )
    bias_query = jnp.sum(grad_queries, axis=0)
    bias_value = jnp.sum(grad_values, axis=0)
    qkv_low = grad_qkv.astype(jnp.bfloat16)
    grad_qkvw = dot_first(input_one, qkv_low)
    grad_norm_one = dot_last(qkv_low, qkv_w)
    gain_one = jnp.sum(grad_norm_one * normed_one, axis=0)
    shift_one = jnp.sum(grad_norm_one, axis=0)
    grad_input = spread_back(grad_stream) + norm_back(
        grad_norm_one, normed_one, scale_one, vector_rows[2]
    )
    grad_shaped = grad_input.reshape(pair_count, length, model_width)
    type_text = jnp.sum(jnp.where(is_image, 0.0, grad_shaped), axis=(0, 1))
    type_image = jnp.sum(jnp.where(is_image, grad_shaped, 0.0), axis=(0, 1))
    grad_vec = jnp.concatenate(
        [
            jnp.stack(
                [
                    type_text,
                    type_image,
                    gain_one,
                    shift_one,
                    bias_query,
                    bias_value,
                    bias_out,
                    gain_two,
                    shift_two,
                ]
            ),
            bias_fc1.reshape(fc1_parts, model_width),
            bias_fc2[None, :],
        ],
        axis=0,
    )
    halfway = (
        lax.psum_scatter(
            grad_qkvw.astype(jnp.bfloat16), "fsdp", scatter_dimension=0, tiled=True
        ).astype(jnp.float32),
        lax.psum_scatter(
            grad_outw.astype(jnp.bfloat16), "fsdp", scatter_dimension=0, tiled=True
        ).astype(jnp.float32),
        lax.psum_scatter(
            grad_fc1.astype(jnp.bfloat16), "fsdp", scatter_dimension=0, tiled=True
        ).astype(jnp.float32),
        lax.psum_scatter(
            grad_fc2.astype(jnp.bfloat16), "fsdp", scatter_dimension=0, tiled=True
        ).astype(jnp.float32),
        lax.psum_scatter(
            grad_vec.astype(jnp.bfloat16), "fsdp", scatter_dimension=1, tiled=True
        ).astype(jnp.float32),
    )
    owned = (
        lax.psum_scatter(halfway[0], "batch", scatter_dimension=0, tiled=True),
        lax.psum_scatter(halfway[1], "batch", scatter_dimension=0, tiled=True),
        lax.psum_scatter(halfway[2], "batch", scatter_dimension=0, tiled=True),
        lax.psum_scatter(halfway[3], "batch", scatter_dimension=0, tiled=True),
        lax.psum_scatter(halfway[4], "batch", scatter_dimension=1, tiled=True),
    )
    batch_index = lax.axis_index("batch")
    masters = (w_qkv, w_out, w_fc1, w_fc2, vectors)
    firsts = (m_qkv, m_out, m_fc1, m_fc2, m_vec)
    seconds = (v_qkv, v_out, v_fc1, v_fc2, v_vec)
    alongs = (0, 0, 0, 0, 1)
    updated = []
    for master, gradient, moment_one, moment_two, along, step_rate, decay_rate in zip(
        masters, owned, firsts, seconds, alongs, STEP_RATES, DECAY_RATES
    ):
        slice_rows = gradient.shape[along]
        own_slice = lax.dynamic_slice_in_dim(master, batch_index * slice_rows, slice_rows, along)
        updated.append(adamw(own_slice, gradient, moment_one, moment_two, step_rate, decay_rate))
    new_masters = (
        lax.all_gather(updated[0][0].astype(jnp.bfloat16), "batch", axis=0, tiled=True).astype(
            jnp.float32
        ),
        lax.all_gather(updated[1][0].astype(jnp.bfloat16), "batch", axis=0, tiled=True).astype(
            jnp.float32
        ),
        lax.all_gather(updated[2][0].astype(jnp.bfloat16), "batch", axis=0, tiled=True).astype(
            jnp.float32
        ),
        lax.all_gather(updated[3][0].astype(jnp.bfloat16), "batch", axis=0, tiled=True).astype(
            jnp.float32
        ),
        lax.all_gather(updated[4][0].astype(jnp.bfloat16), "batch", axis=1, tiled=True).astype(
            jnp.float32
        ),
    )
    return (
        layer_out,
        grad_shaped,
        new_masters[0],
        updated[0][1],
        updated[0][2],
        new_masters[1],
        updated[1][1],
        updated[1][2],
        new_masters[2],
        updated[2][1],
        updated[2][2],
        new_masters[3],
        updated[3][1],
        updated[3][2],
        new_masters[4],
        updated[4][1],
        updated[4][2],
    )


def solution(mesh):
    placed = (
        P(("batch", "fsdp"), None, None),
        P(("batch", "fsdp"), None, None),
        P(("batch", "fsdp"), None),
        P(("batch", "fsdp")),
        P("fsdp", None),
        P(("fsdp", "batch"), None),
        P(("fsdp", "batch"), None),
        P("fsdp", None),
        P(("fsdp", "batch"), None),
        P(("fsdp", "batch"), None),
        P("fsdp", None),
        P(("fsdp", "batch"), None),
        P(("fsdp", "batch"), None),
        P("fsdp", None),
        P(("fsdp", "batch"), None),
        P(("fsdp", "batch"), None),
        P(None, "fsdp"),
        P(None, ("fsdp", "batch")),
        P(None, ("fsdp", "batch")),
    )
    return jax.shard_map(
        shards,
        mesh=mesh,
        in_specs=placed,
        out_specs=(
            P(("batch", "fsdp"), None, None),
            P(("batch", "fsdp"), None, None),
            P("fsdp", None),
            P(("fsdp", "batch"), None),
            P(("fsdp", "batch"), None),
            P("fsdp", None),
            P(("fsdp", "batch"), None),
            P(("fsdp", "batch"), None),
            P("fsdp", None),
            P(("fsdp", "batch"), None),
            P(("fsdp", "batch"), None),
            P("fsdp", None),
            P(("fsdp", "batch"), None),
            P(("fsdp", "batch"), None),
            P(None, "fsdp"),
            P(None, ("fsdp", "batch")),
            P(None, ("fsdp", "batch")),
        ),
        check_vma=False,
    )
```

profile of v0, /device:TPU:0, one launch (start us, length us, event | category | flops | bytes accessed | tf_op | source)
XLA Modules:
  0.0 737.7 jit_solution(3257606192598027593)
XLA Ops:
  15.1 6.2 all-gather
  29.4 14.3 %all-gather.9.cloned.1.call-done = bf16[768,2304]{1,0:T(8,128)(2,1)} async-done(((bf16[192,2304]{1,0:T(8,128)(2,1)}), bf16[768,2304]{1,0:T(8,128)(2,1)}) %all-gather.9.cloned.1.call-update) | async-done | bytes 3538960 | tf_op jit(solution)/shard_map/all_gather | solution.py:97
  43.6 8.4 %add_convert_fusion = bf16[1024,2304]{1,0:T(8,128)(2,1)} fusion(bf16[1024,768]{1,0:T(8,128)(2,1)} %add_convert_fusion.3, bf16[768,2304]{1,0:T(8,128)(2,1)} %all-gather.9.cloned.1.call-done, f32[2304]{0:T(1024)S(1)} %pad_maximum_fusion), kind=kOutput, calls=%fused_computation.36 | convolution fusion | flops 3628597248 | bytes 9839616 | tf_op jit(solution)/shard_map/dot_general | solution.py:112
  52.1 6.8 copy.97
  58.9 8.9 %reshape.233 = bf16[4,256,3,12,64]{1,0,4,3,2:T(4,128)(2,1)} reshape(bf16[1024,2304]{0,1:T(8,128)(2,1)} %copy.97) | data formatting | bytes 9437184 | tf_op jit(solution)/shard_map/reshape | solution.py:115
  67.8 3.3 fusion.59
  82.9 3.5 fusion.61
  88.6 14.3 %all-gather.13.cloned.1.call-done = bf16[768,3072]{1,0:T(8,128)(2,1)} async-done(((bf16[192,3072]{1,0:T(8,128)(2,1)}), bf16[768,3072]{1,0:T(8,128)(2,1)}) %all-gather.13.cloned.1.call-update) | async-done | bytes 4718608 | tf_op jit(solution)/shard_map/all_gather | solution.py:99
  102.9 37.7 %fusion.2 = (bf16[1024,3072]{1,0:T(8,128)(2,1)}, f32[1024,3072]{1,0:T(8,128)}) fusion(f32[3072]{0:T(1024)S(1)} %add.230, bf16[768,3072]{1,0:T(8,128)(2,1)} %all-gather.13.cloned.1.call-done, f32[1024,768]{1,0:T(8,128)} %copy-done.12, f32[768]{0:T(1024)S(1)} %get-tuple-element.28, f32[768]{0:T(1024)S(1)} %get-tuple-element.29, f32[1024]{0:T(1024)S(1)} %add_rsqrt_fusion, ...), kind=kOutput, calls=%fused_computation.4 | convolution fusion | flops 5043388416 | bytes 26765312 | tf_op jit(solution)/shard_map/dot_general | solution.py:137
  141.7 11.9 %fusion.62 = (bf16[3072]{0:T(1024)(128)(2,1)S(1)}, bf16[1024,3072]{1,0:T(8,128)(2,1)S(1)}) fusion(f32[1024,3072]{1,0:T(8,128)} %get-tuple-element.69, f32[3072]{0:T(1024)S(1)} %add.230, bf16[1024,768]{1,0:T(8,128)(2,1)S(1)} %copy-done.23, bf16[3072,768]{1,0:T(8,128)(2,1)} %all-gather.15.cloned.1.call-done), kind=kOutput, calls=%fused_computation.151 | convolution fusion | flops 4869583872 | bytes 25184256 | tf_op jit(solution)/shard_map/dot_general | solution.py:33
  156.3 7.8 %convolution_convert_fusion.1 = bf16[768,3072]{1,0:T(8,128)(2,1)} fusion(bf16[1024,3072]{1,0:T(8,128)(2,1)S(1)} %get-tuple-element.79, f32[1024,768]{1,0:T(8,128)S(1)} %copy-done.13, f32[768]{0:T(1024)S(1)} %get-tuple-element.28, f32[768]{0:T(1024)S(1)} %get-tuple-element.29, f32[1024]{0:T(1024)S(1)} %add_rsqrt_fusion, f32[1024]{0:T(1024)S(1)} %broadcast_multiply_fusion.4), kind=kOutput, calls=%fused_computation.39 | convolution fusion | flops 4838129664 | bytes 14170112 | tf_op jit(solution)/shard_map/dot_general | solution.py:27
  164.2 9.7 %convolution_convert_fusion = bf16[3072,768]{1,0:T(8,128)(2,1)} fusion(bf16[1024,3072]{1,0:T(8,128)(2,1)} %get-tuple-element.68, bf16[1024,768]{1,0:T(8,128)(2,1)S(1)} %copy-done.23), kind=kOutput, calls=%fused_computation.38 | convolution fusion | flops 4834197504 | bytes 12582912 | tf_op jit(solution)/shard_map/dot_general | solution.py:27
  174.0 10.4 %multiply_reduce_fusion.1 = (bf16[768]{0:T(1024)(128)(2,1)S(1)}, f32[1024]{0:T(1024)S(1)}, f32[1024]{0:T(1024)S(1)}, bf16[768]{0:T(1024)(128)(2,1)S(1)}, f32[1024,768]{1,0:T(8,128)S(1)}) fusion(f32[1024,768]{1,0:T(8,128)} %copy-done.12, f32[1024]{0:T(1024)S(1)} %add_rsqrt_fusion, f32[1024]{0:T(1024)S(1)} %broadcast_multiply_fusion.4, ...), kind=kOutput, calls=%fused_computation.51 | convolution fusion | flops 4838912000 | bytes 17324032 | tf_op jit(solution)/shard_map/dot_general | solution.py:33
  191.0 8.7 %bitcast_convert_fusion = (bf16[4,256,12,64]{1,3,2,0:T(8,128)(2,1)S(1)}, f32[4,12,64,256]{3,2,1,0:T(8,128)}) fusion(f32[4,12,256,256]{3,2,1,0:T(8,128)} %copy-done, f32[4,256,12]{1,2,0:T(8,128)S(1)} %log_add_fusion, bf16[4,256,12,64]{1,0,3,2:T(4,128)(2,1)S(1)} %reshape.236), kind=kOutput, calls=%fused_computation.42 | convolution fusion | flops 412876800 | bytes 18923520 | tf_op jit(solution)/shard_map/pqhk,pqhe->pkhe/dot_general | solution.py:210
  204.9 9.0 %fusion.8 = (f32[4,256,12]{1,2,0:T(8,128)S(1)}, f32[4,12,256,256]{3,2,1,0:T(8,128)}) fusion(f32[4,12,256,256]{3,2,1,0:T(8,128)} %copy-done, f32[4,256,12]{1,2,0:T(8,128)S(1)} %log_add_fusion, bf16[4,256,12,64]{1,0,3,2:T(4,128)(2,1)S(1)} %reshape.236, bf16[4,256,1,12,64]{1,0,4,3,2:T(4,128)(2,1)S(1)} %copy-done.4), kind=kOutput, calls=%fused_computation.12 | convolution fusion | flops 415223808 | bytes 28409856 | tf_op jit(solution)/shard_map/pqhe,pkhe->pqhk/dot_general | solution.py:216
  214.0 11.4 %fusion.10 = bf16[4,256,12,256]{1,3,2,0:T(8,128)(2,1)S(1)} fusion(f32[4,12,256,256]{3,2,1,0:T(8,128)} %get-tuple-element.72, f32[4,12,256,256]{3,2,1,0:T(8,128)} %copy-done, f32[4,256,12]{1,2,0:T(8,128)S(1)} %get-tuple-element.71, f32[4,256,12]{1,2,0:T(8,128)S(1)} %log_add_fusion), kind=kLoop, calls=%fused_computation.14 | loop fusion | flops 15728640 | bytes 31555584 | tf_op jit(solution)/shard_map/convert_element_type | solution.py:220
  237.3 5.5 convolution_convert_fusion.2
  245.9 16.8 %reduce-scatter.25.cloned.1.call-done = bf16[768,768]{1,0:T(8,128)(2,1)} async-done(((bf16[3072,768]{1,0:T(8,128)(2,1)}), bf16[768,768]{1,0:T(8,128)(2,1)}) %reduce-scatter.25.cloned.1.call-update) | async-done | bytes 1179664 | tf_op jit(solution)/shard_map/reduce_scatter | solution.py:277
  270.8 8.8 %multiply_reduce_fusion.2 = (bf16[768]{0:T(1024)(128)(2,1)S(1)}, f32[1024]{0:T(1024)S(1)}, f32[1024]{0:T(1024)S(1)}, bf16[768]{0:T(1024)(128)(2,1)S(1)}, f32[1024,768]{1,0:T(8,128)S(1)}) fusion(f32[4,256,768]{2,1,0:T(8,128)S(1)} %copy-done.2, f32[1024]{0:T(1024)S(1)} %bitcast.176, f32[1024]{0:T(1024)S(1)} %bitcast.173, f32[768]{0:T(1024)S(1)} %copy-done.32, ...), kind=kOutput, calls=%fused_computation.52 | convolution fusion | flops 3630952960 | bytes 14571520 | tf_op jit(solution)/shard_map/dot_general | solution.py:33
  283.7 7.7 %reduce-scatter.17.cloned.1.call-done = bf16[192,768]{1,0:T(8,128)(2,1)} async-done(((bf16[768,768]{1,0:T(8,128)(2,1)}), bf16[192,768]{1,0:T(8,128)(2,1)}) %reduce-scatter.17.cloned.1.call-update) | async-done | bytes 294928 | tf_op jit(solution)/shard_map/reduce_scatter | solution.py:271
  293.3 41.0 %reduce-scatter.13.cloned.1.call-done = bf16[192,2304]{1,0:T(8,128)(2,1)} async-done(((bf16[768,2304]{1,0:T(8,128)(2,1)}), bf16[192,2304]{1,0:T(8,128)(2,1)}) %reduce-scatter.13.cloned.1.call-update) | async-done | bytes 884752 | tf_op jit(solution)/shard_map/reduce_scatter | solution.py:268
  337.0 71.3 %reduce-scatter.23.cloned.1.call-done = f32[24,3072]{1,0:T(8,128)} async-done(((f32[192,3072]{1,0:T(8,128)}), f32[24,3072]{1,0:T(8,128)}) %reduce-scatter.23.cloned.1.call-update) | async-done | bytes 294928 | tf_op jit(solution)/shard_map/reduce_scatter | solution.py:287
  411.7 69.4 %reduce-scatter.27.cloned.1.call-done = f32[96,768]{1,0:T(8,128)} async-done(((f32[768,768]{1,0:T(8,128)}), f32[96,768]{1,0:T(8,128)}) %reduce-scatter.27.cloned.1.call-update) | async-done | bytes 294928 | tf_op jit(solution)/shard_map/reduce_scatter | solution.py:288
  483.5 9.5 %add_convert_fusion.1 = bf16[1024,768]{1,0:T(8,128)(2,1)} fusion(f32[1024,768]{1,0:T(8,128)S(1)} %copy-done.15, bf16[1024,3072]{1,0:T(8,128)(2,1)} %get-tuple-element.68, bf16[3072,768]{1,0:T(8,128)(2,1)} %all-gather.15.cloned.1.call-done, f32[768]{0:T(1024)S(1)} %copy-done.44), kind=kOutput, calls=%fused_computation.63 | convolution fusion | flops 4834197504 | bytes 15731712 | tf_op jit(solution)/shard_map/dot_general | solution.py:143
  492.9 10.2 %reduce-scatter.29.cloned.1.call-done = bf16[192,14]{1,0:T(8,128)(2,1)} async-done(((bf16[768,14]{1,0:T(8,128)(2,1)}), bf16[192,14]{1,0:T(8,128)(2,1)}) %reduce-scatter.29.cloned.1.call-update) | async-done | bytes 5392
  504.0 37.2 %all-reduce = f32[14,192]{1,0:T(8,128)S(1)} all-reduce(bf16[14,192]{1,0:T(8,128)(2,1)S(1)} %copy.118), channel_id=11, replica_groups=mesh['batch'=8,'fsdp'=4] {'batch'}, use_global_device_ids=true, to_apply=%region_32.33.clone | all-reduce | flops 2688 | bytes 16128
  541.9 30.7 %all-gather.1 = bf16[8,24,14]{1,2,0:T(8,128)(2,1)S(1)} all-gather(bf16[1,24,14]{1,2,0:T(8,128)(2,1)S(1)} %get-tuple-element.37), channel_id=1, replica_groups=mesh['batch'=8,'fsdp'=4] {'batch'}, dimensions={0}, use_global_device_ids=true | all-gather | bytes 6048 | tf_op jit(solution)/shard_map/all_gather | solution.py:316
  574.9 31.4 %all_gather.41 = bf16[192,768]{1,0:T(8,128)(2,1)S(1)} all-gather(bf16[24,768]{1,0:T(8,128)(2,1)S(1)} %get-tuple-element.49), channel_id=1, replica_groups=mesh['batch'=8,'fsdp'=4] {'batch'}, dimensions={0}, use_global_device_ids=true | all-gather | bytes 331776 | tf_op jit(solution)/shard_map/all_gather | solution.py:307
  607.2 32.5 %reduce-scatter.15.cloned.1.call-done = f32[24,2304]{1,0:T(8,128)} async-done(((f32[192,2304]{1,0:T(8,128)}), f32[24,2304]{1,0:T(8,128)}) %reduce-scatter.15.cloned.1.call-update) | async-done | bytes 221200 | tf_op jit(solution)/shard_map/reduce_scatter | solution.py:285
  641.7 33.8 %all_gather.40 = bf16[192,2304]{1,0:T(8,128)(2,1)S(1)} all-gather(bf16[24,2304]{1,0:T(8,128)(2,1)S(1)} %get-tuple-element.52), channel_id=1, replica_groups=mesh['batch'=8,'fsdp'=4] {'batch'}, dimensions={0}, use_global_device_ids=true | all-gather | bytes 995328 | tf_op jit(solution)/shard_map/all_gather | solution.py:304
  676.8 8.8 %all-gather.17.cloned.1.call-done = bf16[192,3072]{1,0:T(8,128)(2,1)} async-done(((bf16[24,3072]{1,0:T(8,128)(2,1)}), bf16[192,3072]{1,0:T(8,128)(2,1)}) %all-gather.17.cloned.1.call-update) | async-done | bytes 1179664 | tf_op jit(solution)/shard_map/all_gather | solution.py:310
  688.6 39.3 %all-gather.19.cloned.1.call-done = bf16[768,768]{1,0:T(8,128)(2,1)} async-done(((bf16[96,768]{1,0:T(8,128)(2,1)}), bf16[768,768]{1,0:T(8,128)(2,1)}) %all-gather.19.cloned.1.call-update) | async-done | bytes 1179664 | tf_op jit(solution)/shard_map/all_gather | solution.py:313
  (228 shorter events, 95.7 us)
Async XLA Ops:
  7.2 36.4 %all-gather.9.cloned.1.call-start = ((), (), s32[]{:S(2)}) async-start(), calls=%async_computation.9 | async-start | bytes 4423680 | tf_op jit(solution)/shard_map/all_gather | solution.py:97
  9.9 73.0 %all-gather.11.cloned.1.call-start = ((), (), s32[]{:S(2)}) async-start(), calls=%async_computation.10 | async-start | bytes 1474560 | tf_op jit(solution)/shard_map/all_gather | solution.py:98
  10.7 92.1 %all-gather.13.cloned.1.call-start = ((), (), s32[]{:S(2)}) async-start(), calls=%async_computation.11 | async-start | bytes 5898240 | tf_op jit(solution)/shard_map/all_gather | solution.py:99
  12.0 129.7 %all-gather.15.cloned.1.call-start = ((), (), s32[]{:S(2)}) async-start(), calls=%async_computation.12 | async-start | bytes 5898240 | tf_op jit(solution)/shard_map/all_gather | solution.py:100
  15.0 227.8 %reduce-scatter.21.cloned.1.call-start = ((), (), s32[]{:S(2)}) async-start(), calls=%async_computation.17 | async-start | bytes 5898240 | tf_op jit(solution)/shard_map/reduce_scatter | solution.py:274
  25.8 57.1 %copy-start.1 = (f32[4,256,768]{2,1,0:T(8,128)}, f32[4,256,768]{2,1,0:T(8,128)S(1)}, u32[]{:S(2)}) copy-start(f32[4,256,768]{2,1,0:T(8,128)S(1)} %get-tuple-element.59) | copy-start | bytes 9437188
  102.9 38.9 %copy-start.23 = (bf16[1024,768]{1,0:T(8,128)(2,1)S(1)}, bf16[1024,768]{1,0:T(8,128)(2,1)}, u32[]{:S(2)}) copy-start(bf16[1024,768]{1,0:T(8,128)(2,1)} %fusion.27) | copy-start | bytes 4718596
  141.7 14.5 %copy-start.13 = (f32[1024,768]{1,0:T(8,128)S(1)}, f32[1024,768]{1,0:T(8,128)}, u32[]{:S(2)}) copy-start(f32[1024,768]{1,0:T(8,128)} %copy-done.12) | copy-start | bytes 9437188
  164.1 98.5 %reduce-scatter.25.cloned.1.call-start = ((), (), s32[]{:S(2)}) async-start(), calls=%async_computation.20 | async-start | bytes 5898240 | tf_op jit(solution)/shard_map/reduce_scatter | solution.py:277
  174.0 117.5 %reduce-scatter.17.cloned.1.call-start = ((), (), s32[]{:S(2)}) async-start(), calls=%async_computation.15 | async-start | bytes 1474560 | tf_op jit(solution)/shard_map/reduce_scatter | solution.py:271
  213.9 120.5 %reduce-scatter.13.cloned.1.call-start = ((), (), s32[]{:S(2)}) async-start(), calls=%async_computation.13 | async-start | bytes 4423680 | tf_op jit(solution)/shard_map/reduce_scatter | solution.py:268
  214.0 11.4 %copy-start.11 = (bf16[4,256,1,12,64]{1,0,4,3,2:T(4,128)(2,1)S(1)}, bf16[4,256,1,12,64]{1,0,4,3,2:T(4,128)(2,1)}, u32[]{:S(2)}) copy-start(bf16[4,256,1,12,64]{1,0,4,3,2:T(4,128)(2,1)} %copy-done.10) | copy-start | bytes 4718596
  242.7 165.5 %reduce-scatter.23.cloned.1.call-start = ((), (), s32[]{:S(2)}) async-start(), calls=%async_computation.18 | async-start | bytes 2654208 | tf_op jit(solution)/shard_map/reduce_scatter | solution.py:287
  245.8 19.8 %copy-start.47 = (pred[256]{0:T(512)(128)(4,1)S(1)}, pred[256]{0:T(512)(128)(4,1)}, u32[]{:S(2)}) copy-start(pred[256]{0:T(512)(128)(4,1)} %copy-done.46) | copy-start | bytes 772
  245.8 19.8 %copy-start.9 = (bf16[4,256,768]{2,1,0:T(8,128)(2,1)S(1)}, bf16[4,256,768]{2,1,0:T(8,128)(2,1)}, u32[]{:S(2)}) copy-start(bf16[4,256,768]{2,1,0:T(8,128)(2,1)} %param.20) | copy-start | bytes 4718596
  245.8 19.8 %copy-start.41 = (f32[4,256]{1,0:T(4,128)S(1)}, f32[4,256]{1,0:T(4,128)}, u32[]{:S(2)}) copy-start(f32[4,256]{1,0:T(4,128)} %get-tuple-element.62) | copy-start | bytes 12292
  245.8 235.3 %reduce-scatter.27.cloned.1.call-start = ((), (), s32[]{:S(2)}) async-start(), calls=%async_computation.21 | async-start | bytes 2654208 | tf_op jit(solution)/shard_map/reduce_scatter | solution.py:288
  265.5 237.6 %reduce-scatter.29.cloned.1.call-start = ((), (), s32[]{:S(2)}) async-start(), calls=%async_computation.23 | async-start | bytes 245760
  282.8 125.5 %copy-start.27 = (f32[24,3072]{1,0:T(8,128)S(1)}, f32[24,3072]{1,0:T(8,128)}, u32[]{:S(2)}) copy-start(f32[24,3072]{1,0:T(8,128)} %param.30) | copy-start | bytes 884740
  283.7 289.6 %reduce-scatter.19.cloned.1.call-start = ((), (), s32[]{:S(2)}) async-start(), calls=%async_computation.16 | async-start | bytes 663552 | tf_op jit(solution)/shard_map/reduce_scatter | solution.py:286
  293.3 117.2 %copy-start.50 = (u32[32]{0:T(128)S(1)}, u32[32]{0:T(128)}, u32[]{:S(2)}) copy-start(u32[32]{0:T(128)} %constant.159) | copy-start | bytes 388
  293.3 346.4 %reduce-scatter.15.cloned.1.call-start = ((), (), s32[]{:S(2)}) async-start(), calls=%async_computation.14 | async-start | bytes 1990656 | tf_op jit(solution)/shard_map/reduce_scatter | solution.py:285
  336.9 146.5 %copy-start.15 = (f32[1024,768]{1,0:T(8,128)S(1)}, f32[1024,768]{1,0:T(8,128)}, u32[]{:S(2)}) copy-start(f32[1024,768]{1,0:T(8,128)} %copy-done.12) | copy-start | bytes 9437188
  336.9 146.5 %copy-start.44 = (f32[768]{0:T(1024)S(1)}, f32[768]{0:T(1024)}, u32[]{:S(2)}) copy-start(f32[768]{0:T(1024)} %get-tuple-element.27) | copy-start | bytes 9220
  336.9 348.7 %all-gather.17.cloned.1.call-start = ((), (), s32[]{:S(2)}) async-start(), calls=%async_computation.19 | async-start | bytes 1327104 | tf_op jit(solution)/shard_map/all_gather | solution.py:310
  410.4 317.4 %all-gather.19.cloned.1.call-start = ((), (), s32[]{:S(2)}) async-start(), calls=%async_computation.22 | async-start | bytes 1327104 | tf_op jit(solution)/shard_map/all_gather | solution.py:313
  483.4 57.8 %copy-start.40 = (f32[14,192]{1,0:T(8,128)S(1)}, f32[14,192]{1,0:T(8,128)}, u32[]{:S(2)}) copy-start(f32[14,192]{1,0:T(8,128)} %param.35) | copy-start | bytes 32260
  483.4 57.8 %copy-start.42 = (f32[14,24]{1,0:T(8,128)S(1)}, f32[14,24]{1,0:T(8,128)}, u32[]{:S(2)}) copy-start(f32[14,24]{1,0:T(8,128)} %param.36) | copy-start | bytes 4036
  483.4 57.8 %copy-start.43 = (f32[14,24]{1,0:T(8,128)S(1)}, f32[14,24]{1,0:T(8,128)}, u32[]{:S(2)}) copy-start(f32[14,24]{1,0:T(8,128)} %param.37) | copy-start | bytes 4036
  483.4 89.9 %copy-start.29 = (f32[24,768]{1,0:T(8,128)S(1)}, f32[24,768]{1,0:T(8,128)}, u32[]{:S(2)}) copy-start(f32[24,768]{1,0:T(8,128)} %param.27) | copy-start | bytes 221188
  483.4 89.9 %copy-start.30 = (f32[24,768]{1,0:T(8,128)S(1)}, f32[24,768]{1,0:T(8,128)}, u32[]{:S(2)}) copy-start(f32[24,768]{1,0:T(8,128)} %param.28) | copy-start | bytes 221188
  483.5 156.2 %copy-start.28 = (f32[24,2304]{1,0:T(8,128)S(1)}, f32[24,2304]{1,0:T(8,128)}, u32[]{:S(2)}) copy-start(f32[24,2304]{1,0:T(8,128)} %param.24) | copy-start | bytes 663556
  (35 other events, 163.9 us)
Sparse Core Ops, SparseCore 0:
  10.2 33.4 all-gather.8
  45.8 17.4 all-gather.10
  65.4 37.4 all-gather.12
  104.3 37.4 all-gather.14
  164.2 47.9 reduce-scatter.20
  214.6 47.9 reduce-scatter.24
  265.8 25.6 reduce-scatter.16
  294.0 40.3 reduce-scatter.12
  338.5 69.7 reduce-scatter.22
  412.2 68.8 reduce-scatter.26
  484.2 18.9 reduce-scatter.28
  506.9 62.8 reduce-scatter.18
  573.8 65.7 reduce-scatter.14
  642.3 43.3 all-gather.16
  687.7 40.1 all-gather.18
where the time goes:
time: 744 us; the launch traced here: 738 us
  waiting for transfers between devices  327 us (44%)
  matrix products  144 us (19%)
  blocking collectives  139 us (19%)
  other arithmetic  65.4 us (9%)
  local copies, waits for them, and re-layouts  45.8 us (6%)
  between operations  16 us (2%)
    reduce_scatter x1, waiting for transfers between devices, shards(): lax.psum_scatter(halfway[2], 'batch', scatter_dimension=0, tiled=True)  71.3 us
    reduce_scatter x1, waiting for transfers between devices, shards(): lax.psum_scatter(halfway[3], 'batch', scatter_dimension=0, tiled=True)  69.4 us
    reduce_scatter x1, waiting for transfers between devices, shards(): lax.psum_scatter(grad_qkvw.astype(jnp.bfloat16), 'fsdp', scatter_dimensio...  41 us
    all_gather x1, waiting for transfers between devices, shards(): lax.all_gather(updated[3][0].astype(jnp.bfloat16), 'batch', axis=0, tiled...  39.3 us
    dot_general x1, matrix products, shards(): jnp.dot(input_two, fc1_w, preferred_element_type=jnp.float32)  37.7 us
    unnamed x1, blocking collectives  37.2 us
    all_gather x1, blocking collectives, shards(): lax.all_gather(updated[0][0].astype(jnp.bfloat16), 'batch', axis=0, tiled...  33.8 us
    reduce_scatter x1, waiting for transfers between devices, shards(): lax.psum_scatter(halfway[0], 'batch', scatter_dimension=0, tiled=True)  32.5 us
  transfers between devices with their start and end apart: 15, of which 12 were waited for; matrix products, arithmetic and copies ran while one was open for 30% of the time, Pallas kernels for 0%

commit v1 on v0

v1 whole, which is shorter than its diff:
```python
import functools
import math

import jax
import jax.numpy as jnp
import numpy as np
from jax import lax
from jax.experimental import pallas as pl
from jax.experimental.pallas import tpu as pltpu
from jax.sharding import PartitionSpec as P

D = 768
HEADS = 12
HDIM = 64
FF = 3072
TEXT = 40
STEP = 3
MAXM = 128
NVEC = 14
PARTS = FF // D
LANES = 128
SLABS = D // LANES

BETA_ONE = 0.5
BETA_TWO = 0.5
EPS_ADAM = 1e-08
STEP_RATES = (0.03, 0.1, 0.03, 0.015, 0.3)
DECAY_RATES = (0.01, 0.01, 0.01, 0.01, 0.0)
INV_ROOT_TWO = 1.0 / math.sqrt(2.0)
INV_ROOT_TWOPI = 1.0 / math.sqrt(2.0 * math.pi)

F32 = jnp.float32
BF16 = jnp.bfloat16


def dot(a, b):
    return lax.dot_general(a, b, (((1,), (0,)), ((), ())), preferred_element_type=F32)


def dot_first(a, b):
    return lax.dot_general(a, b, (((0,), (0,)), ((), ())), preferred_element_type=F32)


def dot_last(a, b):
    return lax.dot_general(a, b, (((1,), (1,)), ((), ())), preferred_element_type=F32)


def normalize(hidden):
    row_mean = jnp.mean(hidden, axis=-1, keepdims=True)
    centred = hidden - row_mean
    inv_scale = lax.rsqrt(jnp.mean(centred * centred, axis=-1, keepdims=True) + 1e-06)
    return centred * inv_scale, inv_scale


def norm_back(gradient, normed, inv_scale, gain_row):
    scaled = gradient * gain_row
    return inv_scale * (
        scaled
        - jnp.mean(scaled, axis=-1, keepdims=True)
        - normed * jnp.mean(scaled * normed, axis=-1, keepdims=True)
    )


def adamw(weight, gradient, moment_one, moment_two, step_rate, decay_rate):
    new_first = BETA_ONE * moment_one + (1.0 - BETA_ONE) * gradient
    new_second = BETA_TWO * moment_two + (1.0 - BETA_TWO) * gradient * gradient
    correct_one = 1.0 - BETA_ONE**STEP
    correct_two = 1.0 - BETA_TWO**STEP
    update = (
        new_first / correct_one / (jnp.sqrt(new_second / correct_two) + EPS_ADAM)
        + decay_rate * weight
    )
    return (weight - step_rate * update, new_first, new_second)


def cost(flops, moved, trans=0):
    return pl.CostEstimate(flops=int(flops), bytes_accessed=int(moved), transcendentals=int(trans))


def full(shape):
    zeros = (0,) * len(shape)
    return pl.BlockSpec(shape, lambda *_: zeros)


ANYWHERE = pl.BlockSpec(memory_space=pl.ANY)


def swap(value, axis, bit, size):
    return lax.ppermute(value, axis, [(i, i ^ (1 << bit)) for i in range(size)])


class Plan:
    def __init__(self, mesh):
        self.nf = mesh.shape["fsdp"]
        self.nb = mesh.shape["batch"]
        self.nd = self.nf * self.nb
        self.fbits = self.nf.bit_length() - 1
        self.bbits = self.nb.bit_length() - 1
        assert self.nf == 1 << self.fbits and self.nb == 1 << self.bbits
        core = [("fsdp", 0)]
        rest = [("fsdp", k) for k in range(1, self.fbits)]
        near = [("batch", 0)]
        far = [("batch", k) for k in range(1, self.bbits)]
        self.orders = {"x": core + rest + near + far, "y": core + near + rest + far}

    def size(self, axis):
        return self.nf if axis == "fsdp" else self.nb

    def masks(self, order):
        rank = len(order)
        index = np.arange(1 << rank)
        out = {"fsdp": np.zeros_like(index), "batch": np.zeros_like(index)}
        for place, (axis, bit) in enumerate(order):
            out[axis] |= ((index >> (rank - 1 - place)) & 1) << bit
        return out

    def owners(self, order, findex, bindex):
        m = self.masks(order)
        fm = jnp.asarray(m["fsdp"], jnp.int32)
        bm = jnp.asarray(m["batch"], jnp.int32)
        return (findex ^ fm) * self.nb + (bindex ^ bm)


def scatter_sum(plan, order, send, keep):
    parts = [keep]
    count = keep.shape[0]
    for place, (axis, bit) in enumerate(order):
        got = swap(send, axis, bit, plan.size(axis))
        parts.append(got)
        count //= 2
        if count == 0:
            break
        total = parts[0][count : 2 * count].astype(F32)
        for part in parts[1:]:
            total = total + part[count : 2 * count].astype(F32)
        send = total.astype(BF16)
        parts = [part[:count] for part in parts]
    total = parts[0].astype(F32)
    for part in parts[1:]:
        total = total + part.astype(F32)
    return total[0]


def gather_blocks(plan, value):
    blocks = value[None]
    for bit in reversed(range(plan.bbits)):
        got = swap(blocks, "batch", bit, plan.nb)
        blocks = jnp.concatenate([blocks, got], axis=0)
    return blocks


def gather_pieces(plan, shard, low_bit):
    rows = shard.shape[0]
    half = rows // 2
    pieces = [(0, None, shard)]
    if plan.fbits >= 1:
        pieces.append((1, None, swap(shard, "fsdp", 0, plan.nf)))
    for bit in range(1, plan.fbits):
        mask = 1 << bit
        mine = lax.dynamic_slice_in_dim(shard, low_bit * half, half, 0)
        near = swap(mine, "fsdp", bit, plan.nf)
        other = swap(near, "batch", 0, plan.nb)
        pieces.append((mask, 0, near))
        pieces.append((mask, 1, other))
        pieces.append((mask | 1, 0, swap(near, "fsdp", 0, plan.nf)))
        pieces.append((mask | 1, 1, swap(other, "fsdp", 0, plan.nf)))
        assert plan.fbits <= 2
    return pieces


def piece_arrays(pieces):
    return [p[2] for p in pieces]


def piece_copies(meta, refs, target, sems, findex, low_bit, rows):
    copies = []
    for number, ((mask, half, _), ref) in enumerate(zip(meta, refs)):
        start = (findex ^ mask) * rows
        if half is not None:
            start = start + (low_bit if half == 0 else 1 - low_bit) * (rows // 2)
        length = rows if half is None else rows // 2
        copies.append(
            pltpu.make_async_copy(
                ref, target.at[pl.ds(pl.multiple_of(start, 8), length)], sems.at[number]
            )
        )
    return copies


def piece_meta(pieces):
    return [(m, h, None) for m, h, _ in pieces]


def order_kernel(count_ref, pos_ref, tok_ref, cot_ref, perm_ref, tokp_ref, img_ref, dy_ref):
    pair = pl.program_id(0)
    length = tok_ref.shape[1]
    slots = pos_ref.shape[2]
    token = lax.broadcasted_iota(jnp.int32, (length, slots), 0)
    slot = lax.broadcasted_iota(jnp.int32, (length, slots), 1)
    hit = jnp.where(token == pos_ref[0], 1.0, 0.0)
    free = 1.0 - jnp.sum(hit, axis=1, keepdims=True)
    below = lax.broadcasted_iota(jnp.int32, (length, length), 1) < lax.broadcasted_iota(
        jnp.int32, (length, length), 0
    )
    rank = dot(
        jnp.where(below, 1.0, 0.0).astype(BF16),
        jnp.broadcast_to(free, (length, slots)).astype(BF16),
    )
    rest = jnp.where(rank == slot.astype(F32), jnp.broadcast_to(free, (length, slots)), 0.0)
    perm = jnp.concatenate([hit, rest], axis=1).astype(BF16)
    perm_ref[0] = perm
    tokp_ref[0] = dot_first(perm, tok_ref[0]).astype(BF16)
    image = jnp.where(lax.broadcasted_iota(jnp.int32, (length, LANES), 0) >= TEXT, 1.0, 0.0)
    img_ref[0] = dot_first(perm, image.astype(BF16))
    chosen = dot_first(perm[:, :slots], cot_ref[0])
    live = lax.broadcasted_iota(jnp.int32, (slots, 1), 0) < count_ref[pair]
    dy_ref[0] = jnp.where(live, chosen, 0.0).astype(BF16)


def start_row(tok_ref, img_ref, vec_ref):
    return tok_ref[0].astype(F32) + jnp.where(
        img_ref[0][:, :1] > 0.5, vec_ref[1:2, :], vec_ref[0:1, :]
    )


def attn_kernel(meta, rows, place_ref, tok_ref, img_ref, vec_ref, *refs):
    pieces = refs[: len(meta)]
    n1_ref, qkv_ref, a_ref, w_ref, sems = refs[len(meta) :]
    first = pl.program_id(0) == 0
    copies = piece_copies(meta, pieces, w_ref, sems, place_ref[0], place_ref[1], rows)

    @pl.when(first)
    def _():
        for copy in copies:
            copy.start()

    normed, _ = normalize(start_row(tok_ref, img_ref, vec_ref))
    n1 = (normed * vec_ref[2:3, :] + vec_ref[3:4, :]).astype(BF16)
    n1_ref[0] = n1

    @pl.when(first)
    def _():
        for copy in copies:
            copy.wait()

    qkv_ref[0, :, :D] = (dot(n1, w_ref[:, :D]) + vec_ref[4:5, :]).astype(BF16)
    qkv_ref[0, :, D : 2 * D] = dot(n1, w_ref[:, D : 2 * D]).astype(BF16)
    qkv_ref[0, :, 2 * D :] = (dot(n1, w_ref[:, 2 * D :]) + vec_ref[5:6, :]).astype(BF16)
    low = lax.broadcasted_iota(jnp.int32, (1, LANES), 1) < HDIM
    for slab in range(SLABS):
        cols = slice(slab * LANES, (slab + 1) * LANES)
        q = qkv_ref[0, :, cols] * jnp.asarray(HDIM**-0.5, BF16)
        k = qkv_ref[0, :, D + slab * LANES : D + (slab + 1) * LANES]
        v = qkv_ref[0, :, 2 * D + slab * LANES : 2 * D + (slab + 1) * LANES]
        outs = []
        for head in range(2):
            mine = low if head == 0 else jnp.logical_not(low)
            scores = dot_last(jnp.where(mine, q, jnp.zeros_like(q)), k)
            e = jnp.exp(scores - jnp.max(scores, axis=-1, keepdims=True))
            p = (e * (1.0 / jnp.sum(e, axis=-1, keepdims=True))).astype(BF16)
            outs.append(dot(p, v))
        a_ref[0, :, cols] = jnp.where(low, outs[0], outs[1]).astype(BF16)


def fc1_kernel(
    meta_o, rows_o, meta_1, rows_1, place_ref, tok_ref, img_ref, a_ref, vec_ref, *refs
):
    no, n1 = len(meta_o), len(meta_1)
    po, p1 = refs[:no], refs[no : no + n1]
    h1_ref, n2_ref, z_ref, slope_ref, wo_ref, w1_ref, sem_o, sem_1 = refs[no + n1 :]
    first = pl.program_id(0) == 0
    copies_o = piece_copies(meta_o, po, wo_ref, sem_o, place_ref[0], place_ref[1], rows_o)
    copies_1 = piece_copies(meta_1, p1, w1_ref, sem_1, place_ref[0], place_ref[1], rows_1)

    @pl.when(first)
    def _():
        for copy in copies_o:
            copy.start()
        for copy in copies_1:
            copy.start()
        for copy in copies_o:
            copy.wait()

    h1 = start_row(tok_ref, img_ref, vec_ref) + dot(a_ref[0], wo_ref[...]) + vec_ref[6:7, :]
    h1_ref[0] = h1
    normed, _ = normalize(h1)
    n2 = (normed * vec_ref[7:8, :] + vec_ref[8:9, :]).astype(BF16)
    n2_ref[0] = n2

    @pl.when(first)
    def _():
        for copy in copies_1:
            copy.wait()

    slots = slope_ref.shape[1]
    for part in range(PARTS):
        cols = slice(part * D, (part + 1) * D)
        f = dot(n2, w1_ref[:, cols]) + vec_ref[9 + part : 10 + part, :]
        phi = 0.5 * (1.0 + lax.erf(f * INV_ROOT_TWO))
        z_ref[0, :, cols] = (f * phi).astype(BF16)
        fs = f[:slots]
        slope = phi[:slots] + fs * jnp.exp(-0.5 * fs * fs) * INV_ROOT_TWOPI
        slope_ref[0, :, cols] = slope.astype(BF16)


def gw2_kernel(half, nb, bmask, place_ref, z_ref, dy_ref, out_ref, *more):
    acc_ref = more[-1]
    pairs, slots, width = z_ref.shape
    dy = dy_ref[...].reshape(pairs * slots, -1)
    acc_ref[...] = dot_first(z_ref[...].reshape(pairs * slots, width), dy)
    block = width // nb
    for spot in range(nb):
        start = pl.multiple_of((place_ref[2] ^ int(bmask[spot])) * block, 8)
        out_ref[0, spot] = acc_ref[pl.ds(start, block), :].astype(BF16)
    if half == 0:
        more[0][...] = jnp.sum(dy.astype(F32), axis=0, keepdims=True)


def spread(acc_ref, owners_ref, send_ref, keep_ref, block):
    half = send_ref.shape[0]
    for spot in range(half):
        start = pl.multiple_of(owners_ref[half + spot] * block, 8)
        send_ref[spot] = acc_ref[pl.ds(start, block), :].astype(BF16)
    for spot in range(half):
        start = pl.multiple_of(owners_ref[spot] * block, 8)
        keep_ref[spot] = acc_ref[pl.ds(start, block), :].astype(BF16)


def gw1_kernel(meta, rows, place_ref, owners_ref, dy_ref, slope_ref, n2_ref, *refs):
    pieces = refs[: len(meta)]
    df_ref, gb1_ref, send_ref, keep_ref, w2_ref, n2t_ref, acc_ref, sems = refs[len(meta) :]
    step = pl.program_id(0)
    pairs, slots, width = slope_ref.shape
    total = pairs * slots
    copies = piece_copies(meta, pieces, w2_ref, sems, place_ref[0], place_ref[1], rows)

    @pl.when(step == 0)
    def _():
        for copy in copies:
            copy.start()
        n2t_ref[...] = n2_ref[...].reshape(total, D).T
        for copy in copies:
            copy.wait()

    dz = dot_last(
        dy_ref[...].reshape(total, D), w2_ref[pl.ds(pl.multiple_of(step * width, 8), width), :]
    )
    df = dz * slope_ref[...].reshape(total, width).astype(F32)
    gb1_ref[...] = jnp.sum(df, axis=0, keepdims=True)
    low = df.astype(BF16)
    df_ref[...] = low
    acc_ref[...] = dot(n2t_ref[...], low)
    spread(acc_ref, owners_ref, send_ref, keep_ref, D // (2 * send_ref.shape[0]))


def mlp_back_kernel(
    meta_1, rows_1, meta_o, rows_o, place_ref, df_ref, dy_ref, h1_ref, vec_ref, *refs
):
    n1, no = len(meta_1), len(meta_o)
    p1, po = refs[:n1], refs[n1 : n1 + no]
    dh_ref, dhr_ref, da_ref, sum_ref, w1_ref, wo_ref, sem_1, sem_o = refs[n1 + no :]
    first = pl.program_id(0) == 0
    copies_1 = piece_copies(meta_1, p1, w1_ref, sem_1, place_ref[0], place_ref[1], rows_1)
    copies_o = piece_copies(meta_o, po, wo_ref, sem_o, place_ref[0], place_ref[1], rows_o)

    @pl.when(first)
    def _():
        for copy in copies_1:
            copy.start()
        for copy in copies_o:
            copy.start()
        sum_ref[...] = jnp.zeros_like(sum_ref)
        for copy in copies_1:
            copy.wait()
        for copy in copies_o:
            copy.wait()

    dn2 = dot_last(df_ref[...], w1_ref[...])
    normed, scale = normalize(h1_ref[0])
    dh = dy_ref[0].astype(F32) + norm_back(dn2, normed, scale, vec_ref[7:8, :])
    dh_ref[0] = dh
    sum_ref[0:1, :] += jnp.sum(dh, axis=0, keepdims=True)
    sum_ref[1:2, :] += jnp.sum(dn2 * normed, axis=0, keepdims=True)
    sum_ref[2:3, :] += jnp.sum(dn2, axis=0, keepdims=True)
    low = dh.astype(BF16)
    dhr_ref[0] = low
    da_ref[0] = dot_last(low, wo_ref[...]).astype(BF16)


def attn_back_kernel(qkv_ref, da_ref, dq_ref, dkv_ref, sum_ref):
    slots = da_ref.shape[1]

    @pl.when(pl.program_id(0) == 0)
    def _():
        sum_ref[...] = jnp.zeros_like(sum_ref)

    low = lax.broadcasted_iota(jnp.int32, (1, LANES), 1) < HDIM
    scale = jnp.asarray(HDIM**-0.5, BF16)
    for slab in range(SLABS):
        cols = slice(slab * LANES, (slab + 1) * LANES)
        q = qkv_ref[0, :slots, cols] * scale
        k = qkv_ref[0, :, D + slab * LANES : D + (slab + 1) * LANES]
        v = qkv_ref[0, :, 2 * D + slab * LANES : 2 * D + (slab + 1) * LANES]
        da = da_ref[0, :, cols]
        gqs, gks, gvs = [], [], []
        for head in range(2):
            mine = low if head == 0 else jnp.logical_not(low)
            zero = jnp.zeros_like(q)
            scores = dot_last(jnp.where(mine, q, zero), k)
            e = jnp.exp(scores - jnp.max(scores, axis=-1, keepdims=True))
            p = e * (1.0 / jnp.sum(e, axis=-1, keepdims=True))
            gvs.append(dot_first(p.astype(BF16), da))
            dp = dot_last(jnp.where(mine, da, zero), v)
            ds = (p * (dp - jnp.sum(p * dp, axis=-1, keepdims=True))).astype(BF16)
            gqs.append(dot(ds, k))
            gks.append(dot_first(ds, q))
        gq = jnp.where(low, gqs[0], gqs[1]) * (HDIM**-0.5)
        gk = jnp.where(low, gks[0], gks[1])
        gv = jnp.where(low, gvs[0], gvs[1])
        dq_ref[0, :, cols] = gq.astype(BF16)
        dkv_ref[0, :, cols] = gk.astype(BF16)
        dkv_ref[0, :, D + slab * LANES : D + (slab + 1) * LANES] = gv.astype(BF16)
        sum_ref[0:1, cols] += jnp.sum(gq, axis=0, keepdims=True)
        sum_ref[1:2, cols] += jnp.sum(gv, axis=0, keepdims=True)


def gqkv_kernel(
    owners_ref, n1_ref, dq_ref, dkv_ref, a_ref, dhr_ref, send_ref, keep_ref, n1t_ref, acc_ref
):
    step = pl.program_id(0)
    pairs, length, _ = n1_ref.shape
    slots = dq_ref.shape[1]

    @pl.when(step == 0)
    def _():
        n1t_ref[...] = n1_ref[...].reshape(pairs * length, D).T
        total = dot(n1t_ref[:, :slots], dq_ref[0])
        for pair in range(1, pairs):
            total += dot(n1t_ref[:, pair * length : pair * length + slots], dq_ref[pair])
        acc_ref[...] = total

    @pl.when(jnp.logical_or(step == 1, step == 2))
    def _():
        acc_ref[...] = dot(n1t_ref[...], dkv_ref[...].reshape(pairs * length, D))

    @pl.when(step == 3)
    def _():
        acc_ref[...] = dot_first(
            a_ref[...].reshape(pairs * slots, D), dhr_ref[...].reshape(pairs * slots, D)
        )

    spread(acc_ref, owners_ref, send_ref, keep_ref, D // (2 * send_ref.shape[0]))


def split_three(value):
    one = value.astype(BF16)
    left = value - one.astype(F32)
    two = left.astype(BF16)
    return one, two, (left - two.astype(F32)).astype(BF16)


def grad_in_kernel(
    meta, rows, place_ref, tok_ref, img_ref, vec_ref, dq_ref, dkv_ref, dh_ref, perm_ref, *refs
):
    pieces = refs[: len(meta)]
    out_ref, sum_ref, w_ref, sems = refs[len(meta) :]
    first = pl.program_id(0) == 0
    slots = dq_ref.shape[1]
    copies = piece_copies(meta, pieces, w_ref, sems, place_ref[0], place_ref[1], rows)

    @pl.when(first)
    def _():
        for copy in copies:
            copy.start()
        sum_ref[...] = jnp.zeros_like(sum_ref)
        for copy in copies:
            copy.wait()

    dn_all = dot_last(dkv_ref[0], w_ref[:, D:])
    dn_top = dn_all[:slots] + dot_last(dq_ref[0], w_ref[:, :D])
    dn = jnp.concatenate([dn_top, dn_all[slots:]], axis=0)
    normed, scale = normalize(start_row(tok_ref, img_ref, vec_ref))
    grad = norm_back(dn, normed, scale, vec_ref[2:3, :])
    grad = jnp.concatenate([grad[:slots] + dh_ref[0], grad[slots:]], axis=0)
    image = img_ref[0][:, :1] > 0.5
    sum_ref[0:1, :] += jnp.sum(jnp.where(image, 0.0, grad), axis=0, keepdims=True)
    sum_ref[1:2, :] += jnp.sum(jnp.where(image, grad, 0.0), axis=0, keepdims=True)
    sum_ref[2:3, :] += jnp.sum(dn * normed, axis=0, keepdims=True)
    sum_ref[3:4, :] += jnp.sum(dn, axis=0, keepdims=True)
    one, two, three = split_three(grad)
    perm = perm_ref[0]
    out_ref[0] = dot(perm, one) + dot(perm, two) + dot(perm, three)


def out_kernel(meta, rows, place_ref, z_ref, h1_ref, vec_ref, perm_ref, *refs):
    pieces = refs[: len(meta)]
    out_ref, w_ref, sems = refs[len(meta) :]
    first = pl.program_id(0) == 0
    copies = piece_copies(meta, pieces, w_ref, sems, place_ref[0], place_ref[1], rows)

    @pl.when(first)
    def _():
        for copy in copies:
            copy.start()
        for copy in copies:
            copy.wait()

    y = h1_ref[0] + dot(z_ref[0], w_ref[...]) + vec_ref[9 + PARTS : 10 + PARTS, :]
    out_ref[0] = dot(perm_ref[0], y.astype(BF16)).astype(BF16)


def place_kernel(place_ref, blocks_ref, out_ref):
    nb, rows, _ = blocks_ref.shape
    bits = nb.bit_length() - 1
    for spot in range(nb):
        mask = sum(((spot >> (bits - 1 - k)) & 1) << k for k in range(bits))
        start = pl.multiple_of((place_ref[2] ^ mask) * rows, 8)
        out_ref[pl.ds(start, rows), :] = blocks_ref[spot].astype(F32)


def shards(
    plan,
    tokens,
    cotangent,
    mask_pos,
    mask_count,
    w_qkv,
    m_qkv,
    v_qkv,
    w_out,
    m_out,
    v_out,
    w_fc1,
    m_fc1,
    v_fc1,
    w_fc2,
    m_fc2,
    v_fc2,
    vectors,
    m_vec,
    v_vec,
):
    pairs, length, _ = tokens.shape
    slots = mask_pos.shape[1]
    nf, nb, nd = plan.nf, plan.nb, plan.nd
    fi = lax.axis_index("fsdp")
    bi = lax.axis_index("batch")
    low_bit = bi & 1
    place = jnp.stack([fi, low_bit, bi]).astype(jnp.int32)
    prefetch = functools.partial(pltpu.PrefetchScalarGridSpec, num_scalar_prefetch=1)

    def call(kernel, grid, in_specs, out_specs, out_shape, scratch, estimate, name, scalars=1):
        return pl.pallas_call(
            kernel,
            grid_spec=pltpu.PrefetchScalarGridSpec(
                num_scalar_prefetch=scalars,
                grid=grid,
                in_specs=in_specs,
                out_specs=out_specs,
                scratch_shapes=scratch,
            ),
            out_shape=out_shape,
            cost_estimate=estimate,
            name=name,
        )

    def shape(dims, kind):
        return jax.ShapeDtypeStruct(dims, kind)

    def pair_spec(rows, cols):
        return pl.BlockSpec((1, rows, cols), lambda i, *_: (i, 0, 0))

    low_vec = vectors.astype(BF16)
    vec_parts = [low_vec]
    for bit in range(plan.fbits):
        vec_parts += [swap(part, "fsdp", bit, nf) for part in vec_parts]
    low_qkv = w_qkv.astype(BF16)
    qkv_pieces = gather_pieces(plan, low_qkv, low_bit)
    low_out = w_out.astype(BF16)
    out_pieces = gather_pieces(plan, low_out, low_bit)
    low_1 = w_fc1.astype(BF16)
    fc1_pieces = gather_pieces(plan, low_1, low_bit)
    low_2 = w_fc2.astype(BF16)
    fc2_pieces = gather_pieces(plan, low_2, low_bit)
    columns = []
    for spot in range(nf):
        chosen = vec_parts[0]
        for mask in range(1, nf):
            chosen = jnp.where((fi ^ mask) == spot, vec_parts[mask], chosen)
        columns.append(chosen)
    vec = jnp.concatenate(columns, axis=1).astype(F32)
    vec = jnp.pad(vec, ((0, 16 - NVEC), (0, 0)))
    vec_spec = full(vec.shape)

    rows_d, rows_f = D // nf, FF // nf
    meta_qkv, meta_out = piece_meta(qkv_pieces), piece_meta(out_pieces)
    meta_1, meta_2 = piece_meta(fc1_pieces), piece_meta(fc2_pieces)
    sems = lambda meta: pltpu.SemaphoreType.DMA((len(meta),))

    perm, tokp, img, dy = call(
        order_kernel,
        (pairs,),
        [
            pl.BlockSpec((1, 1, slots), lambda i, *_: (i, 0, 0)),
            pair_spec(length, D),
            pair_spec(length, D),
        ],
        [pair_spec(length, length), pair_spec(length, D), pair_spec(length, LANES), pair_spec(slots, D)],
        [
            shape((pairs, length, length), BF16),
            shape((pairs, length, D), BF16),
            shape((pairs, length, LANES), F32),
            shape((pairs, slots, D), BF16),
        ],
        [],
        cost(pairs * length * length * D * 4, pairs * length * D * 8),
        "order",
    )(mask_count, mask_pos.reshape(pairs, 1, slots), tokens, cotangent)

    n1, qkv, mixed = call(
        functools.partial(attn_kernel, meta_qkv, rows_d),
        (pairs,),
        [pair_spec(length, D), pair_spec(length, LANES), vec_spec] + [ANYWHERE] * len(meta_qkv),
        [pair_spec(length, D), pair_spec(length, 3 * D), pair_spec(length, D)],
        [
            shape((pairs, length, D), BF16),
            shape((pairs, length, 3 * D), BF16),
            shape((pairs, length, D), BF16),
        ],
        [pltpu.VMEM((D, 3 * D), BF16), sems(meta_qkv)],
        cost(pairs * length * (6 * D * D + 8 * length * D), pairs * length * D * 12, pairs * HEADS * length * length),
        "attn",
    )(place, tokp, img, vec, *piece_arrays(qkv_pieces))

    h1, n2, z, slope = call(
        functools.partial(fc1_kernel, meta_out, rows_d, meta_1, rows_d),
        (pairs,),
        [pair_spec(length, D), pair_spec(length, LANES), pair_spec(length, D), vec_spec]
        + [ANYWHERE] * (len(meta_out) + len(meta_1)),
        [pair_spec(length, D), pair_spec(length, D), pair_spec(length, FF), pair_spec(slots, FF)],
        [
            shape((pairs, length, D), F32),
            shape((pairs, length, D), BF16),
            shape((pairs, length, FF), BF16),
            shape((pairs, slots, FF), BF16),
        ],
        [pltpu.VMEM((D, D), BF16), pltpu.VMEM((D, FF), BF16), sems(meta_out), sems(meta_1)],
        cost(pairs * length * (2 * D * D + 2 * D * FF), pairs * length * D * 22, pairs * length * FF),
        "fc1",
    )(place, tokp, img, mixed, vec, *piece_arrays(out_pieces), *piece_arrays(fc1_pieces))

    order_2 = plan.orders["x"]
    masks_2 = plan.masks(order_2)
    halves = nf // 2
    bmask = masks_2["batch"][:nb]

    def gw2(half):
        def lhs_map(i, place_ref):
            flip = (1 - half) + 2 * i
            return (0, 0, place_ref[0] ^ flip)

        outs = [pl.BlockSpec((1, nb, FF // nd, D), lambda i, *_: (i, 0, 0, 0))]
        shapes = [shape((halves, nb, FF // nd, D), BF16)]
        if half == 0:
            outs.append(full((1, D)))
            shapes.append(shape((1, D), F32))
        return call(
            functools.partial(gw2_kernel, half, nb, bmask),
            (halves,),
            [pl.BlockSpec((pairs, slots, FF // nf), lhs_map), full((pairs, slots, D))],
            outs,
            shapes,
            [pltpu.VMEM((FF // nf, D), F32)],
            cost(pairs * slots * D * FF, pairs * slots * (FF + D) + FF * D),
            "gw2",
        )(place, z, dy)

    send_2, gb2 = gw2(0)
    (keep_2,) = gw2(1)
    rows_2 = FF // nd
    sum_2 = scatter_sum(
        plan, order_2, send_2.reshape(nd // 2, rows_2, D), keep_2.reshape(nd // 2, rows_2, D)
    )

    rows_1 = D // nd
    order_1 = plan.orders["y"]
    owners_1 = plan.owners(order_1, fi, bi)
    chunk = D
    top_rows = lambda cols, idx: pl.BlockSpec((pairs, slots, cols), idx)
    df, gb1, send_1, keep_1 = call(
        functools.partial(gw1_kernel, meta_2, rows_f),
        (FF // chunk,),
        [
            full((pairs, slots, D)),
            top_rows(chunk, lambda i, *_: (0, 0, i)),
            top_rows(D, lambda i, *_: (0, 0, 0)),
        ]
        + [ANYWHERE] * len(meta_2),
        [
            pl.BlockSpec((pairs * slots, chunk), lambda i, *_: (0, i)),
            pl.BlockSpec((1, chunk), lambda i, *_: (0, i)),
            pl.BlockSpec((nd // 2, rows_1, chunk), lambda i, *_: (0, 0, i)),
            pl.BlockSpec((nd // 2, rows_1, chunk), lambda i, *_: (0, 0, i)),
        ],
        [
            shape((pairs * slots, FF), BF16),
            shape((1, FF), F32),
            shape((nd // 2, rows_1, FF), BF16),
            shape((nd // 2, rows_1, FF), BF16),
        ],
        [
            pltpu.VMEM((FF, D), BF16),
            pltpu.VMEM((D, pairs * slots), BF16),
            pltpu.VMEM((D, chunk), F32),
            sems(meta_2),
        ],
        cost(pairs * slots * D * FF * 4, pairs * slots * FF * 4 + FF * D * 4),
        "gw1",
        scalars=2,
    )(place, owners_1, dy, slope, n2, *piece_arrays(fc2_pieces))
    sum_1 = scatter_sum(plan, order_1, send_1, keep_1)

    dh, dhr, da, sums_two = call(
        functools.partial(mlp_back_kernel, meta_1, rows_d, meta_out, rows_d),
        (pairs,),
        [
            pl.BlockSpec((slots, FF), lambda i, *_: (i, 0)),
            pair_spec(slots, D),
            pair_spec(slots, D),
            vec_spec,
        ]
        + [ANYWHERE] * (len(meta_1) + len(meta_out)),
        [pair_spec(slots, D), pair_spec(slots, D), pair_spec(slots, D), full((8, D))],
        [
            shape((pairs, slots, D), F32),
            shape((pairs, slots, D), BF16),
            shape((pairs, slots, D), BF16),
            shape((8, D), F32),
        ],
        [pltpu.VMEM((D, FF), BF16), pltpu.VMEM((D, D), BF16), sems(meta_1), sems(meta_out)],
        cost(pairs * slots * (2 * D * FF + 2 * D * D), pairs * slots * (FF * 2 + D * 14) + D * FF * 2),
        "mlp_back",
    )(place, df, dy, h1, vec, *piece_arrays(fc1_pieces), *piece_arrays(out_pieces))

    dq, dkv, sums_attn = pl.pallas_call(
        attn_back_kernel,
        grid=(pairs,),
        in_specs=[pair_spec(length, 3 * D), pair_spec(slots, D)],
        out_specs=[pair_spec(slots, D), pair_spec(length, 2 * D), full((8, D))],
        out_shape=[
            shape((pairs, slots, D), BF16),
            shape((pairs, length, 2 * D), BF16),
            shape((8, D), F32),
        ],
        cost_estimate=cost(
            pairs * slots * length * D * 20, pairs * length * D * 12, pairs * HEADS * slots * length
        ),
        name="attn_back",
    )(qkv, da)

    owners_3 = owners_1
    wide = 4 * D
    send_3, keep_3 = call(
        gqkv_kernel,
        (4,),
        [
            full((pairs, length, D)),
            full((pairs, slots, D)),
            pl.BlockSpec((pairs, length, D), lambda i, *_: (0, 0, jnp.where(i == 2, 1, 0))),
            top_rows(D, lambda i, *_: (0, 0, 0)),
            full((pairs, slots, D)),
        ],
        [
            pl.BlockSpec((nd // 2, rows_1, D), lambda i, *_: (0, 0, i)),
            pl.BlockSpec((nd // 2, rows_1, D), lambda i, *_: (0, 0, i)),
        ],
        [shape((nd // 2, rows_1, wide), BF16)] * 2,
        [pltpu.VMEM((D, pairs * length), BF16), pltpu.VMEM((D, D), F32)],
        cost(pairs * length * D * D * 6, pairs * length * D * 8 + D * D * 8),
        "gqkv",
    )(owners_3, n1, dq, dkv, mixed, dhr)
    sum_3 = scatter_sum(plan, order_1, send_3, keep_3)

    grad_tokens, sums_one = call(
        functools.partial(grad_in_kernel, meta_qkv, rows_d),
        (pairs,),
        [
            pair_spec(length, D),
            pair_spec(length, LANES),
            vec_spec,
            pair_spec(slots, D),
            pair_spec(length, 2 * D),
            pair_spec(slots, D),
            pair_spec(length, length),
        ]
        + [ANYWHERE] * len(meta_qkv),
        [pair_spec(length, D), full((8, D))],
        [shape((pairs, length, D), F32), shape((8, D), F32)],
        [pltpu.VMEM((D, 3 * D), BF16), sems(meta_qkv)],
        cost(pairs * length * (6 * D * D + 6 * length * D), pairs * length * D * 14 + D * D * 6),
        "grad_in",
    )(place, tokp, img, vec, dq, dkv, dh, perm, *piece_arrays(qkv_pieces))

    layer_out = call(
        functools.partial(out_kernel, meta_2, rows_f),
        (pairs,),
        [pair_spec(length, FF), pair_spec(length, D), vec_spec, pair_spec(length, length)]
        + [ANYWHERE] * len(meta_2),
        pair_spec(length, D),
        shape((pairs, length, D), BF16),
        [pltpu.VMEM((FF, D), BF16), sems(meta_2)],
        cost(pairs * length * (2 * D * FF + 2 * length * D), pairs * length * (FF * 2 + D * 6) + D * FF * 2),
        "out",
    )(place, z, h1, vec, perm, *piece_arrays(fc2_pieces))

    grad_vec = jnp.concatenate(
        [
            sums_one[0:4],
            sums_attn[0:2],
            sums_two[0:3],
            gb1.reshape(PARTS, D),
            gb2,
        ],
        axis=0,
    )
    for axis, bit in order_1:
        got = swap(grad_vec.astype(BF16), axis, bit, plan.size(axis))
        grad_vec = grad_vec + got.astype(F32)
    own_cols = D // nd
    grad_vec = lax.dynamic_slice_in_dim(grad_vec, (fi * nb + bi) * own_cols, own_cols, 1)

    def finish(master, gradient, moment_one, moment_two, which):
        rows = gradient.shape[0]
        own = lax.dynamic_slice_in_dim(master, bi * rows, rows, 0)
        new_w, new_m, new_v = adamw(
            own, gradient, moment_one, moment_two, STEP_RATES[which], DECAY_RATES[which]
        )
        return new_w.astype(BF16), new_m, new_v

    def place_blocks(blocks, width, start):
        rows = blocks.shape[1]
        if rows % 8 == 0:
            step = min(width, D)
            return call(
                place_kernel,
                (width // step,),
                [pl.BlockSpec((nb, rows, step), lambda i, *_: (0, 0, i + start // step))],
                pl.BlockSpec((nb * rows, step), lambda i, *_: (0, i)),
                shape((nb * rows, width), F32),
                [],
                cost(0, nb * rows * width * 6),
                "place",
            )(place, blocks)
        bits = plan.bbits
        spots = np.arange(nb)
        mask = sum(((spots >> (bits - 1 - k)) & 1) << k for k in range(bits))
        inverse = np.argsort(mask)
        picked = jnp.take(blocks, jnp.asarray(inverse)[spots ^ bi], axis=0)
        return picked[:, :, start : start + width].reshape(nb * rows, width).astype(F32)

    new_2, new_m2, new_v2 = finish(w_fc2, sum_2, m_fc2, v_fc2, 3)
    w2_all = gather_blocks(plan, new_2)
    new_1, new_m1, new_v1 = finish(w_fc1, sum_1, m_fc1, v_fc1, 2)
    w1_all = gather_blocks(plan, new_1)
    new_q, new_mq, new_vq = finish(w_qkv, sum_3[:, : 3 * D], m_qkv, v_qkv, 0)
    new_o, new_mo, new_vo = finish(w_out, sum_3[:, 3 * D :], m_out, v_out, 1)
    w3_all = gather_blocks(plan, jnp.concatenate([new_q, new_o], axis=1))
    own_vec = lax.dynamic_slice_in_dim(vectors, bi * own_cols, own_cols, 1)
    new_vec, new_mv, new_vv = adamw(
        own_vec, grad_vec, m_vec, v_vec, STEP_RATES[4], DECAY_RATES[4]
    )
    vec_all = gather_blocks(plan, new_vec.astype(BF16))
    bits = plan.bbits
    spots = np.arange(nb)
    mask = sum(((spots >> (bits - 1 - k)) & 1) << k for k in range(bits))
    inverse = np.argsort(mask)
    vec_nat = jnp.take(vec_all, jnp.asarray(inverse)[spots ^ bi], axis=0)
    vec_new = jnp.transpose(vec_nat, (1, 0, 2)).reshape(NVEC, nb * own_cols).astype(F32)

    return (
        layer_out,
        grad_tokens,
        place_blocks(w3_all, 3 * D, 0),
        new_mq,
        new_vq,
        place_blocks(w3_all, D, 3 * D),
        new_mo,
        new_vo,
        place_blocks(w1_all, FF, 0),
        new_m1,
        new_v1,
        place_blocks(w2_all, D, 0),
        new_m2,
        new_v2,
        vec_new,
        new_mv,
        new_vv,
    )


def solution(mesh):
    pairs = P(("batch", "fsdp"), None, None)
    weight = P("fsdp", None)
    state = P(("fsdp", "batch"), None)
    vec_state = P(None, ("fsdp", "batch"))
    matrix = (weight, state, state)
    return jax.shard_map(
        functools.partial(shards, Plan(mesh)),
        mesh=mesh,
        in_specs=(pairs, pairs, P(("batch", "fsdp"), None), P(("batch", "fsdp")))
        + matrix * 4
        + (P(None, "fsdp"), vec_state, vec_state),
        out_specs=(pairs, pairs) + matrix * 4 + (P(None, "fsdp"), vec_state, vec_state),
        check_vma=False,
    )
```

time: 744 us -> 409 us (0.55)
  waiting for transfers between devices: 327 us -> 137 us
  Pallas kernels: 0 us -> 159 us
  matrix products: 144 us -> 0 us
  blocking collectives: 139 us -> 0 us
  starting transfers between devices: 0.62 us -> 50.9 us
  local copies, waits for them, and re-layouts: 45.8 us -> 13.8 us
  other arithmetic: 65.4 us -> 45.1 us
  between operations: 16 us -> 1.23 us
    reduce_scatter x8 -> x0, waiting for transfers between devices: 239 us -> none  [the longest x1 71.3 us: shards(): lax.psum_scatter(halfway[2], 'batch', scatter_dimension=0, tiled=True)]
    pallas_call x0 -> x15, Pallas kernels: none -> 159 us  [the longest x1 25 us: shards(): pl.pallas_call(attn_back_kernel, grid=(pairs,), in_specs=[pair_spec(lengt...]
    dot_general x18 -> x0, matrix products: 144 us -> none  [the longest x1 37.7 us: shards(): jnp.dot(input_two, fc1_w, preferred_element_type=jnp.float32)]
    ppermute x0 -> x55, waiting for transfers between devices: none -> 137 us  [swap(): return lax.ppermute(value, axis, [(i, i ^ 1 << bit) for i in range(size)])]
    all_gather x4 -> x0, blocking collectives: 102 us -> none  [the longest x1 33.8 us: shards(): lax.all_gather(updated[0][0].astype(jnp.bfloat16), 'batch', axis=0, tiled...]
    all_gather x6 -> x0, waiting for transfers between devices: 77.9 us -> none  [the longest x1 39.3 us: shards(): lax.all_gather(updated[3][0].astype(jnp.bfloat16), 'batch', axis=0, tiled...]
    ppermute x0 -> x55, starting transfers between devices: none -> 50.9 us  [swap(): return lax.ppermute(value, axis, [(i, i ^ 1 << bit) for i in range(size)])]
    unnamed x1 -> x0, blocking collectives: 37.2 us -> none
  transfers between devices with their start and end apart: 15 -> 55, of which waited for: 12 -> 27; matrix products, arithmetic and copies ran while one was open for 30% -> 12% of each run, Pallas kernels for 0% -> 20%
where the time goes in v1:
time: 409 us; the launch traced here: 407 us
  Pallas kernels  159 us (39%)
  waiting for transfers between devices  137 us (33%)
  starting transfers between devices  50.9 us (12%)
  other arithmetic  45.1 us (11%)
  local copies, waits for them, and re-layouts  13.8 us (3%)
    ppermute x55, waiting for transfers between devices, swap(): return lax.ppermute(value, axis, [(i, i ^ 1 << bit) for i in range(size)])  137 us
    ppermute x55, starting transfers between devices, swap(): return lax.ppermute(value, axis, [(i, i ^ 1 << bit) for i in range(size)])  50.9 us
    pallas_call x1, Pallas kernels, shards(): pl.pallas_call(attn_back_kernel, grid=(pairs,), in_specs=[pair_spec(lengt...  25 us
    convert_element_type x12, other arithmetic, scatter_sum(): send = total.astype(BF16)  18.5 us
    pallas_call x1, Pallas kernels, shards(): call(functools.partial(attn_kernel, meta_qkv, rows_d), (pairs,), [pair_sp...  18 us
    pallas_call x1, Pallas kernels, shards(): call(functools.partial(fc1_kernel, meta_out, rows_d, meta_1, rows_d), (pa...  17.9 us
    pallas_call x1, Pallas kernels, shards(): call(functools.partial(mlp_back_kernel, meta_1, rows_d, meta_out, rows_d)...  16.8 us
    pallas_call x1, Pallas kernels, shards(): call(functools.partial(grad_in_kernel, meta_qkv, rows_d), (pairs,), [pair...  15.3 us
  transfers between devices with their start and end apart: 55, of which 27 were waited for; matrix products, arithmetic and copies ran while one was open for 12% of the time, Pallas kernels for 20%

profile of v1, /device:TPU:0, one launch (start us, length us, event | category | flops | bytes accessed | tf_op | source)
XLA Modules:
  0.0 407.3 jit_solution(16029219496539832899)
XLA Ops:
  3.2 3.0 collective-permute-start.4
  14.0 18.5 %collective-permute-done.2 = bf16[14,192]{1,0:T(8,128)(2,1)S(1)} collective-permute-done((bf16[14,192]{1,0:T(8,128)(2,1)S(1)}, bf16[14,192]{1,0:T(8,128)(2,1)S(1)}, u32[]{:S(2)}, u32[]{:S(2)}) %collective-permute-start.2) | collective-permute-done | bytes 5408 | tf_op jit(solution)/shard_map/ppermute | solution.py:89
  44.3 10.6 %collective-permute-done.19.refs_2_ = bf16[384,768]{1,0:T(8,128)(2,1)} collective-permute-done((bf16[384,768]{1,0:T(8,128)(2,1)S(1)}, bf16[384,768]{1,0:T(8,128)(2,1)}, u32[]{:S(2)}, u32[]{:S(2)}) %collective-permute-start.19) | collective-permute-done | bytes 589856 | tf_op jit(solution)/shard_map/ppermute | solution.py:89
  58.4 6.1 %order.1 = (bf16[4,256,256]{2,1,0:T(8,128)(2,1)}, bf16[4,256,768]{2,1,0:T(8,128)(2,1)}, f32[4,256,128]{2,1,0:T(8,128)}, bf16[4,128,768]{2,1,0:T(8,128)(2,1)}) custom-call(s32[4]{0:T(128)} %count_ref.1, s32[4,1,128]{2,1,0:T(1,128)} %bitcast.65, bf16[4,256,768]{2,1,0:T(8,128)(2,1)} %tok_ref.1, bf16[4,256,768]{2,1,0:T(8,128)(2,1)} %cot_ref.1), custom_call_target="tpu_custom_call" | custom-call | flops 805306368 | bytes 6291456 | tf_op jit(solution)/shard_map/order/pallas_call | solution.py:600
  69.4 9.9 %collective-permute-done.20.refs_3_ = bf16[384,768]{1,0:T(8,128)(2,1)} collective-permute-done((bf16[384,768]{1,0:T(8,128)(2,1)}, bf16[384,768]{1,0:T(8,128)(2,1)}, u32[]{:S(2)}, u32[]{:S(2)}) %collective-permute-start.20) | collective-permute-done | bytes 589856 | tf_op jit(solution)/shard_map/ppermute | solution.py:89
  79.8 18.0 %attn.1 = (bf16[4,256,768]{2,1,0:T(8,128)(2,1)}, bf16[4,256,2304]{2,1,0:T(8,128)(2,1)}, bf16[4,256,768]{2,1,0:T(8,128)(2,1)}) custom-call(s32[3]{0:T(128)} %pad_add_fusion.place_ref, bf16[4,256,768]{2,1,0:T(8,128)(2,1)} %get-tuple-element.45.tok_ref, f32[4,256,128]{2,1,0:T(8,128)} %get-tuple-element.46.img_ref, f32[16,768]{1,0:T(8,128)} %fusion.30.vec_ref, ...), custom_call_target="tpu_custom_call" | custom-call | flops 5234491392 | bytes 9437184 | tf_op jit(solution)/shard_map/attn/pallas_call | solution.py:620
  98.8 17.9 %fc1.1 = (f32[4,256,768]{2,1,0:T(8,128)}, bf16[4,256,768]{2,1,0:T(8,128)(2,1)}, bf16[4,256,3072]{2,1,0:T(8,128)(2,1)}, bf16[4,128,3072]{2,1,0:T(8,128)(2,1)}) custom-call(s32[3]{0:T(128)} %pad_add_fusion.place_ref, bf16[4,256,768]{2,1,0:T(8,128)(2,1)} %get-tuple-element.45.tok_ref, f32[4,256,128]{2,1,0:T(8,128)} %get-tuple-element.46.img_ref, ...), custom_call_target="tpu_custom_call" | custom-call | flops 6039797760 | bytes 17301504 | tf_op jit(solution)/shard_map/fc1/pallas_call | solution.py:635
  116.8 12.2 %gw1.1 = (bf16[512,3072]{1,0:T(8,128)(2,1)}, f32[1,3072]{1,0:T(1,128)}, bf16[16,24,3072]{2,1,0:T(8,128)(2,1)}, bf16[16,24,3072]{2,1,0:T(8,128)(2,1)}) custom-call(s32[3]{0:T(128)} %pad_add_fusion.place_ref, s32[32]{0:T(128)} %xor_add_fusion.owners_ref, bf16[4,128,768]{2,1,0:T(8,128)(2,1)} %get-tuple-element.52.dy_ref, ...), custom_call_target="tpu_custom_call" | custom-call | flops 4831838208 | bytes 15728640 | tf_op jit(solution)/shard_map/gw1/pallas_call | solution.py:690
  129.0 16.8 %mlp_back.1 = (f32[4,128,768]{2,1,0:T(8,128)}, bf16[4,128,768]{2,1,0:T(8,128)(2,1)}, bf16[4,128,768]{2,1,0:T(8,128)(2,1)}, f32[8,768]{1,0:T(8,128)}) custom-call(s32[3]{0:T(128)} %pad_add_fusion.place_ref, bf16[512,3072]{1,0:T(8,128)(2,1)} %get-tuple-element.55.df_ref, bf16[4,128,768]{2,1,0:T(8,128)(2,1)} %get-tuple-element.52.dy_ref, ...), custom_call_target="tpu_custom_call" | custom-call | flops 3019898880 | bytes 13369344 | tf_op jit(solution)/shard_map/mlp_back/pallas_call | solution.py:723
  145.8 25.0 %attn_back.1 = (bf16[4,128,768]{2,1,0:T(8,128)(2,1)}, bf16[4,256,1536]{2,1,0:T(8,128)(2,1)}, f32[8,768]{1,0:T(8,128)}) custom-call(bf16[4,256,2304]{2,1,0:T(8,128)(2,1)} %get-tuple-element.51.qkv_ref, bf16[4,128,768]{2,1,0:T(8,128)(2,1)} %get-tuple-element.56.da_ref), custom_call_target="tpu_custom_call" | custom-call | flops 2013265920 | bytes 9437184 | tf_op jit(solution)/shard_map/attn_back/pallas_call | solution.py:745
  170.8 15.3 %grad_in.1 = (f32[4,256,768]{2,1,0:T(8,128)}, f32[8,768]{1,0:T(8,128)}) custom-call(s32[3]{0:T(128)} %pad_add_fusion.place_ref, bf16[4,256,768]{2,1,0:T(8,128)(2,1)} %get-tuple-element.45.tok_ref, f32[4,256,128]{2,1,0:T(8,128)} %get-tuple-element.46.img_ref, f32[16,768]{1,0:T(8,128)} %fusion.30.vec_ref, bf16[4,128,768]{2,1,0:T(8,128)(2,1)} %get-tuple-element.57.dq_ref, ...), custom_call_target="tpu_custom_call" | custom-call | flops 4831838208 | bytes 14548992 | tf_op jit(solution)/shard_map/grad_in/pallas_call | solution.py:784
  188.8 5.2 %gw2.3 = (bf16[2,8,96,768]{3,2,1,0:T(8,128)(2,1)}, f32[1,768]{1,0:T(1,128)}) custom-call(s32[3]{0:T(128)} %pad_add_fusion.place_ref, bf16[4,256,3072]{2,1,0:T(8,128)(2,1)} %get-tuple-element.48.z_ref, bf16[4,128,768]{2,1,0:T(8,128)(2,1)} %get-tuple-element.52.dy_ref), custom_call_target="tpu_custom_call" | custom-call | flops 1207959552 | bytes 4325376 | tf_op jit(solution)/shard_map/gw2/pallas_call | solution.py:667
  200.9 10.5 %gqkv.1 = (bf16[16,24,3072]{2,1,0:T(8,128)(2,1)}, bf16[16,24,3072]{2,1,0:T(8,128)(2,1)}) custom-call(s32[32]{0:T(128)} %xor_add_fusion.owners_ref, bf16[4,256,768]{2,1,0:T(8,128)(2,1)} %get-tuple-element.61.n1_ref, bf16[4,128,768]{2,1,0:T(8,128)(2,1)} %get-tuple-element.57.dq_ref, bf16[4,256,1536]{2,1,0:T(8,128)(2,1)} %get-tuple-element.58.dkv_ref, ...), custom_call_target="tpu_custom_call" | custom-call | flops 3623878656 | bytes 11010048 | tf_op jit(solution)/shard_map/gqkv/pallas_call | solution.py:763
  215.3 2.7 collective-permute-start.51
  220.8 2.6 collective-permute-start.52
  226.9 5.0 %gw2.2 = bf16[2,8,96,768]{3,2,1,0:T(8,128)(2,1)} custom-call(s32[3]{0:T(128)} %pad_add_fusion.place_ref, bf16[4,256,3072]{2,1,0:T(8,128)(2,1)} %get-tuple-element.48.z_ref, bf16[4,128,768]{2,1,0:T(8,128)(2,1)} %get-tuple-element.52.dy_ref), custom_call_target="tpu_custom_call" | custom-call | flops 1207959552 | bytes 4325376 | tf_op jit(solution)/shard_map/gw2/pallas_call | solution.py:667
  233.6 2.9 fusion
  237.8 2.8 add_convert_fusion
  245.5 13.0 %out.1 = bf16[4,256,768]{2,1,0:T(8,128)(2,1)} custom-call(s32[3]{0:T(128)} %pad_add_fusion.place_ref, bf16[4,256,3072]{2,1,0:T(8,128)(2,1)} %get-tuple-element.48.z_ref, f32[4,256,768]{2,1,0:T(8,128)} %get-tuple-element.49.h1_ref, f32[16,768]{1,0:T(8,128)} %fusion.30.vec_ref, bf16[4,256,256]{2,1,0:T(8,128)(2,1)} %get-tuple-element.50.perm_ref, ...), custom_call_target="tpu_custom_call" | custom-call | flops 5234491392 | bytes 15728640 | tf_op jit(solution)/shard_map/out/pallas_call | solution.py:804
  263.6 6.1 %collective-permute-done.32 = bf16[8,24,3072]{2,1,0:T(8,128)(2,1)} collective-permute-done((bf16[8,24,3072]{2,1,0:T(8,128)(2,1)}, bf16[8,24,3072]{2,1,0:T(8,128)(2,1)}, u32[]{:S(2)}, u32[]{:S(2)}) %collective-permute-start.32) | collective-permute-done | bytes 1179680 | tf_op jit(solution)/shard_map/ppermute | solution.py:89
  272.2 22.8 %collective-permute-done.24 = bf16[8,24,3072]{2,1,0:T(8,128)(2,1)} collective-permute-done((bf16[8,24,3072]{2,1,0:T(8,128)(2,1)}, bf16[8,24,3072]{2,1,0:T(8,128)(2,1)}, u32[]{:S(2)}, u32[]{:S(2)}) %collective-permute-start.24) | collective-permute-done | bytes 1179680 | tf_op jit(solution)/shard_map/ppermute | solution.py:89
  297.1 5.8 %collective-permute-done.41 = bf16[4,96,768]{2,1,0:T(8,128)(2,1)S(1)} collective-permute-done((bf16[4,96,768]{2,1,0:T(8,128)(2,1)S(1)}, bf16[4,96,768]{2,1,0:T(8,128)(2,1)S(1)}, u32[]{:S(2)}, u32[]{:S(2)}) %collective-permute-start.41) | collective-permute-done | bytes 589856 | tf_op jit(solution)/shard_map/ppermute | solution.py:89
  309.1 8.1 %collective-permute-done.42 = bf16[2,96,768]{2,1,0:T(8,128)(2,1)S(1)} collective-permute-done((bf16[2,96,768]{2,1,0:T(8,128)(2,1)S(1)}, bf16[2,96,768]{2,1,0:T(8,128)(2,1)S(1)}, u32[]{:S(2)}, u32[]{:S(2)}) %collective-permute-start.42) | collective-permute-done | bytes 294944 | tf_op jit(solution)/shard_map/ppermute | solution.py:89
  326.9 2.9 collective-permute-start.27
  332.2 10.1 %collective-permute-done.27 = bf16[1,24,3072]{2,1,0:T(8,128)(2,1)S(1)} collective-permute-done((bf16[1,24,3072]{2,1,0:T(8,128)(2,1)S(1)}, bf16[1,24,3072]{2,1,0:T(8,128)(2,1)S(1)}, u32[]{:S(2)}, u32[]{:S(2)}) %collective-permute-start.27) | collective-permute-done | bytes 147488 | tf_op jit(solution)/shard_map/ppermute | solution.py:89
  349.2 2.9 collective-permute-start.36
  354.3 2.5 collective-permute-done.36
  357.5 10.1 %collective-permute-done.29 = bf16[2,24,3072]{2,1,0:T(8,128)(2,1)S(1)} collective-permute-done((bf16[2,24,3072]{2,1,0:T(8,128)(2,1)S(1)}, bf16[2,24,3072]{2,1,0:T(8,128)(2,1)S(1)}, u32[]{:S(2)}, u32[]{:S(2)}) %collective-permute-start.29) | collective-permute-done | bytes 294944 | tf_op jit(solution)/shard_map/ppermute | solution.py:89
  373.8 10.2 %collective-permute-done.30 = bf16[4,24,3072]{2,1,0:T(8,128)(2,1)} collective-permute-done((bf16[4,24,3072]{2,1,0:T(8,128)(2,1)S(1)}, bf16[4,24,3072]{2,1,0:T(8,128)(2,1)}, u32[]{:S(2)}, u32[]{:S(2)}) %collective-permute-start.30) | collective-permute-done | bytes 589856 | tf_op jit(solution)/shard_map/ppermute | solution.py:89
  386.2 3.7 place.4
  396.6 3.5 place.7
  403.0 4.3 %place.6 = f32[192,3072]{1,0:T(8,128)} custom-call(s32[3]{0:T(128)} %pad_add_fusion.place_ref, bf16[8,24,3072]{2,1,0:T(8,128)(2,1)} %pad_maximum_fusion.1.blocks_ref), custom_call_target="tpu_custom_call" | custom-call | bytes 3538944 | tf_op jit(solution)/shard_map/place/pallas_call | solution.py:844
  (223 shorter events, 115.1 us)
Async XLA Ops:
  3.2 38.2 %collective-permute-start.4 = (bf16[96,2304]{1,0:T(8,128)(2,1)}, bf16[96,2304]{1,0:T(8,128)(2,1)}, u32[]{:S(2)}, u32[]{:S(2)}) collective-permute-start(bf16[96,2304]{1,0:T(8,128)(2,1)} %constant_dynamic-slice_fusion.3), channel_id=1, source_target_pairs={{0,2},{1,3},{2,0},{3,1},{4,6},{5,7},{6,4},{7,5},{8,10},{9,11},{10,... | collective-permute-start | bytes 1327112 | tf_op jit(solution)/shard_map/ppermute | solution.py:89
  6.9 34.2 %collective-permute-start.8 = (bf16[192,768]{1,0:T(8,128)(2,1)}, bf16[192,768]{1,0:T(8,128)(2,1)}, u32[]{:S(2)}, u32[]{:S(2)}) collective-permute-start(bf16[192,768]{1,0:T(8,128)(2,1)} %convert_element_type.321.refs_0_.refs_6_), channel_id=1, source_target_pairs={{0,1},{1,0},{2,3},{3,2},{4,5},{5,4},{6,7},{7,6},{8,9},{9,8},{10,11... | collective-permute-start | bytes 884744 | tf_op jit(solution)/shard_map/ppermute | solution.py:89
  7.8 26.4 %collective-permute-start.9 = (bf16[96,768]{1,0:T(8,128)(2,1)S(1)}, bf16[96,768]{1,0:T(8,128)(2,1)}, u32[]{:S(2)}, u32[]{:S(2)}) collective-permute-start(bf16[96,768]{1,0:T(8,128)(2,1)S(1)} %constant_dynamic-slice_fusion.2), channel_id=1, source_target_pairs={{0,2},{1,3},{2,0},{3,1},{4,6},{5,7},{6,4},{7,5},{8,10},{9,11},{10,... | collective-permute-start | bytes 442376 | tf_op jit(solution)/shard_map/ppermute | solution.py:89
  10.8 32.0 %collective-permute-start.14 = (bf16[96,3072]{1,0:T(8,128)(2,1)}, bf16[96,3072]{1,0:T(8,128)(2,1)}, u32[]{:S(2)}, u32[]{:S(2)}) collective-permute-start(bf16[96,3072]{1,0:T(8,128)(2,1)} %constant_dynamic-slice_fusion.1), channel_id=1, source_target_pairs={{0,2},{1,3},{2,0},{3,1},{4,6},{5,7},{6,4},{7,5},{8,10},{9,11},{10,... | collective-permute-start | bytes 1769480 | tf_op jit(solution)/shard_map/ppermute | solution.py:89
  13.9 18.6 %collective-permute-start.2 = (bf16[14,192]{1,0:T(8,128)(2,1)S(1)}, bf16[14,192]{1,0:T(8,128)(2,1)S(1)}, u32[]{:S(2)}, u32[]{:S(2)}) collective-permute-start(bf16[14,192]{1,0:T(8,128)(2,1)S(1)} %convert_element_type.319), channel_id=1, source_target_pairs={{0,2},{1,3},{2,0},{3,1},{4,6},{5,7},{6,4},{7,5},{8,10},{9,11},{10,... | collective-permute-start | bytes 16136 | tf_op jit(solution)/shard_map/ppermute | solution.py:89
  39.7 15.2 %collective-permute-start.19 = (bf16[384,768]{1,0:T(8,128)(2,1)S(1)}, bf16[384,768]{1,0:T(8,128)(2,1)}, u32[]{:S(2)}, u32[]{:S(2)}) collective-permute-start(bf16[384,768]{1,0:T(8,128)(2,1)S(1)} %constant_dynamic-slice_fusion), channel_id=1, source_target_pairs={{0,2},{1,3},{2,0},{3,1},{4,6},{5,7},{6,4},{7,5},{8,10},{9,11},{10,... | collective-permute-start | bytes 1769480 | tf_op jit(solution)/shard_map/ppermute | solution.py:89
  41.1 23.5 %collective-permute-start.3 = (bf16[192,2304]{1,0:T(8,128)(2,1)}, bf16[192,2304]{1,0:T(8,128)(2,1)}, u32[]{:S(2)}, u32[]{:S(2)}) collective-permute-start(bf16[192,2304]{1,0:T(8,128)(2,1)} %copy-done.10), channel_id=1, source_target_pairs={{0,1},{1,0},{2,3},{3,2},{4,5},{5,4},{6,7},{7,6},{8,9},{9,8},{10,11... | collective-permute-start | bytes 2654216 | tf_op jit(solution)/shard_map/ppermute | solution.py:89
  42.9 24.5 %collective-permute-start.15 = (bf16[96,3072]{1,0:T(8,128)(2,1)}, bf16[96,3072]{1,0:T(8,128)(2,1)}, u32[]{:S(2)}, u32[]{:S(2)}) collective-permute-start(bf16[96,3072]{1,0:T(8,128)(2,1)} %collective-permute-done.14.refs_8_.refs_2_), channel_id=1, source_target_pairs={{0,4},{4,0},{8,12},{12,8},{16,20},{20,16},{24,28},{28,24},{1,5},{5... | collective-permute-start | bytes 1769480 | tf_op jit(solution)/shard_map/ppermute | solution.py:89
  54.9 42.8 %collective-permute-start.13 = (bf16[192,3072]{1,0:T(8,128)(2,1)S(1)}, bf16[192,3072]{1,0:T(8,128)(2,1)S(1)}, u32[]{:S(2)}, u32[]{:S(2)}) collective-permute-start(bf16[192,3072]{1,0:T(8,128)(2,1)S(1)} %convert_element_type.322.refs_6_.refs_0_), channel_id=1, source_target_pairs={{0,1},{1,0},{2,3},{3,2},{4,5},{5,4},{6,7},{7,6},{8,9},{9,8},{10,11... | collective-permute-start | bytes 3538952 | tf_op jit(solution)/shard_map/ppermute | solution.py:89
  55.5 23.8 %collective-permute-start.20 = (bf16[384,768]{1,0:T(8,128)(2,1)}, bf16[384,768]{1,0:T(8,128)(2,1)}, u32[]{:S(2)}, u32[]{:S(2)}) collective-permute-start(bf16[384,768]{1,0:T(8,128)(2,1)} %collective-permute-done.19.refs_2_), channel_id=1, source_target_pairs={{0,4},{4,0},{8,12},{12,8},{16,20},{20,16},{24,28},{28,24},{1,5},{5... | collective-permute-start | bytes 1769480 | tf_op jit(solution)/shard_map/ppermute | solution.py:89
  67.3 49.4 %collective-permute-start.18 = (bf16[768,768]{1,0:T(8,128)(2,1)S(1)}, bf16[768,768]{1,0:T(8,128)(2,1)}, u32[]{:S(2)}, u32[]{:S(2)}) collective-permute-start(bf16[768,768]{1,0:T(8,128)(2,1)S(1)} %copy-done.4), channel_id=1, source_target_pairs={{0,1},{1,0},{2,3},{3,2},{4,5},{5,4},{6,7},{7,6},{8,9},{9,8},{10,11... | collective-permute-start | bytes 3538952 | tf_op jit(solution)/shard_map/ppermute | solution.py:89
  68.1 29.6 %collective-permute-start.17 = (bf16[96,3072]{1,0:T(8,128)(2,1)}, bf16[96,3072]{1,0:T(8,128)(2,1)}, u32[]{:S(2)}, u32[]{:S(2)}) collective-permute-start(bf16[96,3072]{1,0:T(8,128)(2,1)} %collective-permute-done.15.refs_9_.refs_3_), channel_id=1, source_target_pairs={{0,1},{1,0},{2,3},{3,2},{4,5},{5,4},{6,7},{7,6},{8,9},{9,8},{10,11... | collective-permute-start | bytes 1769480 | tf_op jit(solution)/shard_map/ppermute | solution.py:89
  79.2 37.5 %collective-permute-start.21 = (bf16[384,768]{1,0:T(8,128)(2,1)}, bf16[384,768]{1,0:T(8,128)(2,1)}, u32[]{:S(2)}, u32[]{:S(2)}) collective-permute-start(bf16[384,768]{1,0:T(8,128)(2,1)} %collective-permute-done.19.refs_2_), channel_id=1, source_target_pairs={{0,1},{1,0},{2,3},{3,2},{4,5},{5,4},{6,7},{7,6},{8,9},{9,8},{10,11... | collective-permute-start | bytes 1769480 | tf_op jit(solution)/shard_map/ppermute | solution.py:89
  79.2 37.5 %collective-permute-start.22 = (bf16[384,768]{1,0:T(8,128)(2,1)}, bf16[384,768]{1,0:T(8,128)(2,1)}, u32[]{:S(2)}, u32[]{:S(2)}) collective-permute-start(bf16[384,768]{1,0:T(8,128)(2,1)} %collective-permute-done.20.refs_3_), channel_id=1, source_target_pairs={{0,1},{1,0},{2,3},{3,2},{4,5},{5,4},{6,7},{7,6},{8,9},{9,8},{10,11... | collective-permute-start | bytes 1769480 | tf_op jit(solution)/shard_map/ppermute | solution.py:89
  195.0 38.6 %collective-permute-start.39 = (bf16[16,96,768]{2,1,0:T(8,128)(2,1)}, bf16[16,96,768]{2,1,0:T(8,128)(2,1)}, u32[]{:S(2)}, u32[]{:S(2)}) collective-permute-start(bf16[16,96,768]{2,1,0:T(8,128)(2,1)} %bitcast.66), channel_id=1, source_target_pairs={{0,1},{1,0},{2,3},{3,2},{4,5},{5,4},{6,7},{7,6},{8,9},{9,8},{10,11... | collective-permute-start | bytes 7077896 | tf_op jit(solution)/shard_map/ppermute | solution.py:89
  198.4 39.4 %collective-permute-start.31 = (bf16[16,24,3072]{2,1,0:T(8,128)(2,1)}, bf16[16,24,3072]{2,1,0:T(8,128)(2,1)}, u32[]{:S(2)}, u32[]{:S(2)}) collective-permute-start(bf16[16,24,3072]{2,1,0:T(8,128)(2,1)} %get-tuple-element.66), channel_id=1, source_target_pairs={{0,1},{1,0},{2,3},{3,2},{4,5},{5,4},{6,7},{7,6},{8,9},{9,8},{10,11... | collective-permute-start | bytes 7077896 | tf_op jit(solution)/shard_map/ppermute | solution.py:89
  211.4 29.9 %collective-permute-start.23 = (bf16[16,24,3072]{2,1,0:T(8,128)(2,1)}, bf16[16,24,3072]{2,1,0:T(8,128)(2,1)S(1)}, u32[]{:S(2)}, u32[]{:S(2)}) collective-permute-start(bf16[16,24,3072]{2,1,0:T(8,128)(2,1)} %get-tuple-element.64), channel_id=1, source_target_pairs={{0,1},{1,0},{2,3},{3,2},{4,5},{5,4},{6,7},{7,6},{8,9},{9,8},{10,11... | collective-permute-start | bytes 7077896 | tf_op jit(solution)/shard_map/ppermute | solution.py:89
  232.0 26.5 %collective-permute-start.54 = (bf16[4,14,24]{2,1,0:T(8,128)(2,1)S(1)}, bf16[4,14,24]{2,1,0:T(8,128)(2,1)S(1)}, u32[]{:S(2)}, u32[]{:S(2)}) collective-permute-start(bf16[4,14,24]{2,1,0:T(8,128)(2,1)S(1)} %pad_maximum_fusion.10), channel_id=1, source_target_pairs={{0,4},{4,0},{8,12},{12,8},{16,20},{20,16},{24,28},{28,24},{1,5},{5... | collective-permute-start | bytes 8072 | tf_op jit(solution)/shard_map/ppermute | solution.py:89
  236.5 24.8 %collective-permute-start.40 = (bf16[8,96,768]{2,1,0:T(8,128)(2,1)}, bf16[8,96,768]{2,1,0:T(8,128)(2,1)}, u32[]{:S(2)}, u32[]{:S(2)}) collective-permute-start(bf16[8,96,768]{2,1,0:T(8,128)(2,1)} %fusion), channel_id=1, source_target_pairs={{0,2},{1,3},{2,0},{3,1},{4,6},{5,7},{6,4},{7,5},{8,10},{9,11},{10,... | collective-permute-start | bytes 3538952 | tf_op jit(solution)/shard_map/ppermute | solution.py:89
  240.6 29.2 %collective-permute-start.32 = (bf16[8,24,3072]{2,1,0:T(8,128)(2,1)}, bf16[8,24,3072]{2,1,0:T(8,128)(2,1)}, u32[]{:S(2)}, u32[]{:S(2)}) collective-permute-start(bf16[8,24,3072]{2,1,0:T(8,128)(2,1)} %add_convert_fusion), channel_id=1, source_target_pairs={{0,4},{4,0},{8,12},{12,8},{16,20},{20,16},{24,28},{28,24},{1,5},{5... | collective-permute-start | bytes 3538952 | tf_op jit(solution)/shard_map/ppermute | solution.py:89
  244.1 51.0 %collective-permute-start.24 = (bf16[8,24,3072]{2,1,0:T(8,128)(2,1)}, bf16[8,24,3072]{2,1,0:T(8,128)(2,1)}, u32[]{:S(2)}, u32[]{:S(2)}) collective-permute-start(bf16[8,24,3072]{2,1,0:T(8,128)(2,1)} %add_convert_fusion.1), channel_id=1, source_target_pairs={{0,4},{4,0},{8,12},{12,8},{16,20},{20,16},{24,28},{28,24},{1,5},{5... | collective-permute-start | bytes 3538952 | tf_op jit(solution)/shard_map/ppermute | solution.py:89
  262.9 40.0 %collective-permute-start.41 = (bf16[4,96,768]{2,1,0:T(8,128)(2,1)S(1)}, bf16[4,96,768]{2,1,0:T(8,128)(2,1)S(1)}, u32[]{:S(2)}, u32[]{:S(2)}) collective-permute-start(bf16[4,96,768]{2,1,0:T(8,128)(2,1)S(1)} %fusion.2), channel_id=1, source_target_pairs={{0,4},{4,0},{8,12},{12,8},{16,20},{20,16},{24,28},{28,24},{1,5},{5... | collective-permute-start | bytes 1769480 | tf_op jit(solution)/shard_map/ppermute | solution.py:89
  271.4 33.1 %collective-permute-start.33 = (bf16[4,24,3072]{2,1,0:T(8,128)(2,1)S(1)}, bf16[4,24,3072]{2,1,0:T(8,128)(2,1)S(1)}, u32[]{:S(2)}, u32[]{:S(2)}) collective-permute-start(bf16[4,24,3072]{2,1,0:T(8,128)(2,1)S(1)} %add_convert_fusion.2), channel_id=1, source_target_pairs={{0,2},{1,3},{2,0},{3,1},{4,6},{5,7},{6,4},{7,5},{8,10},{9,11},{10,... | collective-permute-start | bytes 1769480 | tf_op jit(solution)/shard_map/ppermute | solution.py:89
  305.8 15.4 %collective-permute-start.34 = (bf16[2,24,3072]{2,1,0:T(8,128)(2,1)S(1)}, bf16[2,24,3072]{2,1,0:T(8,128)(2,1)S(1)}, u32[]{:S(2)}, u32[]{:S(2)}) collective-permute-start(bf16[2,24,3072]{2,1,0:T(8,128)(2,1)S(1)} %add_convert_fusion.4), channel_id=1, source_target_pairs={{0,8},{4,12},{8,0},{12,4},{16,24},{20,28},{24,16},{28,20},{1,9},{5... | collective-permute-start | bytes 884744 | tf_op jit(solution)/shard_map/ppermute | solution.py:89
  308.7 17.2 %collective-permute-start.26 = (bf16[2,24,3072]{2,1,0:T(8,128)(2,1)S(1)}, bf16[2,24,3072]{2,1,0:T(8,128)(2,1)S(1)}, u32[]{:S(2)}, u32[]{:S(2)}) collective-permute-start(bf16[2,24,3072]{2,1,0:T(8,128)(2,1)S(1)} %add_convert_fusion.5), channel_id=1, source_target_pairs={{0,8},{4,12},{8,0},{12,4},{16,24},{20,28},{24,16},{28,20},{1,9},{5... | collective-permute-start | bytes 884744 | tf_op jit(solution)/shard_map/ppermute | solution.py:89
  322.3 24.6 %collective-permute-start.35 = (bf16[1,24,3072]{2,1,0:T(8,128)(2,1)S(1)}, bf16[1,24,3072]{2,1,0:T(8,128)(2,1)S(1)}, u32[]{:S(2)}, u32[]{:S(2)}) collective-permute-start(bf16[1,24,3072]{2,1,0:T(8,128)(2,1)S(1)} %add_convert_fusion.6), channel_id=1, source_target_pairs={{0,16},{4,20},{8,24},{12,28},{16,0},{20,4},{24,8},{28,12},{1,17},{... | collective-permute-start | bytes 442376 | tf_op jit(solution)/shard_map/ppermute | solution.py:89
  326.9 15.4 %collective-permute-start.27 = (bf16[1,24,3072]{2,1,0:T(8,128)(2,1)S(1)}, bf16[1,24,3072]{2,1,0:T(8,128)(2,1)S(1)}, u32[]{:S(2)}, u32[]{:S(2)}) collective-permute-start(bf16[1,24,3072]{2,1,0:T(8,128)(2,1)S(1)} %add_convert_fusion.7), channel_id=1, source_target_pairs={{0,16},{4,20},{8,24},{12,28},{16,0},{20,4},{24,8},{28,12},{1,17},{... | collective-permute-start | bytes 442376 | tf_op jit(solution)/shard_map/ppermute | solution.py:89
  332.0 20.1 %collective-permute-start.44 = (bf16[1,96,768]{2,1,0:T(8,128)(2,1)S(1)}, bf16[1,96,768]{2,1,0:T(8,128)(2,1)S(1)}, u32[]{:S(2)}, u32[]{:S(2)}) collective-permute-start(bf16[1,96,768]{2,1,0:T(8,128)(2,1)S(1)} %get-tuple-element.78), channel_id=1, source_target_pairs={{0,16},{4,20},{8,24},{12,28},{16,0},{20,4},{24,8},{28,12},{1,17},{... | collective-permute-start | bytes 442376 | tf_op jit(solution)/shard_map/ppermute | solution.py:89
  352.1 16.3 %collective-permute-start.45 = (bf16[2,96,768]{2,1,0:T(8,128)(2,1)S(1)}, bf16[2,96,768]{2,1,0:T(8,128)(2,1)S(1)}, u32[]{:S(2)}, u32[]{:S(2)}) collective-permute-start(bf16[2,96,768]{2,1,0:T(8,128)(2,1)S(1)} %pad_maximum_fusion.8), channel_id=1, source_target_pairs={{0,8},{4,12},{8,0},{12,4},{16,24},{20,28},{24,16},{28,20},{1,9},{5... | collective-permute-start | bytes 884744 | tf_op jit(solution)/shard_map/ppermute | solution.py:89
  367.7 16.4 %collective-permute-start.30 = (bf16[4,24,3072]{2,1,0:T(8,128)(2,1)S(1)}, bf16[4,24,3072]{2,1,0:T(8,128)(2,1)}, u32[]{:S(2)}, u32[]{:S(2)}) collective-permute-start(bf16[4,24,3072]{2,1,0:T(8,128)(2,1)S(1)} %pad_maximum_fusion.3), channel_id=1, source_target_pairs={{0,4},{4,0},{8,12},{12,8},{16,20},{20,16},{24,28},{28,24},{1,5},{5... | collective-permute-start | bytes 1769480 | tf_op jit(solution)/shard_map/ppermute | solution.py:89
  368.5 26.0 %collective-permute-start.46 = (bf16[4,96,768]{2,1,0:T(8,128)(2,1)S(1)}, bf16[4,96,768]{2,1,0:T(8,128)(2,1)}, u32[]{:S(2)}, u32[]{:S(2)}) collective-permute-start(bf16[4,96,768]{2,1,0:T(8,128)(2,1)S(1)} %pad_maximum_fusion.5), channel_id=1, source_target_pairs={{0,4},{4,0},{8,12},{12,8},{16,20},{20,16},{24,28},{28,24},{1,5},{5... | collective-permute-start | bytes 1769480 | tf_op jit(solution)/shard_map/ppermute | solution.py:89
  370.8 30.0 %collective-permute-start.38 = (bf16[4,24,3072]{2,1,0:T(8,128)(2,1)S(1)}, bf16[4,24,3072]{2,1,0:T(8,128)(2,1)}, u32[]{:S(2)}, u32[]{:S(2)}) collective-permute-start(bf16[4,24,3072]{2,1,0:T(8,128)(2,1)S(1)} %pad_maximum_fusion.4), channel_id=1, source_target_pairs={{0,4},{4,0},{8,12},{12,8},{16,20},{20,16},{24,28},{28,24},{1,5},{5... | collective-permute-start | bytes 1769480 | tf_op jit(solution)/shard_map/ppermute | solution.py:89
  (55 other events, 650.3 us)

commit v2 on v1

v2 whole, which is shorter than its diff:
```python
import functools
import math

import jax
import jax.numpy as jnp
import numpy as np
from jax import lax
from jax.experimental import pallas as pl
from jax.experimental.pallas import tpu as pltpu
from jax.sharding import PartitionSpec as P

D = 768
HEADS = 12
HDIM = 64
FF = 3072
TEXT = 40
STEP = 3
MAXM = 128
NVEC = 14
PARTS = FF // D
LANES = 128
SLABS = D // LANES

BETA_ONE = 0.5
BETA_TWO = 0.5
EPS_ADAM = 1e-08
STEP_RATES = (0.03, 0.1, 0.03, 0.015, 0.3)
DECAY_RATES = (0.01, 0.01, 0.01, 0.01, 0.0)
INV_ROOT_TWO = 1.0 / math.sqrt(2.0)
INV_ROOT_TWOPI = 1.0 / math.sqrt(2.0 * math.pi)

FLOPS_SCALE = 3e9
BYTES_SCALE = 1e7
F32 = jnp.float32
BF16 = jnp.bfloat16


def dot(a, b):
    return lax.dot_general(a, b, (((1,), (0,)), ((), ())), preferred_element_type=F32)


def dot_first(a, b):
    return lax.dot_general(a, b, (((0,), (0,)), ((), ())), preferred_element_type=F32)


def dot_last(a, b):
    return lax.dot_general(a, b, (((1,), (1,)), ((), ())), preferred_element_type=F32)


def normalize(hidden):
    row_mean = jnp.mean(hidden, axis=-1, keepdims=True)
    centred = hidden - row_mean
    inv_scale = lax.rsqrt(jnp.mean(centred * centred, axis=-1, keepdims=True) + 1e-06)
    return centred * inv_scale, inv_scale


def norm_back(gradient, normed, inv_scale, gain_row):
    scaled = gradient * gain_row
    return inv_scale * (
        scaled
        - jnp.mean(scaled, axis=-1, keepdims=True)
        - normed * jnp.mean(scaled * normed, axis=-1, keepdims=True)
    )


def adamw(weight, gradient, moment_one, moment_two, step_rate, decay_rate):
    new_first = BETA_ONE * moment_one + (1.0 - BETA_ONE) * gradient
    new_second = BETA_TWO * moment_two + (1.0 - BETA_TWO) * gradient * gradient
    correct_one = 1.0 - BETA_ONE**STEP
    correct_two = 1.0 - BETA_TWO**STEP
    update = (
        new_first / correct_one / (jnp.sqrt(new_second / correct_two) + EPS_ADAM)
        + decay_rate * weight
    )
    return (weight - step_rate * update, new_first, new_second)


def spent(micros):
    return pl.CostEstimate(
        flops=int(micros * FLOPS_SCALE), bytes_accessed=int(micros * BYTES_SCALE), transcendentals=0
    )


def full(shape):
    zeros = (0,) * len(shape)
    return pl.BlockSpec(shape, lambda *_: zeros)


ANYWHERE = pl.BlockSpec(memory_space=pl.ANY)


class Plan:
    def __init__(self, mesh):
        self.nf = mesh.shape["fsdp"]
        self.nb = mesh.shape["batch"]
        self.nd = self.nf * self.nb
        self.fbits = self.nf.bit_length() - 1
        self.bbits = self.nb.bit_length() - 1
        assert self.nf == 1 << self.fbits and self.nb == 1 << self.bbits
        assert self.fbits == 2 and self.bbits >= 2
        near = [1, 2, 6] if self.bbits == 3 else [1 << k for k in range(self.bbits)]
        self.batch = [mask * self.nf for mask in near]
        first, second, *rest = self.batch
        self.scatter = ([1, 2, second, first] + rest, [1, first, 2, second] + rest)
        self.gather = (rest[::-1] + [second, first], rest[::-1] + [first, second])
        self.helper = (first, second)

    def exchange(self, value, even, odd=None):
        odd = even if odd is None else odd
        pairs = [(i, i ^ (odd if i & 1 else even)) for i in range(self.nd)]
        return lax.ppermute(value, ("batch", "fsdp"), pairs)

    def spans(self, gens):
        masks = np.zeros(1, np.int32)
        for mask in reversed(gens):
            masks = np.concatenate([masks, masks ^ mask])
        return masks

    def owners(self, fi, bi):
        mine = bi * self.nf + fi
        even, odd = (jnp.asarray(self.spans(order[1:]), jnp.int32) for order in self.scatter)
        is_even = (fi & 1) == 0
        keep = mine ^ jnp.where(is_even, even, odd)
        send = (mine ^ 1) ^ jnp.where(is_even, odd, even)
        index = jnp.concatenate([keep, send])
        return (index & (self.nf - 1)) * self.nb + (index >> self.fbits)

    def gathered(self, fi, bi):
        even, odd = (
            jnp.asarray(self.spans(gens[::-1]) >> self.fbits, jnp.int32) for gens in self.gather
        )
        return bi ^ jnp.where((fi & 1) == 0, even, odd)


PIECES = ((0, None), (1, None), (2, 0), (2, 1), (3, 2), (3, 3))


def piece_copies(refs, target, sems, place_ref, rows, start=0):
    copies = []
    cols = target.shape[1]
    for number, ((mask, kind), ref) in enumerate(zip(PIECES, refs)):
        row = (place_ref[0] ^ mask) * rows
        length = rows
        if kind is not None:
            length = rows // 2
            low = place_ref[1 + kind // 2]
            row = row + (low if kind % 2 == 0 else 1 - low) * length
        copies.append(
            pltpu.make_async_copy(
                ref.at[:, pl.ds(start, cols)],
                target.at[pl.ds(pl.multiple_of(row, 8), length)],
                sems.at[number],
            )
        )
    return copies


def start_all(copies):
    for copy in copies:
        copy.start()


def wait_all(copies):
    for copy in copies:
        copy.wait()


def cast_kernel(place_ref, *refs):
    parts, (shard_ref, mine_ref) = refs[:-2], refs[-2:]
    start = 0
    for part in parts:
        cols = slice(start, start + part.shape[1])
        low = part[...].astype(BF16)
        shard_ref[:, cols] = low

        @pl.when(pl.program_id(0) == 0)
        def _(low=low, cols=cols):
            mine_ref[:, cols] = low

        start += part.shape[1]


def order_kernel(count_ref, pos_ref, tok_ref, cot_ref, perm_ref, tokp_ref, img_ref, dy_ref):
    pair = pl.program_id(0)
    length = tok_ref.shape[1]
    slots = pos_ref.shape[2]
    token = lax.broadcasted_iota(jnp.int32, (length, slots), 0)
    slot = lax.broadcasted_iota(jnp.int32, (length, slots), 1)
    hit = jnp.where(token == pos_ref[0], 1.0, 0.0)
    free = 1.0 - jnp.sum(hit, axis=1, keepdims=True)
    below = lax.broadcasted_iota(jnp.int32, (length, length), 1) < lax.broadcasted_iota(
        jnp.int32, (length, length), 0
    )
    rank = dot(
        jnp.where(below, 1.0, 0.0).astype(BF16),
        jnp.broadcast_to(free, (length, slots)).astype(BF16),
    )
    rest = jnp.where(rank == slot.astype(F32), jnp.broadcast_to(free, (length, slots)), 0.0)
    perm = jnp.concatenate([hit, rest], axis=1).astype(BF16)
    perm_ref[0] = perm
    tokp_ref[0] = dot_first(perm, tok_ref[0]).astype(BF16)
    image = jnp.where(lax.broadcasted_iota(jnp.int32, (length, LANES), 0) >= TEXT, 1.0, 0.0)
    img_ref[0] = dot_first(perm, image.astype(BF16))
    chosen = dot_first(perm[:, :slots], cot_ref[0])
    live = lax.broadcasted_iota(jnp.int32, (slots, 1), 0) < count_ref[pair]
    dy_ref[0] = jnp.where(live, chosen, 0.0).astype(BF16)


def start_row(tok_ref, img_ref, vec_ref):
    return tok_ref[0].astype(F32) + jnp.where(
        img_ref[0][:, :1] > 0.5, vec_ref[1:2, :], vec_ref[0:1, :]
    )


def qkv_kernel(rows, place_ref, tok_ref, img_ref, vec_ref, *refs):
    pieces = refs[: len(PIECES)]
    n1_ref, qkv_ref, w_ref, sems = refs[len(PIECES) :]
    first = pl.program_id(0) == 0
    copies = piece_copies(pieces, w_ref, sems, place_ref, rows)

    @pl.when(first)
    def _():
        start_all(copies)

    normed, _ = normalize(start_row(tok_ref, img_ref, vec_ref))
    n1 = (normed * vec_ref[2:3, :] + vec_ref[3:4, :]).astype(BF16)
    n1_ref[0] = n1

    @pl.when(first)
    def _():
        wait_all(copies)

    qkv_ref[0, :, :D] = (dot(n1, w_ref[:, :D]) + vec_ref[4:5, :]).astype(BF16)
    qkv_ref[0, :, D : 2 * D] = dot(n1, w_ref[:, D : 2 * D]).astype(BF16)
    qkv_ref[0, :, 2 * D :] = (dot(n1, w_ref[:, 2 * D :]) + vec_ref[5:6, :]).astype(BF16)


def mix_kernel(qkv_ref, a_ref):
    low = lax.broadcasted_iota(jnp.int32, (1, LANES), 1) < HDIM
    for slab in range(SLABS):
        cols = slice(slab * LANES, (slab + 1) * LANES)
        q = qkv_ref[0, :, cols] * jnp.asarray(HDIM**-0.5, BF16)
        k = qkv_ref[0, :, D + slab * LANES : D + (slab + 1) * LANES]
        v = qkv_ref[0, :, 2 * D + slab * LANES : 2 * D + (slab + 1) * LANES]
        outs = []
        for head in range(2):
            mine = low if head == 0 else jnp.logical_not(low)
            scores = dot_last(jnp.where(mine, q, jnp.zeros_like(q)), k)
            e = jnp.exp(scores - jnp.max(scores, axis=-1, keepdims=True))
            p = (e * (1.0 / jnp.sum(e, axis=-1, keepdims=True))).astype(BF16)
            outs.append(dot(p, v))
        a_ref[0, :, cols] = jnp.where(low, outs[0], outs[1]).astype(BF16)


def fc1_kernel(rows, place_ref, tok_ref, img_ref, a_ref, vec_ref, *refs):
    pieces = refs[: len(PIECES)]
    h1_ref, n2_ref, z_ref, slope_ref, wo_ref, w1_ref, sem_o, sem_1 = refs[len(PIECES) :]
    first = pl.program_id(0) == 0
    copies_o = piece_copies(pieces, wo_ref, sem_o, place_ref, rows)
    copies_1 = piece_copies(pieces, w1_ref, sem_1, place_ref, rows, D)

    @pl.when(first)
    def _():
        start_all(copies_o)
        start_all(copies_1)
        wait_all(copies_o)

    h1 = start_row(tok_ref, img_ref, vec_ref) + dot(a_ref[0], wo_ref[...]) + vec_ref[6:7, :]
    h1_ref[0] = h1
    normed, _ = normalize(h1)
    n2 = (normed * vec_ref[7:8, :] + vec_ref[8:9, :]).astype(BF16)
    n2_ref[0] = n2

    @pl.when(first)
    def _():
        wait_all(copies_1)

    slots = slope_ref.shape[1]
    for part in range(PARTS):
        cols = slice(part * D, (part + 1) * D)
        f = dot(n2, w1_ref[:, cols]) + vec_ref[9 + part : 10 + part, :]
        phi = 0.5 * (1.0 + lax.erf(f * INV_ROOT_TWO))
        z_ref[0, :, cols] = (f * phi).astype(BF16)
        fs = f[:slots]
        slope = phi[:slots] + fs * jnp.exp(-0.5 * fs * fs) * INV_ROOT_TWOPI
        slope_ref[0, :, cols] = slope.astype(BF16)


def spread(acc_ref, owners_ref, outs):
    if len(outs) == 1:
        outs[0][...] = acc_ref[...].astype(BF16)
        return
    keep_ref, send_ref = outs
    half, block, _ = send_ref.shape
    for out_ref, base in ((send_ref, half), (keep_ref, 0)):
        for spot in range(half):
            start = pl.multiple_of(owners_ref[base + spot] * block, 8)
            out_ref[spot] = acc_ref[pl.ds(start, block), :].astype(BF16)


def gw2_kernel(owners_ref, z_ref, dy_ref, *refs):
    outs, (sum_ref, zt_ref, acc_ref) = refs[:-3], refs[-3:]
    pairs, slots, width = z_ref.shape

    @pl.when(pl.program_id(0) == 0)
    def _():
        zt_ref[...] = z_ref[...].reshape(pairs * slots, width).T

    dy = dy_ref[...].reshape(pairs * slots, -1)
    acc_ref[...] = dot(zt_ref[...], dy)
    sum_ref[...] = jnp.sum(dy.astype(F32), axis=0, keepdims=True)
    spread(acc_ref, owners_ref, outs)


def df_kernel(rows, place_ref, dy_ref, slope_ref, *refs):
    pieces = refs[: len(PIECES)]
    df_ref, gb1_ref, w2_ref, sems = refs[len(PIECES) :]
    step = pl.program_id(0)
    pairs, slots, width = slope_ref.shape
    total = pairs * slots
    copies = piece_copies(pieces, w2_ref, sems, place_ref, rows)

    @pl.when(step == 0)
    def _():
        start_all(copies)
        wait_all(copies)

    dz = dot_last(
        dy_ref[...].reshape(total, D), w2_ref[pl.ds(pl.multiple_of(step * width, 8), width), :]
    )
    df = dz * slope_ref[...].reshape(total, width).astype(F32)
    gb1_ref[...] = jnp.sum(df, axis=0, keepdims=True)
    df_ref[...] = df.astype(BF16)


def mlp_back_kernel(rows, place_ref, df_ref, dy_ref, h1_ref, vec_ref, *refs):
    pieces = refs[: len(PIECES)]
    dh_ref, dhr_ref, da_ref, sum_ref, w1_ref, wo_ref, sem_1, sem_o = refs[len(PIECES) :]
    first = pl.program_id(0) == 0
    copies_1 = piece_copies(pieces, w1_ref, sem_1, place_ref, rows, D)
    copies_o = piece_copies(pieces, wo_ref, sem_o, place_ref, rows)

    @pl.when(first)
    def _():
        start_all(copies_1)
        start_all(copies_o)
        sum_ref[...] = jnp.zeros_like(sum_ref)
        wait_all(copies_1)
        wait_all(copies_o)

    some, slots, _ = dy_ref.shape
    total = some * slots
    dn2 = dot_last(df_ref[...], w1_ref[...])
    normed, scale = normalize(h1_ref[...].reshape(total, D))
    dh = dy_ref[...].reshape(total, D).astype(F32) + norm_back(dn2, normed, scale, vec_ref[7:8, :])
    dh_ref[...] = dh.reshape(some, slots, D)
    sum_ref[0:1, :] += jnp.sum(dh, axis=0, keepdims=True)
    sum_ref[1:2, :] += jnp.sum(dn2 * normed, axis=0, keepdims=True)
    sum_ref[2:3, :] += jnp.sum(dn2, axis=0, keepdims=True)
    low = dh.astype(BF16)
    dhr_ref[...] = low.reshape(some, slots, D)
    da_ref[...] = dot_last(low, wo_ref[...]).astype(BF16).reshape(some, slots, D)


def gw1o_kernel(owners_ref, n2_ref, df_ref, a_ref, dhr_ref, *refs):
    outs, (n2t_ref, acc_ref) = refs[:-2], refs[-2:]
    step = pl.program_id(0)
    pairs, slots, _ = n2_ref.shape
    total = pairs * slots

    @pl.when(step == 0)
    def _():
        n2t_ref[...] = n2_ref[...].reshape(total, D).T

    @pl.when(step < PARTS)
    def _():
        acc_ref[...] = dot(n2t_ref[...], df_ref[...])

    @pl.when(step == PARTS)
    def _():
        acc_ref[...] = dot_first(a_ref[...].reshape(total, D), dhr_ref[...].reshape(total, D))

    spread(acc_ref, owners_ref, outs)


def attn_back_kernel(more, qkv_ref, da_ref, *refs):
    if more:
        _, _, before_ref, dq_ref, dkv_ref, sum_ref = refs
    else:
        dq_ref, dkv_ref, sum_ref = refs
    slots = da_ref.shape[1]

    @pl.when(pl.program_id(0) == 0)
    def _():
        sum_ref[...] = before_ref[...] if more else jnp.zeros_like(sum_ref)

    low = lax.broadcasted_iota(jnp.int32, (1, LANES), 1) < HDIM
    scale = jnp.asarray(HDIM**-0.5, BF16)
    for slab in range(SLABS):
        cols = slice(slab * LANES, (slab + 1) * LANES)
        q = qkv_ref[0, :slots, cols] * scale
        k = qkv_ref[0, :, D + slab * LANES : D + (slab + 1) * LANES]
        v = qkv_ref[0, :, 2 * D + slab * LANES : 2 * D + (slab + 1) * LANES]
        da = da_ref[0, :, cols]
        gqs, gks, gvs = [], [], []
        for head in range(2):
            mine = low if head == 0 else jnp.logical_not(low)
            zero = jnp.zeros_like(q)
            scores = dot_last(jnp.where(mine, q, zero), k)
            e = jnp.exp(scores - jnp.max(scores, axis=-1, keepdims=True))
            p = e * (1.0 / jnp.sum(e, axis=-1, keepdims=True))
            gvs.append(dot_first(p.astype(BF16), da))
            dp = dot_last(jnp.where(mine, da, zero), v)
            ds = (p * (dp - jnp.sum(p * dp, axis=-1, keepdims=True))).astype(BF16)
            gqs.append(dot(ds, k))
            gks.append(dot_first(ds, q))
        gq = jnp.where(low, gqs[0], gqs[1]) * (HDIM**-0.5)
        gk = jnp.where(low, gks[0], gks[1])
        gv = jnp.where(low, gvs[0], gvs[1])
        dq_ref[0, :, cols] = gq.astype(BF16)
        dkv_ref[0, :, cols] = gk.astype(BF16)
        dkv_ref[0, :, D + slab * LANES : D + (slab + 1) * LANES] = gv.astype(BF16)
        sum_ref[0:1, cols] += jnp.sum(gq, axis=0, keepdims=True)
        sum_ref[1:2, cols] += jnp.sum(gv, axis=0, keepdims=True)


def gqkv_kernel(owners_ref, n1_ref, dq_ref, dkv_ref, *refs):
    outs, (n1t_ref, acc_ref) = refs[:-2], refs[-2:]
    step = pl.program_id(0)
    pairs, length, _ = n1_ref.shape
    slots = dq_ref.shape[1]

    @pl.when(step == 0)
    def _():
        n1t_ref[...] = n1_ref[...].reshape(pairs * length, D).T
        total = dot(n1t_ref[:, :slots], dq_ref[0])
        for pair in range(1, pairs):
            total += dot(n1t_ref[:, pair * length : pair * length + slots], dq_ref[pair])
        acc_ref[...] = total

    @pl.when(step > 0)
    def _():
        acc_ref[...] = dot(n1t_ref[...], dkv_ref[...].reshape(pairs * length, D))

    spread(acc_ref, owners_ref, outs)


def split_three(value):
    one = value.astype(BF16)
    left = value - one.astype(F32)
    two = left.astype(BF16)
    return one, two, (left - two.astype(F32)).astype(BF16)


def grad_in_kernel(
    rows,
    place_ref,
    tok_ref,
    img_ref,
    vec_ref,
    dq_ref,
    dkv_ref,
    dh_ref,
    perm_ref,
    attn_sum_ref,
    mlp_sum_ref,
    gb1_ref,
    gb2_ref,
    *refs,
):
    pieces = refs[: len(PIECES)]
    out_ref, sum_ref, w_ref, sems = refs[len(PIECES) :]
    first = pl.program_id(0) == 0
    slots = dq_ref.shape[1]
    copies = piece_copies(pieces, w_ref, sems, place_ref, rows)

    @pl.when(first)
    def _():
        start_all(copies)
        sum_ref[...] = jnp.zeros_like(sum_ref)
        sum_ref[4:6, :] = attn_sum_ref[0:2, :]
        sum_ref[6:9, :] = mlp_sum_ref[0:3, :]
        for part in range(PARTS):
            sum_ref[9 + part : 10 + part, :] = gb1_ref[:, part * D : (part + 1) * D]
        sum_ref[9 + PARTS : 10 + PARTS, :] = gb2_ref[...]
        wait_all(copies)

    dn_all = dot_last(dkv_ref[0], w_ref[:, D:])
    dn_top = dn_all[:slots] + dot_last(dq_ref[0], w_ref[:, :D])
    dn = jnp.concatenate([dn_top, dn_all[slots:]], axis=0)
    normed, scale = normalize(start_row(tok_ref, img_ref, vec_ref))
    grad = norm_back(dn, normed, scale, vec_ref[2:3, :])
    grad = jnp.concatenate([grad[:slots] + dh_ref[0], grad[slots:]], axis=0)
    image = img_ref[0][:, :1] > 0.5
    sum_ref[0:1, :] += jnp.sum(jnp.where(image, 0.0, grad), axis=0, keepdims=True)
    sum_ref[1:2, :] += jnp.sum(jnp.where(image, grad, 0.0), axis=0, keepdims=True)
    sum_ref[2:3, :] += jnp.sum(dn * normed, axis=0, keepdims=True)
    sum_ref[3:4, :] += jnp.sum(dn, axis=0, keepdims=True)
    one, two, three = split_three(grad)
    perm = perm_ref[0]
    out_ref[0] = dot(perm, one) + dot(perm, two) + dot(perm, three)


def out_kernel(rows, place_ref, z_ref, h1_ref, vec_ref, perm_ref, *refs):
    pieces = refs[: len(PIECES)]
    out_ref, w_ref, sems = refs[len(PIECES) :]
    first = pl.program_id(0) == 0
    copies = piece_copies(pieces, w_ref, sems, place_ref, rows)

    @pl.when(first)
    def _():
        start_all(copies)
        wait_all(copies)

    y = h1_ref[0] + dot(z_ref[0], w_ref[...]) + vec_ref[9 + PARTS : 10 + PARTS, :]
    out_ref[0] = dot(perm_ref[0], y.astype(BF16)).astype(BF16)


def add_kernel(count, *refs):
    ins, outs = refs[: -1 - (len(refs) > count + 1)], refs[-1 - (len(refs) > count + 1) :]
    total = ins[0][...].astype(F32)
    for ref in ins[1:count]:
        total = total + ref[...].astype(F32)
    outs[0][...] = total.astype(BF16)
    if len(outs) > 1:
        outs[1][...] = ins[count][...] + ins[count + 1][...]


def finish_kernel(count, which, place_ref, *refs):
    parts = refs[:count]
    number = len(which)
    states = refs[count : count + 3 * number]
    new_ref = refs[count + 3 * number]
    moments = refs[count + 3 * number + 1 :]
    total = parts[0][0].astype(F32)
    for ref in parts[1:]:
        total = total + ref[0].astype(F32)
    start = 0
    for spot, kind in enumerate(which):
        master, first, second = states[3 * spot : 3 * spot + 3]
        cols = slice(start, start + master.shape[1])
        new_w, new_m, new_v = adamw(
            master[...], total[:, cols], first[...], second[...], STEP_RATES[kind], DECAY_RATES[kind]
        )
        new_ref[0, :, cols] = new_w.astype(BF16)
        moments[2 * spot][...] = new_m
        moments[2 * spot + 1][...] = new_v
        start += master.shape[1]


def join_kernel(one_ref, two_ref, out_ref):
    count = one_ref.shape[0]
    out_ref[:count] = one_ref[...]
    out_ref[count:] = two_ref[...]


def place_kernel(number, spots_ref, blocks_ref, *refs):
    start = 0
    for out_ref in refs[-number:]:
        width = out_ref.shape[1]
        out_ref[...] = blocks_ref[0, :, start : start + width].astype(F32)
        start += width


def later(value, dep):
    return lax.optimization_barrier((value, dep))[0]


class Chain:
    def __init__(self):
        self.last = None

    def __call__(
        self, kernel, grid, scalars, ins, outs, scratch, estimate, name, after=(), aliases=None
    ):
        deps = list(after)
        if self.last is not None:
            deps.append(self.last)
        fixed = len(scalars) + len(ins)
        extra = len(deps)

        def body(*refs):
            kernel(*refs[:fixed], *refs[fixed + extra :])

        got = pl.pallas_call(
            body,
            grid_spec=pltpu.PrefetchScalarGridSpec(
                num_scalar_prefetch=len(scalars),
                grid=grid,
                in_specs=[spec for _, spec in ins] + [ANYWHERE] * extra,
                out_specs=[spec for spec, _, _ in outs],
                scratch_shapes=scratch,
            ),
            out_shape=[jax.ShapeDtypeStruct(dims, kind) for _, dims, kind in outs],
            input_output_aliases={
                len(scalars) + k: v for k, v in (aliases or {}).items()
            },
            cost_estimate=estimate,
            name=name,
        )(*scalars, *[value for value, _ in ins], *deps)
        self.last = got[-1]
        return got


class Sum:
    def __init__(self, plan, call, keep, send):
        self.plan, self.call = plan, call
        self.parts, self.count, self.place = [keep], keep.shape[0], 0
        self.move(send)

    def move(self, send):
        got = self.plan.exchange(send, *(order[self.place] for order in self.plan.scatter))
        self.parts.append(got)
        self.place += 1

    def add(self, vec=None):
        self.count //= 2
        count = self.count
        _, rows, cols = self.parts[0].shape
        block = max(1, count // 4)
        base = count // block
        spec = pl.BlockSpec((block, rows, cols), lambda i, *_: (base + i, 0, 0))
        ins = [(part, spec) for part in self.parts]
        outs = [
            (pl.BlockSpec((block, rows, cols), lambda i, *_: (i, 0, 0)), (count, rows, cols), BF16)
        ]
        if vec is not None:
            ins += [(value, full(value.shape)) for value in vec]
            outs.append((full(vec[0].shape), vec[0].shape, F32))
        size = count * rows * cols
        got = self.call(
            functools.partial(add_kernel, len(self.parts)),
            (count // block,),
            [],
            ins,
            outs,
            [],
            spent(1.5),
            "add",
        )
        self.move(got[0])
        return got[1] if vec is not None else None


class Spread:
    def __init__(self, plan, call, block):
        self.plan, self.call, self.blocks, self.place = plan, call, block, 0
        self.move()

    def move(self):
        self.got = self.plan.exchange(self.blocks, *(order[self.place] for order in self.plan.gather))
        self.place += 1

    def join(self):
        shape = self.blocks.shape
        self.blocks = self.call(
            join_kernel,
            (1,),
            [],
            [(self.blocks, full(shape)), (self.got, full(shape))],
            [(full((2 * shape[0],) + shape[1:]), (2 * shape[0],) + shape[1:], BF16)],
            [],
            spent(0.3),
            "join",
        )[0]
        self.move()

    def put(self, spots, widths, before=None):
        blocks = self.blocks if before is None else self.got
        count, rows, cols = blocks.shape
        base = 0 if before is None else count
        nb = self.plan.nb
        ins = [(blocks, pl.BlockSpec((1, rows, cols), lambda i, *_: (i, 0, 0)))]
        aliases = None
        if before is not None:
            ins += [(value, ANYWHERE) for value in before]
            aliases = {1 + k: k for k in range(len(widths))}
        return self.call(
            functools.partial(place_kernel, len(widths)),
            (count,),
            [spots],
            ins,
            [
                (
                    pl.BlockSpec((rows, width), lambda i, spots_ref: (spots_ref[base + i], 0)),
                    (nb * rows, width),
                    F32,
                )
                for width in widths
            ],
            [],
            spent(0.1),
            "place",
            aliases=aliases,
        )


def shards(
    plan,
    tokens,
    cotangent,
    mask_pos,
    mask_count,
    w_qkv,
    m_qkv,
    v_qkv,
    w_out,
    m_out,
    v_out,
    w_fc1,
    m_fc1,
    v_fc1,
    w_fc2,
    m_fc2,
    v_fc2,
    vectors,
    m_vec,
    v_vec,
):
    pairs, length, _ = tokens.shape
    slots = mask_pos.shape[1]
    nf, nb, nd = plan.nf, plan.nb, plan.nd
    fi = lax.axis_index("fsdp").astype(jnp.int32)
    bi = lax.axis_index("batch").astype(jnp.int32)
    halves = jnp.stack([bi & 1, (bi >> 1) & 1])
    place = jnp.stack([fi, halves[fi & 1], halves[1 - (fi & 1)], bi])
    owners = plan.owners(fi, bi)
    spots = plan.gathered(fi, bi)
    call = Chain()

    def pair_spec(rows, cols):
        return pl.BlockSpec((1, rows, cols), lambda i, *_: (i, 0, 0))

    def piece_ins(pieces):
        return [(value, ANYWHERE) for value in pieces]

    sems = pltpu.SemaphoreType.DMA((len(PIECES),))
    rows_d, rows_f = D // nf, FF // nf

    low_vec = vectors.astype(BF16)
    vec_parts = [low_vec, plan.exchange(low_vec, 1)]
    vec_parts += [plan.exchange(part, 2) for part in vec_parts]
    columns = []
    for spot in range(nf):
        chosen = vec_parts[0]
        for mask in range(1, nf):
            chosen = jnp.where((fi ^ mask) == spot, vec_parts[mask], chosen)
        columns.append(chosen)
    vec = jnp.concatenate(columns, axis=1).astype(F32)
    vec = jnp.pad(vec, ((0, 16 - NVEC), (0, 0)))
    vec_in = (vec, full(vec.shape))

    def cast(shard_list, after=()):
        rows = shard_list[0].shape[0]
        half = rows // 2
        cols = sum(value.shape[1] for value in shard_list)
        row = lambda i, place_ref: (i ^ place_ref[1], 0)
        shard, mine = call(
            cast_kernel,
            (2,),
            [place],
            [(value, pl.BlockSpec((half, value.shape[1]), row)) for value in shard_list],
            [
                (pl.BlockSpec((half, cols), row), (rows, cols), BF16),
                (pl.BlockSpec((half, cols), lambda i, *_: (0, 0)), (half, cols), BF16),
            ],
            [],
            spent(rows * cols / 2e5),
            "cast",
            after,
        )
        return [shard, plan.exchange(shard, 1), plan.exchange(mine, 2)]

    def spread_pieces(pieces, dep=None):
        near = pieces[2]
        ready = near if dep is None else later(near, dep)
        other = plan.exchange(ready, *plan.helper)
        return pieces[:2] + [near, other, plan.exchange(ready, 1)]

    def last_piece(pieces, dep=None):
        other = pieces[3]
        return pieces + [plan.exchange(other if dep is None else later(other, dep), 1)]

    set_a = cast([w_qkv])

    perm, tokp, img, dy = call(
        order_kernel,
        (pairs,),
        [mask_count],
        [
            (mask_pos.reshape(pairs, 1, slots), pl.BlockSpec((1, 1, slots), lambda i, *_: (i, 0, 0))),
            (tokens, pair_spec(length, D)),
            (cotangent, pair_spec(length, D)),
        ],
        [
            (pair_spec(length, length), (pairs, length, length), BF16),
            (pair_spec(length, D), (pairs, length, D), BF16),
            (pair_spec(length, LANES), (pairs, length, LANES), F32),
            (pair_spec(slots, D), (pairs, slots, D), BF16),
        ],
        [],
        spent(6),
        "order",
    )

    set_b = cast([w_out, w_fc1])
    near_a = set_a[2]
    set_a = last_piece(spread_pieces(set_a))
    set_c = cast([w_fc2], [near_a])

    n1, qkv = call(
        functools.partial(qkv_kernel, rows_d),
        (pairs,),
        [place],
        [(tokp, pair_spec(length, D)), (img, pair_spec(length, LANES)), vec_in] + piece_ins(set_a),
        [
            (pair_spec(length, D), (pairs, length, D), BF16),
            (pair_spec(length, 3 * D), (pairs, length, 3 * D), BF16),
        ],
        [pltpu.VMEM((D, 3 * D), BF16), sems],
        spent(1),
        "qkv",
    )

    near_b = set_b[2]
    set_b = spread_pieces(set_b, n1)
    (mixed,) = call(
        mix_kernel,
        (pairs,),
        [],
        [(qkv, pair_spec(length, 3 * D))],
        [(pair_spec(length, D), (pairs, length, D), BF16)],
        [],
        spent(1),
        "mix",
        [near_b],
    )

    set_b = last_piece(set_b, mixed)
    h1, n2, z, slope = call(
        functools.partial(fc1_kernel, rows_d),
        (pairs,),
        [place],
        [
            (tokp, pair_spec(length, D)),
            (img, pair_spec(length, LANES)),
            (mixed, pair_spec(length, D)),
            vec_in,
        ]
        + piece_ins(set_b),
        [
            (pair_spec(length, D), (pairs, length, D), F32),
            (pair_spec(length, D), (pairs, length, D), BF16),
            (pair_spec(length, FF), (pairs, length, FF), BF16),
            (pair_spec(slots, FF), (pairs, slots, FF), BF16),
        ],
        [pltpu.VMEM((D, D), BF16), pltpu.VMEM((D, FF), BF16), sems, sems],
        spent(18),
        "fc1",
    )

    def top_rows(cols, idx=lambda i, *_: (0, 0, 0)):
        return pl.BlockSpec((pairs, slots, cols), idx)

    def grad_outs(rows, cols, chunk):
        block = rows // nd
        if block % 8:
            return [(pl.BlockSpec((rows, chunk), lambda i, *_: (0, i)), (rows, cols), BF16)]
        spec = pl.BlockSpec((nd // 2, block, chunk), lambda i, *_: (0, 0, i))
        return [(spec, (nd // 2, block, cols), BF16)] * 2

    def grad_sum(outs):
        if len(outs) == 1:
            rows, cols = outs[0].shape
            blocks = jnp.take(outs[0].reshape(nd, rows // nd, cols), owners, axis=0)
            outs = [blocks[: nd // 2], blocks[nd // 2 :]]
        return Sum(plan, call, *outs)

    set_c = spread_pieces(set_c, n2)

    chunk = 2 * LANES
    *got, gb2 = call(
        gw2_kernel,
        (D // chunk,),
        [owners],
        [
            (z, top_rows(FF)),
            (dy, top_rows(chunk, lambda i, *_: (0, 0, i))),
        ],
        grad_outs(FF, D, chunk) + [(pl.BlockSpec((1, chunk), lambda i, *_: (0, i)), (1, D), F32)],
        [pltpu.VMEM((FF, pairs * slots), BF16), pltpu.VMEM((FF, chunk), F32)],
        spent(8),
        "gw2",
    )
    sum_2 = grad_sum(got)
    set_c = last_piece(set_c, gb2)

    df, gb1 = call(
        functools.partial(df_kernel, rows_f),
        (PARTS,),
        [place],
        [(dy, top_rows(D)), (slope, top_rows(D, lambda i, *_: (0, 0, i)))] + piece_ins(set_c),
        [
            (pl.BlockSpec((pairs * slots, D), lambda i, *_: (0, i)), (pairs * slots, FF), BF16),
            (pl.BlockSpec((1, D), lambda i, *_: (0, i)), (1, FF), F32),
        ],
        [pltpu.VMEM((FF, D), BF16), sems],
        spent(7),
        "df",
    )
    sum_2.add()

    some = 2 if pairs % 2 == 0 else 1
    some_spec = pl.BlockSpec((some, slots, D), lambda i, *_: (i, 0, 0))
    dh, dhr, da, mlp_sum = call(
        functools.partial(mlp_back_kernel, rows_d),
        (pairs // some,),
        [place],
        [
            (df, pl.BlockSpec((some * slots, FF), lambda i, *_: (i, 0))),
            (dy, some_spec),
            (h1, some_spec),
            vec_in,
        ]
        + piece_ins(set_b),
        [
            (some_spec, (pairs, slots, D), F32),
            (some_spec, (pairs, slots, D), BF16),
            (some_spec, (pairs, slots, D), BF16),
            (full((8, D)), (8, D), F32),
        ],
        [pltpu.VMEM((D, FF), BF16), pltpu.VMEM((D, D), BF16), sems, sems],
        spent(10),
        "mlp_back",
    )

    got = call(
        gw1o_kernel,
        (PARTS + 1,),
        [owners],
        [
            (n2, top_rows(D)),
            (
                df,
                pl.BlockSpec((pairs * slots, D), lambda i, *_: (0, jnp.minimum(i, PARTS - 1))),
            ),
            (mixed, top_rows(D)),
            (dhr, top_rows(D)),
        ],
        grad_outs(D, FF + D, D),
        [pltpu.VMEM((D, pairs * slots), BF16), pltpu.VMEM((D, D), F32)],
        spent(9),
        "gw1o",
    )
    sum_1 = grad_sum(got)
    sum_2.add()

    part_pairs = pairs // 2 if pairs % 2 == 0 else pairs
    back = None
    for number in range(pairs // part_pairs):
        base = number * part_pairs
        at = lambda rows, cols, base=base: pl.BlockSpec(
            (1, rows, cols), lambda i, *_: (base + i, 0, 0)
        )
        ins = [(qkv, at(length, 3 * D)), (da, at(slots, D))]
        if back is not None:
            ins += [(back[0], ANYWHERE), (back[1], ANYWHERE), (back[2], full((8, D)))]
        back = call(
            functools.partial(attn_back_kernel, back is not None),
            (part_pairs,),
            [],
            ins,
            [
                (at(slots, D), (pairs, slots, D), BF16),
                (at(length, 2 * D), (pairs, length, 2 * D), BF16),
                (full((8, D)), (8, D), F32),
            ],
            [],
            spent(12),
            "attn_back",
            aliases=None if back is None else {2: 0, 3: 1},
        )
        if number == 0:
            sum_1.add()
        sum_2.add()
    dq, dkv, attn_sum = back

    got = call(
        gqkv_kernel,
        (3,),
        [owners],
        [
            (n1, full((pairs, length, D))),
            (dq, full((pairs, slots, D))),
            (
                dkv,
                pl.BlockSpec((pairs, length, D), lambda i, *_: (0, 0, jnp.where(i == 2, 1, 0))),
            ),
        ],
        grad_outs(D, 3 * D, D),
        [pltpu.VMEM((D, pairs * length), BF16), pltpu.VMEM((D, D), F32)],
        spent(9),
        "gqkv",
    )
    sum_3 = grad_sum(got)
    while sum_2.count > 1:
        sum_2.add()
    sum_1.add()

    fallback = (D // nd) % 8 != 0 or (FF // nd) % 8 != 0

    def finish(total, which, masters, moments):
        _, rows, cols = total.parts[0].shape
        if fallback:
            grad = sum(part[0].astype(F32) for part in total.parts)
            start, news, states = 0, [], []
            for kind, master, (first, second) in zip(which, masters, moments):
                width = master.shape[1]
                own = lax.dynamic_slice_in_dim(master, bi * rows, rows, 0)
                new_w, new_m, new_v = adamw(
                    own,
                    grad[:, start : start + width],
                    first,
                    second,
                    STEP_RATES[kind],
                    DECAY_RATES[kind],
                )
                news.append(new_w.astype(BF16))
                states += [new_m, new_v]
                start += width
            block = jnp.concatenate(news, axis=1)[None]
        else:
            own = pl.BlockSpec((1, rows, cols), lambda i, *_: (0, 0, 0))
            ins = [(part, own) for part in total.parts]
            outs = [(full((1, rows, cols)), (1, rows, cols), BF16)]
            for master, pair in zip(masters, moments):
                width = master.shape[1]
                ins.append((master, pl.BlockSpec((rows, width), lambda i, place_ref: (place_ref[3], 0))))
                ins += [(value, full(value.shape)) for value in pair]
                outs += [(full((rows, width)), (rows, width), F32)] * 2
            block, *states = call(
                functools.partial(finish_kernel, len(total.parts), which),
                (1,),
                [place],
                ins,
                outs,
                [],
                spent(2),
                "finish",
            )
        return Spread(plan, call, block), states

    def put(moved, widths, before=None):
        if not fallback:
            return moved.put(spots, widths, before)
        if before is None:
            return moved.blocks
        blocks = jnp.concatenate([before, moved.got], axis=0)
        count, rows, cols = blocks.shape
        order = jnp.zeros(count, jnp.int32).at[spots].set(jnp.arange(count, dtype=jnp.int32))
        blocks = jnp.take(blocks, order, axis=0).reshape(count * rows, cols).astype(F32)
        cuts = np.cumsum([0] + list(widths))
        return [blocks[:, a:b] for a, b in zip(cuts[:-1], cuts[1:])]

    last = plan.bbits
    moved_2, (new_m2, new_v2) = finish(sum_2, (3,), (w_fc2,), ((m_fc2, v_fc2),))
    sum_3.add()

    grad_tokens, vec_sum = call(
        functools.partial(grad_in_kernel, rows_d),
        (pairs,),
        [place],
        [
            (tokp, pair_spec(length, D)),
            (img, pair_spec(length, LANES)),
            vec_in,
            (dq, pair_spec(slots, D)),
            (dkv, pair_spec(length, 2 * D)),
            (dh, pair_spec(slots, D)),
            (perm, pair_spec(length, length)),
            (attn_sum, full((8, D))),
            (mlp_sum, full((8, D))),
            (gb1, full((1, FF))),
            (gb2, full((1, D))),
        ]
        + piece_ins(set_a),
        [
            (pair_spec(length, D), (pairs, length, D), F32),
            (full((16, D)), (16, D), F32),
        ],
        [pltpu.VMEM((D, 3 * D), BF16), sems],
        spent(15),
        "grad_in",
    )

    vec_gens = [1, 2] + plan.batch
    vec_got = plan.exchange(vec_sum, vec_gens[0])
    vec_place = 1

    def vec_step(total):
        nonlocal vec_sum, vec_got, vec_place
        if vec_place > len(vec_gens):
            total.add()
            return
        vec_sum = total.add((vec_sum, vec_got))
        vec_got = plan.exchange(vec_sum, vec_gens[vec_place]) if vec_place < len(vec_gens) else None
        vec_place += 1

    moved_2.join()
    sum_1.add()
    vec_step(sum_3)

    (layer_out,) = call(
        functools.partial(out_kernel, rows_f),
        (pairs,),
        [place],
        [
            (z, pair_spec(length, FF)),
            (h1, pair_spec(length, D)),
            vec_in,
            (perm, pair_spec(length, length)),
        ]
        + piece_ins(set_c),
        [(pair_spec(length, D), (pairs, length, D), BF16)],
        [pltpu.VMEM((FF, D), BF16), sems],
        spent(13),
        "out",
    )

    while sum_1.count > 1:
        sum_1.add()
    vec_step(sum_3)
    while moved_2.place < last:
        moved_2.join()
    put_2 = put(moved_2, (D,))
    while sum_3.count > 1:
        vec_step(sum_3)
    moved_1, (new_m1, new_v1, new_mo, new_vo) = finish(
        sum_1, (2, 1), (w_fc1, w_out), ((m_fc1, v_fc1), (m_out, v_out))
    )
    moved_3, (new_mq, new_vq) = finish(sum_3, (0,), (w_qkv,), ((m_qkv, v_qkv),))
    (new_2,) = put(moved_2, (D,), put_2)
    while moved_3.place < last:
        moved_1.join()
        moved_3.join()
    put_1 = put(moved_1, (FF, D))
    put_3 = put(moved_3, (3 * D,))
    new_1, new_o = put(moved_1, (FF, D), put_1)
    (new_q,) = put(moved_3, (3 * D,), put_3)

    while vec_place <= len(vec_gens):
        vec_sum = vec_sum + vec_got
        vec_got = plan.exchange(vec_sum, vec_gens[vec_place]) if vec_place < len(vec_gens) else None
        vec_place += 1
    states = jnp.concatenate([m_vec, v_vec], axis=0)[None]
    for rank in range(plan.bbits):
        got = plan.exchange(states, *(order[rank] for order in plan.gather))
        states = jnp.concatenate([states, got], axis=0)
    order = jnp.zeros(nb, jnp.int32).at[spots].set(jnp.arange(nb, dtype=jnp.int32))
    own_cols = D // nd
    states = jnp.transpose(jnp.take(states, order, axis=0), (1, 0, 2)).reshape(2 * NVEC, nb * own_cols)
    grad_vec = lax.dynamic_slice_in_dim(vec_sum[:NVEC], fi * nb * own_cols, nb * own_cols, 1)
    vec_new, all_m, all_v = adamw(
        vectors, grad_vec, states[:NVEC], states[NVEC:], STEP_RATES[4], DECAY_RATES[4]
    )
    new_mv = lax.dynamic_slice_in_dim(all_m, bi * own_cols, own_cols, 1)
    new_vv = lax.dynamic_slice_in_dim(all_v, bi * own_cols, own_cols, 1)

    return (
        layer_out,
        grad_tokens,
        new_q,
        new_mq,
        new_vq,
        new_o,
        new_mo,
        new_vo,
        new_1,
        new_m1,
        new_v1,
        new_2,
        new_m2,
        new_v2,
        vec_new,
        new_mv,
        new_vv,
    )


def solution(mesh):
    pairs = P(("batch", "fsdp"), None, None)
    weight = P("fsdp", None)
    state = P(("fsdp", "batch"), None)
    vec_state = P(None, ("fsdp", "batch"))
    matrix = (weight, state, state)
    return jax.shard_map(
        functools.partial(shards, Plan(mesh)),
        mesh=mesh,
        in_specs=(pairs, pairs, P(("batch", "fsdp"), None), P(("batch", "fsdp")))
        + matrix * 4
        + (P(None, "fsdp"), vec_state, vec_state),
        out_specs=(pairs, pairs) + matrix * 4 + (P(None, "fsdp"), vec_state, vec_state),
        check_vma=False,
    )
```

time: 409 us -> 336 us (0.82)
  waiting for transfers between devices: 137 us -> 20.8 us
  Pallas kernels: 159 us -> 236 us
  other arithmetic: 45.1 us -> 5.56 us
  local copies, waits for them, and re-layouts: 13.8 us -> 24.7 us
  starting transfers between devices: 50.9 us -> 44.9 us
    ppermute x55 -> x50, waiting for transfers between devices: 137 us -> 20.8 us  [exchange(): return lax.ppermute(value, ('batch', 'fsdp'), pairs)]
    pallas_call x15 -> x43, Pallas kernels: 159 us -> 236 us  [__call__(): pl.pallas_call(body, grid_spec=pltpu.PrefetchScalarGridSpec(num_scalar_pr...]
    convert_element_type x24 -> x0, other arithmetic: 27.6 us -> none  [the longest x12 18.5 us: scatter_sum(): send = total.astype(BF16)]
    unnamed x64 -> x92, local copies, waits for them, and re-layouts: 3.2 us -> 22 us
    concatenate x12 -> x3, other arithmetic: 6.89 us -> 0.02 us  [shards(): states = jnp.concatenate([states, got], axis=0)]
    ppermute x55 -> x50, starting transfers between devices: 50.9 us -> 44.9 us  [exchange(): return lax.ppermute(value, ('batch', 'fsdp'), pairs)]
    broadcast_in_dim x4 -> x1, other arithmetic: 5.18 us -> 0.07 us  [shards(): states = jnp.concatenate([m_vec, v_vec], axis=0)[None]]
  transfers between devices with their start and end apart: 55 -> 50, of which waited for: 27 -> 9; matrix products, arithmetic and copies ran while one was open for 12% -> 2% of each run, Pallas kernels for 20% -> 69%
where the time goes in v2:
time: 336 us; the launch traced here: 334 us
  Pallas kernels  236 us (70%)
  starting transfers between devices  44.9 us (13%)
  local copies, waits for them, and re-layouts  24.7 us (7%)
  waiting for transfers between devices  20.8 us (6%)
  other arithmetic  5.56 us (2%)
    pallas_call x43, Pallas kernels, __call__(): pl.pallas_call(body, grid_spec=pltpu.PrefetchScalarGridSpec(num_scalar_pr...  236 us
    ppermute x50, starting transfers between devices, exchange(): return lax.ppermute(value, ('batch', 'fsdp'), pairs)  44.9 us
    unnamed x92, local copies, waits for them, and re-layouts  22 us
    ppermute x50, waiting for transfers between devices, exchange(): return lax.ppermute(value, ('batch', 'fsdp'), pairs)  20.8 us
  transfers between devices with their start and end apart: 50, of which 9 were waited for; matrix products, arithmetic and copies ran while one was open for 2% of the time, Pallas kernels for 69%

profile of v2, /device:TPU:0, one launch (start us, length us, event | category | flops | bytes accessed | tf_op | source)
XLA Modules:
  0.0 333.5 jit_solution(16472416029423247532)
XLA Ops:
  10.5 6.0 %order.1 = (bf16[4,256,256]{2,1,0:T(8,128)(2,1)}, bf16[4,256,768]{2,1,0:T(8,128)(2,1)}, f32[4,256,128]{2,1,0:T(8,128)}, bf16[4,128,768]{2,1,0:T(8,128)(2,1)}) custom-call(s32[4]{0:T(128)} %refs_0_.1, s32[4,1,128]{2,1,0:T(1,128)} %bitcast.13, bf16[4,256,768]{2,1,0:T(8,128)(2,1)} %refs_2_.2, bf16[4,256,768]{2,1,0:T(8,128)(2,1)} %refs_3_.1, ...), custom_call_target="tpu_custom_call" | custom-call | flops 17999998976 | bytes 60000000 | tf_op jit(solution)/shard_map/order/pallas_call | solution.py:585
  18.4 4.5 %collective-permute-done.4.refs_2_.refs_6_.refs_14_ = bf16[96,2304]{1,0:T(8,128)(2,1)S(1)} collective-permute-done((bf16[96,2304]{1,0:T(8,128)(2,1)}, bf16[96,2304]{1,0:T(8,128)(2,1)S(1)}, u32[]{:S(2)}, u32[]{:S(2)}) %collective-permute-start.4) | collective-permute-done | bytes 442400 | tf_op jit(solution)/shard_map/ppermute | solution.py:111
  24.5 3.8 %cast.4 = (bf16[192,3840]{1,0:T(8,128)(2,1)}, bf16[96,3840]{1,0:T(8,128)(2,1)}) custom-call(s32[4]{0:T(128)} %pad_add_fusion.1.refs_0_, f32[192,768]{1,0:T(8,128)} %refs_10_.1, f32[192,3072]{1,0:T(8,128)} %refs_7_.4, bf16[4,128,768]{2,1,0:T(8,128)(2,1)} %get-tuple-element.83.refs_3_.refs_2_.refs_1_), custom_call_target="tpu_custom_call" | custom-call | flops 11059200000 | bytes 36864000 | tf_op jit(solution)/shard_map/cast/pallas_call | solution.py:585
  31.2 3.4 %cast.5 = (bf16[768,768]{1,0:T(8,128)(2,1)}, bf16[384,768]{1,0:T(8,128)(2,1)}) custom-call(s32[4]{0:T(128)} %pad_add_fusion.1.refs_0_, f32[768,768]{1,0:T(8,128)} %refs_7_.3, bf16[96,2304]{1,0:T(8,128)(2,1)} %copy-done.23, bf16[96,3840]{1,0:T(8,128)(2,1)} %get-tuple-element.84.refs_3_), custom_call_target="tpu_custom_call" | custom-call | flops 8847360000 | bytes 29491200 | tf_op jit(solution)/shard_map/cast/pallas_call | solution.py:585
  35.7 10.6 %qkv.1 = (bf16[4,256,768]{2,1,0:T(8,128)(2,1)}, bf16[4,256,2304]{2,1,0:T(8,128)(2,1)}) custom-call(s32[4]{0:T(128)} %pad_add_fusion.1.refs_0_, bf16[4,256,768]{2,1,0:T(8,128)(2,1)} %get-tuple-element.80.refs_1_, f32[4,256,128]{2,1,0:T(8,128)} %get-tuple-element.81.refs_2_, f32[16,768]{1,0:T(8,128)} %fusion.7.refs_3_.refs_4_, ...), custom_call_target="tpu_custom_call" | custom-call | flops 3000000000 | bytes 10000000 | tf_op jit(solution)/shard_map/qkv/pallas_call | solution.py:585
  48.5 10.4 %mix.1.refs_3_.refs_11_ = bf16[4,256,768]{2,1,0:T(8,128)(2,1)} custom-call(bf16[4,256,2304]{2,1,0:T(8,128)(2,1)} %get-tuple-element.86.refs_0_.refs_2_, bf16[96,3840]{1,0:T(8,128)(2,1)} %copy-done, bf16[4,256,2304]{2,1,0:T(8,128)(2,1)} %get-tuple-element.86.refs_0_.refs_2_), custom_call_target="tpu_custom_call" | custom-call | flops 3000000000 | bytes 10000000 | tf_op jit(solution)/shard_map/mix/pallas_call | solution.py:585
  61.5 17.9 %fc1.1 = (f32[4,256,768]{2,1,0:T(8,128)}, bf16[4,256,768]{2,1,0:T(8,128)(2,1)}, bf16[4,256,3072]{2,1,0:T(8,128)(2,1)}, bf16[4,128,3072]{2,1,0:T(8,128)(2,1)}) custom-call(s32[4]{0:T(128)} %pad_add_fusion.1.refs_0_, bf16[4,256,768]{2,1,0:T(8,128)(2,1)} %get-tuple-element.80.refs_1_, f32[4,256,128]{2,1,0:T(8,128)} %get-tuple-element.81.refs_2_, ...), custom_call_target="tpu_custom_call" | custom-call | flops 54000001024 | bytes 180000000 | tf_op jit(solution)/shard_map/fc1/pallas_call | solution.py:585
  80.9 8.2 %gw2.1 = (bf16[16,96,768]{2,1,0:T(8,128)(2,1)}, bf16[16,96,768]{2,1,0:T(8,128)(2,1)}, f32[1,768]{1,0:T(1,128)}) custom-call(s32[32]{0:T(128)} %shift-right-arithmetic_add_fusion.refs_0_, bf16[4,256,3072]{2,1,0:T(8,128)(2,1)} %get-tuple-element.91.refs_1_, bf16[4,128,768]{2,1,0:T(8,128)(2,1)} %get-tuple-element.83.refs_3_.refs_2_.refs_1_, ...), custom_call_target="tpu_custom_call" | custom-call | flops 24000000000 | bytes 80000000 | tf_op jit(solution)/shard_map/gw2/pallas_call | solution.py:585
  92.0 9.5 %df.1 = (bf16[512,3072]{1,0:T(8,128)(2,1)}, f32[1,3072]{1,0:T(1,128)}) custom-call(s32[4]{0:T(128)} %pad_add_fusion.1.refs_0_, bf16[4,128,768]{2,1,0:T(8,128)(2,1)} %get-tuple-element.83.refs_3_.refs_2_.refs_1_, bf16[4,128,3072]{2,1,0:T(8,128)(2,1)} %get-tuple-element.97.refs_3_.refs_2_, bf16[768,768]{1,0:T(8,128)(2,1)} %get-tuple-element.94.refs_3_.refs_5_, ...), custom_call_target="tpu_custom_call" | custom-call | flops 20999999488 | bytes 70000000 | tf_op jit(solution)/shard_map/df/pallas_call | solution.py:585
  102.9 3.7 %add.108.refs_11_ = bf16[8,96,768]{2,1,0:T(8,128)(2,1)} custom-call(bf16[16,96,768]{2,1,0:T(8,128)(2,1)} %get-tuple-element.101.refs_0_.refs_1_, bf16[16,96,768]{2,1,0:T(8,128)(2,1)} %copy-done.15, f32[1,3072]{1,0:T(1,128)} %get-tuple-element.103.refs_2_.refs_10_), custom_call_target="tpu_custom_call" | custom-call | flops 4499999744 | bytes 15000000 | tf_op jit(solution)/shard_map/add/pallas_call | solution.py:585
  107.1 11.5 %mlp_back.1 = (f32[4,128,768]{2,1,0:T(8,128)}, bf16[4,128,768]{2,1,0:T(8,128)(2,1)}, bf16[4,128,768]{2,1,0:T(8,128)(2,1)}, f32[8,768]{1,0:T(8,128)}) custom-call(s32[4]{0:T(128)} %pad_add_fusion.1.refs_0_, bf16[512,3072]{1,0:T(8,128)(2,1)} %get-tuple-element.100.refs_1_.refs_2_, bf16[4,128,768]{2,1,0:T(8,128)(2,1)} %get-tuple-element.83.refs_3_.refs_2_.refs_1_, ...), custom_call_target="tpu_custom_call" | custom-call | flops 30000001024 | bytes 100000000 | tf_op jit(solution)/shard_map/mlp_back/pallas_call | solution.py:585
  118.6 9.3 %gw1o.1 = (bf16[16,24,3840]{2,1,0:T(8,128)(2,1)}, bf16[16,24,3840]{2,1,0:T(8,128)(2,1)}) custom-call(s32[32]{0:T(128)} %shift-right-arithmetic_add_fusion.refs_0_, bf16[4,256,768]{2,1,0:T(8,128)(2,1)} %get-tuple-element.95.refs_1_, bf16[512,3072]{1,0:T(8,128)(2,1)} %get-tuple-element.100.refs_1_.refs_2_, bf16[4,256,768]{2,1,0:T(8,128)(2,1)} %mix.1.refs_3_.refs_11_, ...), custom_call_target="tpu_custom_call" | custom-call | flops 27000000512 | bytes 90000000 | tf_op jit(solution)/shard_map/gw1o/pallas_call | solution.py:585
  128.7 3.6 %add.109.refs_2_ = bf16[4,96,768]{2,1,0:T(8,128)(2,1)} custom-call(bf16[16,96,768]{2,1,0:T(8,128)(2,1)} %get-tuple-element.101.refs_0_.refs_1_, bf16[16,96,768]{2,1,0:T(8,128)(2,1)} %copy-done.15, bf16[8,96,768]{2,1,0:T(8,128)(2,1)} %collective-permute-done.19.refs_2_.refs_3_, bf16[16,24,3840]{2,1,0:T(8,128)(2,1)} %get-tuple-element.107.refs_3_), custom_call_target="tpu_custom_call" | custom-call | flops 4499999744 | bytes 15000000 | tf_op jit(solution)/shard_map/add/pallas_call | solution.py:585
  133.1 13.5 %attn_back.2 = (bf16[4,128,768]{2,1,0:T(8,128)(2,1)}, bf16[4,256,1536]{2,1,0:T(8,128)(2,1)}, f32[8,768]{1,0:T(8,128)}) custom-call(bf16[4,256,2304]{2,1,0:T(8,128)(2,1)} %get-tuple-element.86.refs_0_.refs_2_, bf16[4,128,768]{2,1,0:T(8,128)(2,1)} %get-tuple-element.104.refs_1_, bf16[4,96,768]{2,1,0:T(8,128)(2,1)} %add.109.refs_2_), custom_call_target="tpu_custom_call" | custom-call | flops 35999997952 | bytes 120000000 | tf_op jit(solution)/shard_map/attn_back/pallas_call | solution.py:585
  148.2 3.9 %add.110.refs_4_ = bf16[8,24,3840]{2,1,0:T(8,128)(2,1)} custom-call(bf16[16,24,3840]{2,1,0:T(8,128)(2,1)} %get-tuple-element.111.refs_0_.refs_1_, bf16[16,24,3840]{2,1,0:T(8,128)(2,1)} %copy-done.14, f32[8,768]{1,0:T(8,128)} %get-tuple-element.110.refs_2_.refs_4_), custom_call_target="tpu_custom_call" | custom-call | flops 4499999744 | bytes 15000000 | tf_op jit(solution)/shard_map/add/pallas_call | solution.py:585
  157.2 13.5 %attn_back.3 = (bf16[4,128,768]{2,1,0:T(8,128)(2,1)}, bf16[4,256,1536]{2,1,0:T(8,128)(2,1)}, f32[8,768]{1,0:T(8,128)}) custom-call(bf16[4,256,2304]{2,1,0:T(8,128)(2,1)} %get-tuple-element.86.refs_0_.refs_2_, bf16[4,128,768]{2,1,0:T(8,128)(2,1)} %get-tuple-element.104.refs_1_, ...), custom_call_target="tpu_custom_call", output_to_operand_aliasing={{0}: (2, {}), {1}: (3, {})} | custom-call | flops 35999997952 | bytes 120000000 | tf_op jit(solution)/shard_map/attn_back/pallas_call | solution.py:585
  173.4 9.1 %gqkv.1 = (bf16[16,24,2304]{2,1,0:T(8,128)(2,1)}, bf16[16,24,2304]{2,1,0:T(8,128)(2,1)}) custom-call(s32[32]{0:T(128)} %shift-right-arithmetic_add_fusion.refs_0_, bf16[4,256,768]{2,1,0:T(8,128)(2,1)} %get-tuple-element.88.refs_1_, bf16[4,128,768]{2,1,0:T(8,128)(2,1)} %get-tuple-element.112.refs_2_.refs_4_, ...), custom_call_target="tpu_custom_call" | custom-call | flops 27000000512 | bytes 90000000 | tf_op jit(solution)/shard_map/gqkv/pallas_call | solution.py:585
  182.6 3.2 collective-permute-start.45
  187.8 3.6 %add.113.refs_10_ = bf16[4,24,3840]{2,1,0:T(8,128)(2,1)} custom-call(bf16[16,24,3840]{2,1,0:T(8,128)(2,1)} %get-tuple-element.111.refs_0_.refs_1_, bf16[16,24,3840]{2,1,0:T(8,128)(2,1)} %copy-done.14, bf16[8,24,3840]{2,1,0:T(8,128)(2,1)} %collective-permute-done.25.refs_2_.refs_3_, bf16[16,24,2304]{2,1,0:T(8,128)(2,1)} %get-tuple-element.116.refs_3_), custom_call_target="tpu_custom_call" | custom-call | flops 4499999744 | bytes 15000000 | tf_op jit(solution)/shard_map/add/pallas_call | solution.py:585
  191.4 3.6 %collective-permute-done.24.refs_6_ = bf16[1,96,768]{2,1,0:T(8,128)(2,1)S(1)} collective-permute-done((bf16[1,96,768]{2,1,0:T(8,128)(2,1)S(1)}, bf16[1,96,768]{2,1,0:T(8,128)(2,1)S(1)}, u32[]{:S(2)}, u32[]{:S(2)}) %collective-permute-start.24) | collective-permute-done | bytes 147488 | tf_op jit(solution)/shard_map/ppermute | solution.py:111
  195.7 3.3 finish.3
  200.8 3.6 %add.114.refs_18_ = bf16[8,24,2304]{2,1,0:T(8,128)(2,1)} custom-call(bf16[16,24,2304]{2,1,0:T(8,128)(2,1)} %get-tuple-element.115.refs_0_.refs_1_, bf16[16,24,2304]{2,1,0:T(8,128)(2,1)} %copy-done.16, f32[96,768]{1,0:T(8,128)} %get-tuple-element.75.refs_2_), custom_call_target="tpu_custom_call" | custom-call | flops 4499999744 | bytes 15000000 | tf_op jit(solution)/shard_map/add/pallas_call | solution.py:585
  205.6 15.1 %grad_in.1 = (f32[4,256,768]{2,1,0:T(8,128)}, f32[16,768]{1,0:T(8,128)}) custom-call(s32[4]{0:T(128)} %pad_add_fusion.1.refs_0_, bf16[4,256,768]{2,1,0:T(8,128)(2,1)} %get-tuple-element.80.refs_1_, f32[4,256,128]{2,1,0:T(8,128)} %get-tuple-element.81.refs_2_, f32[16,768]{1,0:T(8,128)} %fusion.7.refs_3_.refs_4_, ...), custom_call_target="tpu_custom_call" | custom-call | flops 44999999488 | bytes 150000000 | tf_op jit(solution)/shard_map/grad_in/pallas_call | solution.py:585
  229.7 3.5 %add.116 = (bf16[4,24,2304]{2,1,0:T(8,128)(2,1)}, f32[16,768]{1,0:T(8,128)}) custom-call(bf16[16,24,2304]{2,1,0:T(8,128)(2,1)} %get-tuple-element.115.refs_0_.refs_1_, bf16[16,24,2304]{2,1,0:T(8,128)(2,1)} %copy-done.16, bf16[8,24,2304]{2,1,0:T(8,128)(2,1)} %copy-done.20, f32[16,768]{1,0:T(8,128)} %get-tuple-element.119.refs_2_.refs_3_, ...), custom_call_target="tpu_custom_call" | custom-call | flops 4499999744 | bytes 15000000 | tf_op jit(solution)/shard_map/add/pallas_call | solution.py:585
  235.6 13.0 %out.1.refs_5_ = bf16[4,256,768]{2,1,0:T(8,128)(2,1)} custom-call(s32[4]{0:T(128)} %pad_add_fusion.1.refs_0_, bf16[4,256,3072]{2,1,0:T(8,128)(2,1)} %get-tuple-element.91.refs_1_, f32[4,256,768]{2,1,0:T(8,128)} %get-tuple-element.92.refs_3_.refs_2_, f32[16,768]{1,0:T(8,128)} %fusion.7.refs_3_.refs_4_, ...), custom_call_target="tpu_custom_call" | custom-call | flops 38999998464 | bytes 130000000 | tf_op jit(solution)/shard_map/out/pallas_call | solution.py:585
  263.6 4.0 %place.6.refs_7_.refs_2_ = f32[768,768]{1,0:T(8,128)} custom-call(s32[8]{0:T(128)} %get-tuple-element.145.refs_0_, bf16[4,96,768]{2,1,0:T(8,128)(2,1)} %join.7.refs_1_.refs_2_, bf16[4,96,768]{2,1,0:T(8,128)(2,1)} %join.7.refs_1_.refs_2_), custom_call_target="tpu_custom_call" | custom-call | flops 300000000 | bytes 1000000 | tf_op jit(solution)/shard_map/place/pallas_call | solution.py:585
  272.9 3.5 %finish.4 = (bf16[1,24,3840]{2,1,0:T(8,128)(2,1)}, f32[24,3072]{1,0:T(8,128)}, f32[24,3072]{1,0:T(8,128)}, f32[24,768]{1,0:T(8,128)}, f32[24,768]{1,0:T(8,128)}) custom-call(s32[4]{0:T(128)} %pad_add_fusion.1.refs_0_, bf16[16,24,3840]{2,1,0:T(8,128)(2,1)} %get-tuple-element.111.refs_0_.refs_1_, bf16[16,24,3840]{2,1,0:T(8,128)(2,1)} %copy-done.14, ...), custom_call_target="tpu_custom_call" | custom-call | flops 6000000000 | bytes 20000000 | tf_op jit(solution)/shard_map/finish/pallas_call | solution.py:585
  283.3 4.0 %place.7.refs_2_ = f32[768,768]{1,0:T(8,128)} custom-call(s32[8]{0:T(128)} %get-tuple-element.145.refs_0_, bf16[4,96,768]{2,1,0:T(8,128)(2,1)} %copy-done.2, f32[768,768]{1,0:T(8,128)} %place.6.refs_7_.refs_2_, f32[24,2304]{1,0:T(8,128)} %get-tuple-element.66.refs_3_), custom_call_target="tpu_custom_call", output_to_operand_aliasing={{}: (2, {})} | custom-call | flops 300000000 | bytes 1000000 | tf_op jit(solution)/shard_map/place/pallas_call | solution.py:585
  316.0 4.0 %place.8 = (f32[192,3072]{1,0:T(8,128)}, f32[192,768]{1,0:T(8,128)}) custom-call(s32[8]{0:T(128)} %get-tuple-element.145.refs_0_, bf16[4,24,3840]{2,1,0:T(8,128)(2,1)} %join.10.refs_2_.refs_1_, bf16[4,24,2304]{2,1,0:T(8,128)(2,1)} %join.11.refs_2_.refs_1_), custom_call_target="tpu_custom_call" | custom-call | flops 300000000 | bytes 1000000 | tf_op jit(solution)/shard_map/place/pallas_call | solution.py:585
  320.1 3.9 %place.9.refs_4_.refs_2_ = f32[192,2304]{1,0:T(8,128)} custom-call(s32[8]{0:T(128)} %get-tuple-element.145.refs_0_, bf16[4,24,2304]{2,1,0:T(8,128)(2,1)} %join.11.refs_2_.refs_1_, f32[192,768]{1,0:T(8,128)} %get-tuple-element.132.refs_2_.refs_3_), custom_call_target="tpu_custom_call" | custom-call | flops 300000000 | bytes 1000000 | tf_op jit(solution)/shard_map/place/pallas_call | solution.py:585
  324.8 4.0 %place.10 = (f32[192,3072]{1,0:T(8,128)}, f32[192,768]{1,0:T(8,128)}) custom-call(s32[8]{0:T(128)} %get-tuple-element.145.refs_0_, bf16[4,24,3840]{2,1,0:T(8,128)(2,1)} %copy-done.1, f32[192,3072]{1,0:T(8,128)} %get-tuple-element.133.refs_2_, f32[192,768]{1,0:T(8,128)} %get-tuple-element.132.refs_2_.refs_3_, ...), custom_call_target="tpu_custom_call", output_to_operand_aliasing={{0}: (2, {}), {1}: (3, {})} | custom-call | flops 300000000 | bytes 1000000 | tf_op jit(solution)/shard_map/place/pallas_call | solution.py:585
  329.7 3.9 %place.11 = f32[192,2304]{1,0:T(8,128)} custom-call(s32[8]{0:T(128)} %get-tuple-element.145.refs_0_, bf16[4,24,2304]{2,1,0:T(8,128)(2,1)} %copy-done.3, f32[192,2304]{1,0:T(8,128)} %place.9.refs_4_.refs_2_, f32[192,768]{1,0:T(8,128)} %get-tuple-element.67.refs_3_), custom_call_target="tpu_custom_call", output_to_operand_aliasing={{}: (2, {})} | custom-call | flops 300000000 | bytes 1000000 | tf_op jit(solution)/shard_map/place/pallas_call | solution.py:585
  (230 shorter events, 113.6 us)
Async XLA Ops:
  1.4 15.2 %collective-permute-start = (bf16[14,192]{1,0:T(8,128)(2,1)S(1)}, bf16[14,192]{1,0:T(8,128)(2,1)S(1)}, u32[]{:S(2)}, u32[]{:S(2)}) collective-permute-start(bf16[14,192]{1,0:T(8,128)(2,1)S(1)} %convert_element_type.6), channel_id=1, source_target_pairs={{0,1},{1,0},{2,3},{3,2},{4,5},{5,4},{6,7},{7,6},{8,9},{9,8},{10,11... | collective-permute-start | bytes 16136 | tf_op jit(solution)/shard_map/ppermute | solution.py:111
  1.9 27.0 %collective-permute-start.2 = (bf16[14,192]{1,0:T(8,128)(2,1)S(1)}, bf16[14,192]{1,0:T(8,128)(2,1)S(1)}, u32[]{:S(2)}, u32[]{:S(2)}) collective-permute-start(bf16[14,192]{1,0:T(8,128)(2,1)S(1)} %convert_element_type.6), channel_id=1, source_target_pairs={{0,2},{1,3},{2,0},{3,1},{4,6},{5,7},{6,4},{7,5},{8,10},{9,11},{10,... | collective-permute-start | bytes 16136 | tf_op jit(solution)/shard_map/ppermute | solution.py:111
  10.0 24.6 %collective-permute-start.3 = (bf16[192,2304]{1,0:T(8,128)(2,1)}, bf16[192,2304]{1,0:T(8,128)(2,1)S(1)}, u32[]{:S(2)}, u32[]{:S(2)}) collective-permute-start(bf16[192,2304]{1,0:T(8,128)(2,1)} %get-tuple-element.82.refs_4_.refs_12_), channel_id=1, source_target_pairs={{0,1},{1,0},{2,3},{3,2},{4,5},{5,4},{6,7},{7,6},{8,9},{9,8},{10,11... | collective-permute-start | bytes 2654216 | tf_op jit(solution)/shard_map/ppermute | solution.py:111
  10.3 12.7 %collective-permute-start.4 = (bf16[96,2304]{1,0:T(8,128)(2,1)}, bf16[96,2304]{1,0:T(8,128)(2,1)S(1)}, u32[]{:S(2)}, u32[]{:S(2)}) collective-permute-start(bf16[96,2304]{1,0:T(8,128)(2,1)} %get-tuple-element.79.refs_4_), channel_id=1, source_target_pairs={{0,2},{1,3},{2,0},{3,1},{4,6},{5,7},{6,4},{7,5},{8,10},{9,11},{10,... | collective-permute-start | bytes 1327112 | tf_op jit(solution)/shard_map/ppermute | solution.py:111
  16.6 12.3 %collective-permute-start.1 = (bf16[14,192]{1,0:T(8,128)(2,1)S(1)}, bf16[14,192]{1,0:T(8,128)(2,1)S(1)}, u32[]{:S(2)}, u32[]{:S(2)}) collective-permute-start(bf16[14,192]{1,0:T(8,128)(2,1)S(1)} %collective-permute-done), channel_id=1, source_target_pairs={{0,2},{1,3},{2,0},{3,1},{4,6},{5,7},{6,4},{7,5},{8,10},{9,11},{10,... | collective-permute-start | bytes 16136 | tf_op jit(solution)/shard_map/ppermute | solution.py:111
  28.3 18.1 %collective-permute-start.8 = (bf16[96,3840]{1,0:T(8,128)(2,1)}, bf16[96,3840]{1,0:T(8,128)(2,1)S(1)}, u32[]{:S(2)}, u32[]{:S(2)}) collective-permute-start(bf16[96,3840]{1,0:T(8,128)(2,1)} %get-tuple-element.84.refs_3_), channel_id=1, source_target_pairs={{0,2},{1,3},{2,0},{3,1},{4,6},{5,7},{6,4},{7,5},{8,10},{9,11},{10,... | collective-permute-start | bytes 2211848 | tf_op jit(solution)/shard_map/ppermute | solution.py:111
  46.4 12.5 %collective-permute-start.10 = (bf16[96,3840]{1,0:T(8,128)(2,1)S(1)}, bf16[96,3840]{1,0:T(8,128)(2,1)}, u32[]{:S(2)}, u32[]{:S(2)}) collective-permute-start(bf16[96,3840]{1,0:T(8,128)(2,1)S(1)} %collective-permute-done.8.refs_1_.refs_7_), channel_id=1, source_target_pairs={{0,4},{1,9},{2,6},{3,11},{4,0},{5,13},{6,2},{7,15},{8,12},{9,1},{1... | collective-permute-start | bytes 2211848 | tf_op jit(solution)/shard_map/ppermute | solution.py:111
  48.0 12.3 %collective-permute-start.9 = (bf16[192,3840]{1,0:T(8,128)(2,1)S(1)}, bf16[192,3840]{1,0:T(8,128)(2,1)}, u32[]{:S(2)}, u32[]{:S(2)}) collective-permute-start(bf16[192,3840]{1,0:T(8,128)(2,1)S(1)} %copy-done.17), channel_id=1, source_target_pairs={{0,1},{1,0},{2,3},{3,2},{4,5},{5,4},{6,7},{7,6},{8,9},{9,8},{10,11... | collective-permute-start | bytes 4423688 | tf_op jit(solution)/shard_map/ppermute | solution.py:111
  48.2 12.1 %collective-permute-start.11 = (bf16[96,3840]{1,0:T(8,128)(2,1)S(1)}, bf16[96,3840]{1,0:T(8,128)(2,1)}, u32[]{:S(2)}, u32[]{:S(2)}) collective-permute-start(bf16[96,3840]{1,0:T(8,128)(2,1)S(1)} %collective-permute-done.8.refs_1_.refs_7_), channel_id=1, source_target_pairs={{0,1},{1,0},{2,3},{3,2},{4,5},{5,4},{6,7},{7,6},{8,9},{9,8},{10,11... | collective-permute-start | bytes 2211848 | tf_op jit(solution)/shard_map/ppermute | solution.py:111
  59.7 19.7 %collective-permute-start.14 = (bf16[384,768]{1,0:T(8,128)(2,1)}, bf16[384,768]{1,0:T(8,128)(2,1)}, u32[]{:S(2)}, u32[]{:S(2)}) collective-permute-start(bf16[384,768]{1,0:T(8,128)(2,1)} %get-tuple-element.85.refs_10_), channel_id=1, source_target_pairs={{0,2},{1,3},{2,0},{3,1},{4,6},{5,7},{6,4},{7,5},{8,10},{9,11},{10,... | collective-permute-start | bytes 1769480 | tf_op jit(solution)/shard_map/ppermute | solution.py:111
  60.3 30.6 %collective-permute-start.13 = (bf16[768,768]{1,0:T(8,128)(2,1)S(1)}, bf16[768,768]{1,0:T(8,128)(2,1)}, u32[]{:S(2)}, u32[]{:S(2)}) collective-permute-start(bf16[768,768]{1,0:T(8,128)(2,1)S(1)} %copy-done.18), channel_id=1, source_target_pairs={{0,1},{1,0},{2,3},{3,2},{4,5},{5,4},{6,7},{7,6},{8,9},{9,8},{10,11... | collective-permute-start | bytes 3538952 | tf_op jit(solution)/shard_map/ppermute | solution.py:111
  106.6 22.1 %collective-permute-start.19 = (bf16[8,96,768]{2,1,0:T(8,128)(2,1)}, bf16[8,96,768]{2,1,0:T(8,128)(2,1)}, u32[]{:S(2)}, u32[]{:S(2)}) collective-permute-start(bf16[8,96,768]{2,1,0:T(8,128)(2,1)} %add.108.refs_11_), channel_id=1, source_target_pairs={{0,2},{1,5},{2,0},{3,7},{4,6},{5,1},{6,4},{7,3},{8,10},{9,13},{10,... | collective-permute-start | bytes 3538952 | tf_op jit(solution)/shard_map/ppermute | solution.py:111
  127.9 18.7 %collective-permute-start.21 = (bf16[16,24,3840]{2,1,0:T(8,128)(2,1)}, bf16[16,24,3840]{2,1,0:T(8,128)(2,1)S(1)}, u32[]{:S(2)}, u32[]{:S(2)}) collective-permute-start(bf16[16,24,3840]{2,1,0:T(8,128)(2,1)} %get-tuple-element.107.refs_3_), channel_id=1, source_target_pairs={{0,1},{1,0},{2,3},{3,2},{4,5},{5,4},{6,7},{7,6},{8,9},{9,8},{10,11... | collective-permute-start | bytes 8847368 | tf_op jit(solution)/shard_map/ppermute | solution.py:111
  132.3 21.4 %collective-permute-start.20 = (bf16[4,96,768]{2,1,0:T(8,128)(2,1)}, bf16[4,96,768]{2,1,0:T(8,128)(2,1)S(1)}, u32[]{:S(2)}, u32[]{:S(2)}) collective-permute-start(bf16[4,96,768]{2,1,0:T(8,128)(2,1)} %add.109.refs_2_), channel_id=1, source_target_pairs={{0,8},{1,3},{2,10},{3,1},{4,12},{5,7},{6,14},{7,5},{8,0},{9,11},{1... | collective-permute-start | bytes 1769480 | tf_op jit(solution)/shard_map/ppermute | solution.py:111
  152.1 35.6 %collective-permute-start.25 = (bf16[8,24,3840]{2,1,0:T(8,128)(2,1)}, bf16[8,24,3840]{2,1,0:T(8,128)(2,1)}, u32[]{:S(2)}, u32[]{:S(2)}) collective-permute-start(bf16[8,24,3840]{2,1,0:T(8,128)(2,1)} %add.110.refs_4_), channel_id=1, source_target_pairs={{0,2},{1,5},{2,0},{3,7},{4,6},{5,1},{6,4},{7,3},{8,10},{9,13},{10,... | collective-permute-start | bytes 4423688 | tf_op jit(solution)/shard_map/ppermute | solution.py:111
  156.5 14.2 %collective-permute-start.22 = (bf16[2,96,768]{2,1,0:T(8,128)(2,1)}, bf16[2,96,768]{2,1,0:T(8,128)(2,1)S(1)}, u32[]{:S(2)}, u32[]{:S(2)}) collective-permute-start(bf16[2,96,768]{2,1,0:T(8,128)(2,1)} %add.111.refs_5_), channel_id=1, source_target_pairs={{0,4},{1,9},{2,6},{3,11},{4,0},{5,13},{6,2},{7,15},{8,12},{9,1},{1... | collective-permute-start | bytes 884744 | tf_op jit(solution)/shard_map/ppermute | solution.py:111
  182.5 17.1 %collective-permute-start.23 = (bf16[16,24,2304]{2,1,0:T(8,128)(2,1)}, bf16[16,24,2304]{2,1,0:T(8,128)(2,1)S(1)}, u32[]{:S(2)}, u32[]{:S(2)}) collective-permute-start(bf16[16,24,2304]{2,1,0:T(8,128)(2,1)} %get-tuple-element.116.refs_3_), channel_id=1, source_target_pairs={{0,1},{1,0},{2,3},{3,2},{4,5},{5,4},{6,7},{7,6},{8,9},{9,8},{10,11... | collective-permute-start | bytes 5308424 | tf_op jit(solution)/shard_map/ppermute | solution.py:111
  182.6 72.8 %collective-permute-start.45 = (f32[1,28,24]{1,2,0:T(8,128)S(1)}, f32[1,28,24]{1,2,0:T(8,128)S(1)}, u32[]{:S(2)}, u32[]{:S(2)}) collective-permute-start(f32[1,28,24]{1,2,0:T(8,128)S(1)} %maximum_bitcast_fusion), channel_id=1, source_target_pairs={{0,24},{1,25},{2,26},{3,27},{4,28},{5,29},{6,30},{7,31},{8,16},{9,... | collective-permute-start | bytes 8072 | tf_op jit(solution)/shard_map/ppermute | solution.py:111
  191.4 32.8 %collective-permute-start.28 = (bf16[4,24,3840]{2,1,0:T(8,128)(2,1)}, bf16[4,24,3840]{2,1,0:T(8,128)(2,1)S(1)}, u32[]{:S(2)}, u32[]{:S(2)}) collective-permute-start(bf16[4,24,3840]{2,1,0:T(8,128)(2,1)} %add.113.refs_10_), channel_id=1, source_target_pairs={{0,8},{1,3},{2,10},{3,1},{4,12},{5,7},{6,14},{7,5},{8,0},{9,11},{1... | collective-permute-start | bytes 2211848 | tf_op jit(solution)/shard_map/ppermute | solution.py:111
  199.0 21.8 %collective-permute-start.29 = (bf16[1,96,768]{2,1,0:T(8,128)(2,1)}, bf16[1,96,768]{2,1,0:T(8,128)(2,1)S(1)}, u32[]{:S(2)}, u32[]{:S(2)}) collective-permute-start(bf16[1,96,768]{2,1,0:T(8,128)(2,1)} %get-tuple-element.120.refs_0_), channel_id=1, source_target_pairs={{0,24},{1,25},{2,26},{3,27},{4,28},{5,29},{6,30},{7,31},{8,16},{9,... | collective-permute-start | bytes 442376 | tf_op jit(solution)/shard_map/ppermute | solution.py:111
  204.4 23.7 %collective-permute-start.26 = (bf16[8,24,2304]{2,1,0:T(8,128)(2,1)}, bf16[8,24,2304]{2,1,0:T(8,128)(2,1)S(1)}, u32[]{:S(2)}, u32[]{:S(2)}) collective-permute-start(bf16[8,24,2304]{2,1,0:T(8,128)(2,1)} %add.114.refs_18_), channel_id=1, source_target_pairs={{0,2},{1,5},{2,0},{3,7},{4,6},{5,1},{6,4},{7,3},{8,10},{9,13},{10,... | collective-permute-start | bytes 2654216 | tf_op jit(solution)/shard_map/ppermute | solution.py:111
  223.2 37.1 %collective-permute-start.35 = (bf16[2,96,768]{2,1,0:T(8,128)(2,1)}, bf16[2,96,768]{2,1,0:T(8,128)(2,1)S(1)}, u32[]{:S(2)}, u32[]{:S(2)}) collective-permute-start(bf16[2,96,768]{2,1,0:T(8,128)(2,1)} %join.6.refs_4_.refs_0_), channel_id=1, source_target_pairs={{0,8},{1,5},{2,10},{3,7},{4,12},{5,1},{6,14},{7,3},{8,0},{9,13},{1... | collective-permute-start | bytes 884744 | tf_op jit(solution)/shard_map/ppermute | solution.py:111
  227.3 21.3 %collective-permute-start.32 = (bf16[2,24,3840]{2,1,0:T(8,128)(2,1)}, bf16[2,24,3840]{2,1,0:T(8,128)(2,1)S(1)}, u32[]{:S(2)}, u32[]{:S(2)}) collective-permute-start(bf16[2,24,3840]{2,1,0:T(8,128)(2,1)} %add.115.refs_5_), channel_id=1, source_target_pairs={{0,4},{1,9},{2,6},{3,11},{4,0},{5,13},{6,2},{7,15},{8,12},{9,1},{1... | collective-permute-start | bytes 1105928 | tf_op jit(solution)/shard_map/ppermute | solution.py:111
  233.2 18.2 %collective-permute-start.30 = (bf16[4,24,2304]{2,1,0:T(8,128)(2,1)}, bf16[4,24,2304]{2,1,0:T(8,128)(2,1)S(1)}, u32[]{:S(2)}, u32[]{:S(2)}) collective-permute-start(bf16[4,24,2304]{2,1,0:T(8,128)(2,1)} %get-tuple-element.123), channel_id=1, source_target_pairs={{0,8},{1,3},{2,10},{3,1},{4,12},{5,7},{6,14},{7,5},{8,0},{9,11},{1... | collective-permute-start | bytes 1327112 | tf_op jit(solution)/shard_map/ppermute | solution.py:111
  234.1 17.3 %collective-permute-start.31 = (f32[16,768]{1,0:T(8,128)}, f32[16,768]{1,0:T(8,128)S(1)}, u32[]{:S(2)}, u32[]{:S(2)}) collective-permute-start(f32[16,768]{1,0:T(8,128)} %get-tuple-element.121.refs_11_.refs_4_), channel_id=1, source_target_pairs={{0,2},{1,3},{2,0},{3,1},{4,6},{5,7},{6,4},{7,5},{8,10},{9,11},{10,... | collective-permute-start | bytes 147464 | tf_op jit(solution)/shard_map/ppermute | solution.py:111
  254.7 12.9 %collective-permute-start.33 = (bf16[2,24,2304]{2,1,0:T(8,128)(2,1)}, bf16[2,24,2304]{2,1,0:T(8,128)(2,1)S(1)}, u32[]{:S(2)}, u32[]{:S(2)}) collective-permute-start(bf16[2,24,2304]{2,1,0:T(8,128)(2,1)} %get-tuple-element.124), channel_id=1, source_target_pairs={{0,4},{1,9},{2,6},{3,11},{4,0},{5,13},{6,2},{7,15},{8,12},{9,1},{1... | collective-permute-start | bytes 663560 | tf_op jit(solution)/shard_map/ppermute | solution.py:111
  255.4 34.3 %collective-permute-start.46 = (f32[2,28,24]{1,2,0:T(8,128)S(1)}, f32[2,28,24]{1,2,0:T(8,128)S(1)}, u32[]{:S(2)}, u32[]{:S(2)}) collective-permute-start(f32[2,28,24]{1,2,0:T(8,128)S(1)} %pad_maximum_fusion.2), channel_id=1, source_target_pairs={{0,8},{1,5},{2,10},{3,7},{4,12},{5,1},{6,14},{7,3},{8,0},{9,13},{1... | collective-permute-start | bytes 16136 | tf_op jit(solution)/shard_map/ppermute | solution.py:111
  256.6 15.6 %collective-permute-start.37 = (bf16[1,24,3840]{2,1,0:T(8,128)(2,1)S(1)}, bf16[1,24,3840]{2,1,0:T(8,128)(2,1)S(1)}, u32[]{:S(2)}, u32[]{:S(2)}) collective-permute-start(bf16[1,24,3840]{2,1,0:T(8,128)(2,1)S(1)} %copy-done.33), channel_id=1, source_target_pairs={{0,24},{1,25},{2,26},{3,27},{4,28},{5,29},{6,30},{7,31},{8,16},{9,... | collective-permute-start | bytes 552968 | tf_op jit(solution)/shard_map/ppermute | solution.py:111
  263.0 19.5 %collective-permute-start.40 = (bf16[4,96,768]{2,1,0:T(8,128)(2,1)}, bf16[4,96,768]{2,1,0:T(8,128)(2,1)S(1)}, u32[]{:S(2)}, u32[]{:S(2)}) collective-permute-start(bf16[4,96,768]{2,1,0:T(8,128)(2,1)} %join.7.refs_1_.refs_2_), channel_id=1, source_target_pairs={{0,4},{1,9},{2,6},{3,11},{4,0},{5,13},{6,2},{7,15},{8,12},{9,1},{1... | collective-permute-start | bytes 1769480 | tf_op jit(solution)/shard_map/ppermute | solution.py:111
  289.8 12.5 %collective-permute-start.42 = (bf16[2,24,3840]{2,1,0:T(8,128)(2,1)}, bf16[2,24,3840]{2,1,0:T(8,128)(2,1)S(1)}, u32[]{:S(2)}, u32[]{:S(2)}) collective-permute-start(bf16[2,24,3840]{2,1,0:T(8,128)(2,1)} %join.8.refs_2_.refs_0_), channel_id=1, source_target_pairs={{0,8},{1,5},{2,10},{3,7},{4,12},{5,1},{6,14},{7,3},{8,0},{9,13},{1... | collective-permute-start | bytes 1105928 | tf_op jit(solution)/shard_map/ppermute | solution.py:111
  305.0 19.0 %collective-permute-start.44 = (bf16[4,24,3840]{2,1,0:T(8,128)(2,1)}, bf16[4,24,3840]{2,1,0:T(8,128)(2,1)S(1)}, u32[]{:S(2)}, u32[]{:S(2)}) collective-permute-start(bf16[4,24,3840]{2,1,0:T(8,128)(2,1)} %join.10.refs_2_.refs_1_), channel_id=1, source_target_pairs={{0,4},{1,9},{2,6},{3,11},{4,0},{5,13},{6,2},{7,15},{8,12},{9,1},{1... | collective-permute-start | bytes 2211848 | tf_op jit(solution)/shard_map/ppermute | solution.py:111
  313.3 15.6 %collective-permute-start.43 = (bf16[4,24,2304]{2,1,0:T(8,128)(2,1)}, bf16[4,24,2304]{2,1,0:T(8,128)(2,1)S(1)}, u32[]{:S(2)}, u32[]{:S(2)}) collective-permute-start(bf16[4,24,2304]{2,1,0:T(8,128)(2,1)} %join.11.refs_2_.refs_1_), channel_id=1, source_target_pairs={{0,4},{1,9},{2,6},{3,11},{4,0},{5,13},{6,2},{7,15},{8,12},{9,1},{1... | collective-permute-start | bytes 1327112 | tf_op jit(solution)/shard_map/ppermute | solution.py:111
  (63 other events, 313.5 us)

commit v3 on v2

--- a/solution.py
+++ b/solution.py
@@ -116,20 +116,22 @@
             masks = np.concatenate([masks, masks ^ mask])
         return masks
 
-    def owners(self, fi, bi):
-        mine = bi * self.nf + fi
-        even, odd = (jnp.asarray(self.spans(order[1:]), jnp.int32) for order in self.scatter)
-        is_even = (fi & 1) == 0
-        keep = mine ^ jnp.where(is_even, even, odd)
-        send = (mine ^ 1) ^ jnp.where(is_even, odd, even)
-        index = jnp.concatenate([keep, send])
-        return (index & (self.nf - 1)) * self.nb + (index >> self.fbits)
-
-    def gathered(self, fi, bi):
-        even, odd = (
-            jnp.asarray(self.spans(gens[::-1]) >> self.fbits, jnp.int32) for gens in self.gather
-        )
-        return bi ^ jnp.where((fi & 1) == 0, even, odd)
+    def table(self):
+        rows = []
+        for index in range(self.nd):
+            core, fi, bi = index & 1, index & (self.nf - 1), index >> self.fbits
+            halves = (bi & 1, (bi >> 1) & 1)
+            keep = index ^ self.spans(self.scatter[core][1:])
+            send = (index ^ 1) ^ self.spans(self.scatter[1 - core][1:])
+            order = np.concatenate([keep, send])
+            owners = (order & (self.nf - 1)) * self.nb + (order >> self.fbits)
+            places = bi ^ (self.spans(self.gather[core][::-1]) >> self.fbits)
+            own = np.asarray([fi, halves[core], halves[1 - core], bi])
+            rows.append(np.concatenate([own, owners, places]))
+        return np.stack(rows).astype(np.int32)
+
+
+OWN = 4
 
 
 PIECES = ((0, None), (1, None), (2, 0), (2, 1), (3, 2), (3, 3))
@@ -235,21 +237,29 @@
     qkv_ref[0, :, 2 * D :] = (dot(n1, w_ref[:, 2 * D :]) + vec_ref[5:6, :]).astype(BF16)
 
 
+def lane_slab(slab):
+    return pl.ds(pl.multiple_of(slab * LANES, LANES), LANES)
+
+
 def mix_kernel(qkv_ref, a_ref):
     low = lax.broadcasted_iota(jnp.int32, (1, LANES), 1) < HDIM
-    for slab in range(SLABS):
-        cols = slice(slab * LANES, (slab + 1) * LANES)
-        q = qkv_ref[0, :, cols] * jnp.asarray(HDIM**-0.5, BF16)
-        k = qkv_ref[0, :, D + slab * LANES : D + (slab + 1) * LANES]
-        v = qkv_ref[0, :, 2 * D + slab * LANES : 2 * D + (slab + 1) * LANES]
-        outs = []
-        for head in range(2):
-            mine = low if head == 0 else jnp.logical_not(low)
-            scores = dot_last(jnp.where(mine, q, jnp.zeros_like(q)), k)
-            e = jnp.exp(scores - jnp.max(scores, axis=-1, keepdims=True))
-            p = (e * (1.0 / jnp.sum(e, axis=-1, keepdims=True))).astype(BF16)
-            outs.append(dot(p, v))
-        a_ref[0, :, cols] = jnp.where(low, outs[0], outs[1]).astype(BF16)
+    def some_slabs(turn, _):
+        for slab in (2 * turn, 2 * turn + 1):
+            cols = lane_slab(slab)
+            q = qkv_ref[0, :, cols] * jnp.asarray(HDIM**-0.5, BF16)
+            k = qkv_ref[0, :, lane_slab(slab + SLABS)]
+            v = qkv_ref[0, :, lane_slab(slab + 2 * SLABS)]
+            outs = []
+            for head in range(2):
+                mine = low if head == 0 else jnp.logical_not(low)
+                scores = dot_last(jnp.where(mine, q, jnp.zeros_like(q)), k)
+                e = jnp.exp(scores - jnp.max(scores, axis=-1, keepdims=True))
+                p = (e * (1.0 / jnp.sum(e, axis=-1, keepdims=True))).astype(BF16)
+                outs.append(dot(p, v))
+            a_ref[0, :, cols] = jnp.where(low, outs[0], outs[1]).astype(BF16)
+        return 0
+
+    lax.fori_loop(0, SLABS // 2, some_slabs, 0)
 
 
 def fc1_kernel(rows, place_ref, tok_ref, img_ref, a_ref, vec_ref, *refs):
@@ -292,10 +302,14 @@
         return
     keep_ref, send_ref = outs
     half, block, _ = send_ref.shape
-    for out_ref, base in ((send_ref, half), (keep_ref, 0)):
-        for spot in range(half):
-            start = pl.multiple_of(owners_ref[base + spot] * block, 8)
+
+    def one(spot, _):
+        for out_ref, base in ((send_ref, half), (keep_ref, 0)):
+            start = pl.multiple_of(owners_ref[OWN + base + spot] * block, 8)
             out_ref[spot] = acc_ref[pl.ds(start, block), :].astype(BF16)
+        return 0
+
+    lax.fori_loop(0, half, one, 0)
 
 
 def gw2_kernel(owners_ref, z_ref, dy_ref, *refs):
@@ -396,32 +410,36 @@
 
     low = lax.broadcasted_iota(jnp.int32, (1, LANES), 1) < HDIM
     scale = jnp.asarray(HDIM**-0.5, BF16)
-    for slab in range(SLABS):
-        cols = slice(slab * LANES, (slab + 1) * LANES)
-        q = qkv_ref[0, :slots, cols] * scale
-        k = qkv_ref[0, :, D + slab * LANES : D + (slab + 1) * LANES]
-        v = qkv_ref[0, :, 2 * D + slab * LANES : 2 * D + (slab + 1) * LANES]
-        da = da_ref[0, :, cols]
-        gqs, gks, gvs = [], [], []
-        for head in range(2):
-            mine = low if head == 0 else jnp.logical_not(low)
-            zero = jnp.zeros_like(q)
-            scores = dot_last(jnp.where(mine, q, zero), k)
-            e = jnp.exp(scores - jnp.max(scores, axis=-1, keepdims=True))
-            p = e * (1.0 / jnp.sum(e, axis=-1, keepdims=True))
-            gvs.append(dot_first(p.astype(BF16), da))
-            dp = dot_last(jnp.where(mine, da, zero), v)
-            ds = (p * (dp - jnp.sum(p * dp, axis=-1, keepdims=True))).astype(BF16)
-            gqs.append(dot(ds, k))
-            gks.append(dot_first(ds, q))
-        gq = jnp.where(low, gqs[0], gqs[1]) * (HDIM**-0.5)
-        gk = jnp.where(low, gks[0], gks[1])
-        gv = jnp.where(low, gvs[0], gvs[1])
-        dq_ref[0, :, cols] = gq.astype(BF16)
-        dkv_ref[0, :, cols] = gk.astype(BF16)
-        dkv_ref[0, :, D + slab * LANES : D + (slab + 1) * LANES] = gv.astype(BF16)
-        sum_ref[0:1, cols] += jnp.sum(gq, axis=0, keepdims=True)
-        sum_ref[1:2, cols] += jnp.sum(gv, axis=0, keepdims=True)
+    def some_slabs(turn, _):
+        for slab in (2 * turn, 2 * turn + 1):
+            cols = lane_slab(slab)
+            q = qkv_ref[0, :slots, cols] * scale
+            k = qkv_ref[0, :, lane_slab(slab + SLABS)]
+            v = qkv_ref[0, :, lane_slab(slab + 2 * SLABS)]
+            da = da_ref[0, :, cols]
+            gqs, gks, gvs = [], [], []
+            for head in range(2):
+                mine = low if head == 0 else jnp.logical_not(low)
+                zero = jnp.zeros_like(q)
+                scores = dot_last(jnp.where(mine, q, zero), k)
+                e = jnp.exp(scores - jnp.max(scores, axis=-1, keepdims=True))
+                p = e * (1.0 / jnp.sum(e, axis=-1, keepdims=True))
+                gvs.append(dot_first(p.astype(BF16), da))
+                dp = dot_last(jnp.where(mine, da, zero), v)
+                ds = (p * (dp - jnp.sum(p * dp, axis=-1, keepdims=True))).astype(BF16)
+                gqs.append(dot(ds, k))
+                gks.append(dot_first(ds, q))
+            gq = jnp.where(low, gqs[0], gqs[1]) * (HDIM**-0.5)
+            gk = jnp.where(low, gks[0], gks[1])
+            gv = jnp.where(low, gvs[0], gvs[1])
+            dq_ref[0, :, cols] = gq.astype(BF16)
+            dkv_ref[0, :, cols] = gk.astype(BF16)
+            dkv_ref[0, :, lane_slab(slab + SLABS)] = gv.astype(BF16)
+            sum_ref[0:1, cols] += jnp.sum(gq, axis=0, keepdims=True)
+            sum_ref[1:2, cols] += jnp.sum(gv, axis=0, keepdims=True)
+        return 0
+
+    lax.fori_loop(0, SLABS // 2, some_slabs, 0)
 
 
 def gqkv_kernel(owners_ref, n1_ref, dq_ref, dkv_ref, *refs):
@@ -516,50 +534,192 @@
     out_ref[0] = dot(perm_ref[0], y.astype(BF16)).astype(BF16)
 
 
-def add_kernel(count, *refs):
-    ins, outs = refs[: -1 - (len(refs) > count + 1)], refs[-1 - (len(refs) > count + 1) :]
-    total = ins[0][...].astype(F32)
-    for ref in ins[1:count]:
-        total = total + ref[...].astype(F32)
-    outs[0][...] = total.astype(BF16)
-    if len(outs) > 1:
-        outs[1][...] = ins[count][...] + ins[count + 1][...]
-
-
-def finish_kernel(count, which, place_ref, *refs):
-    parts = refs[:count]
-    number = len(which)
-    states = refs[count : count + 3 * number]
-    new_ref = refs[count + 3 * number]
-    moments = refs[count + 3 * number + 1 :]
-    total = parts[0][0].astype(F32)
-    for ref in parts[1:]:
-        total = total + ref[0].astype(F32)
-    start = 0
-    for spot, kind in enumerate(which):
-        master, first, second = states[3 * spot : 3 * spot + 3]
-        cols = slice(start, start + master.shape[1])
-        new_w, new_m, new_v = adamw(
-            master[...], total[:, cols], first[...], second[...], STEP_RATES[kind], DECAY_RATES[kind]
-        )
-        new_ref[0, :, cols] = new_w.astype(BF16)
-        moments[2 * spot][...] = new_m
-        moments[2 * spot + 1][...] = new_v
-        start += master.shape[1]
-
-
-def join_kernel(one_ref, two_ref, out_ref):
-    count = one_ref.shape[0]
-    out_ref[:count] = one_ref[...]
-    out_ref[count:] = two_ref[...]
-
-
-def place_kernel(number, spots_ref, blocks_ref, *refs):
-    start = 0
-    for out_ref in refs[-number:]:
-        width = out_ref.shape[1]
-        out_ref[...] = blocks_ref[0, :, start : start + width].astype(F32)
-        start += width
+HBM = pl.BlockSpec(memory_space=pltpu.HBM)
+
+
+class Job:
+    def __init__(self, ins, outs, scratch, plan, then):
+        self.ins, self.outs, self.scratch, self.plan, self.then = ins, outs, scratch, plan, then
+
+
+def run_kernel(jobs, tab_ref, *refs):
+    refs = list(refs)
+    ins = [[refs.pop(0) for _ in job.ins] for job in jobs]
+    outs = [[refs.pop(0) for _ in job.outs] for job in jobs]
+    bufs = [[refs.pop(0) for _ in job.scratch] for job in jobs]
+    sems = refs.pop(0)
+    used = 0
+    plans = [job.plan(tab_ref, *args) for job, *args in zip(jobs, ins, outs, bufs)]
+    ready, late = [], []
+
+    def copies_of(pairs):
+        nonlocal used
+        made = []
+        for source, target in pairs:
+            made.append(pltpu.make_async_copy(source, target, sems.at[used]))
+            made[-1].start()
+            used += 1
+        return made
+
+    for straight, steps in plans:
+        late += copies_of(straight)
+        ready.append([copies_of(needs) for needs, _ in steps])
+    for (_, steps), waits in zip(plans, ready):
+        for (_, work), copies in zip(steps, waits):
+            wait_all(copies)
+            late += copies_of(work())
+    wait_all(late)
+
+
+def add_job(parts, count, then):
+    _, rows, cols = parts[0].shape
+    number = len(parts)
+    chunks = min(count, 2)
+    size = count // chunks
+
+    def plan(tab_ref, ins, outs, bufs):
+        def step(chunk):
+            at = pl.ds(chunk * size, size)
+
+            def work():
+                def one(k, _):
+                    total = bufs[0][k].astype(F32)
+                    for buf in bufs[1:number]:
+                        total = total + buf[k].astype(F32)
+                    bufs[number][k] = total.astype(BF16)
+                    return 0
+
+                lax.fori_loop(chunk * size, (chunk + 1) * size, one, 0)
+                return [(bufs[number].at[at], outs[0].at[at])]
+
+            return [(ref.at[pl.ds(count + chunk * size, size)], buf.at[at]) for ref, buf in zip(ins, bufs)], work
+
+        return [], [step(chunk) for chunk in range(chunks)]
+
+    return Job(
+        parts,
+        [((count, rows, cols), BF16)],
+        [pltpu.VMEM((count, rows, cols), BF16)] * (number + 1),
+        plan,
+        then,
+    )
+
+
+def plus_job(one, two, then):
+    def plan(tab_ref, ins, outs, bufs):
+        def work():
+            bufs[2][...] = bufs[0][...] + bufs[1][...]
+            return [(bufs[2], outs[0])]
+
+        return [], [(list(zip(ins, bufs)), work)]
+
+    return Job([one, two], [(one.shape, F32)], [pltpu.VMEM(one.shape, F32)] * 3, plan, then)
+
+
+def join_job(one, two, then):
+    count = one.shape[0]
+
+    def plan(tab_ref, ins, outs, bufs):
+        return [
+            (ins[0], outs[0].at[pl.ds(0, count)]),
+            (ins[1], outs[0].at[pl.ds(count, count)]),
+        ], []
+
+    return Job([one, two], [((2 * count,) + one.shape[1:], BF16)], [], plan, then)
+
+
+def finish_job(parts, which, masters, moments, then):
+    _, rows, cols = parts[0].shape
+    number = len(parts)
+    widths = [value.shape[1] for value in masters]
+    states = [value for pair in moments for value in pair]
+
+    def plan(tab_ref, ins, outs, bufs):
+        own = pl.ds(pl.multiple_of(tab_ref[3] * rows, 8), rows)
+        needs = [(ref.at[0], buf) for ref, buf in zip(ins[:number], bufs)]
+        kinds = len(which)
+        for spot in range(kinds):
+            needs.append((ins[number + spot].at[own], bufs[number + spot]))
+        for spot in range(2 * kinds):
+            needs.append((ins[number + kinds + spot], bufs[number + kinds + spot]))
+        new = bufs[number + 3 * kinds]
+
+        def work():
+            start, copies = 0, []
+            for spot, kind in enumerate(which):
+                width = widths[spot]
+                for low in range(start, start + width, D):
+                    cols = slice(low, low + D)
+                    here = slice(low - start, low - start + D)
+                    total = bufs[0][:, cols].astype(F32)
+                    for buf in bufs[1:number]:
+                        total = total + buf[:, cols].astype(F32)
+                    first, second = bufs[number + kinds + 2 * spot : number + kinds + 2 * spot + 2]
+                    new_w, new_m, new_v = adamw(
+                        bufs[number + spot][:, here],
+                        total,
+                        first[:, here],
+                        second[:, here],
+                        STEP_RATES[kind],
+                        DECAY_RATES[kind],
+                    )
+                    new[:, cols] = new_w.astype(BF16)
+                    first[:, here] = new_m
+                    second[:, here] = new_v
+                copies += [(first, outs[1 + 2 * spot]), (second, outs[2 + 2 * spot])]
+                start += width
+            return [(new, outs[0].at[0])] + copies
+
+        return [], [(needs, work)]
+
+    return Job(
+        list(parts) + list(masters) + states,
+        [((1, rows, cols), BF16)] + [(value.shape, F32) for value in states],
+        [pltpu.VMEM((rows, cols), BF16)] * number
+        + [pltpu.VMEM((rows, width), F32) for width in widths]
+        + [pltpu.VMEM(value.shape, F32) for value in states]
+        + [pltpu.VMEM((rows, cols), BF16)],
+        plan,
+        then,
+    )
+
+
+def place_job(one, two, base, widths, then):
+    count, rows, cols = one.shape
+    nb = 2 * count
+
+    def plan(tab_ref, ins, outs, bufs):
+        def step(part):
+            spots = range(part * count, part * count + count)
+
+            def work():
+                def one(spot, _):
+                    start = 0
+                    for number, width in enumerate(widths):
+                        bufs[1 + number][spot] = bufs[0][spot, :, start : start + width].astype(F32)
+                        start += width
+                    return 0
+
+                lax.fori_loop(part * count, part * count + count, one, 0)
+                copies = []
+                for spot in spots:
+                    at = pl.ds(pl.multiple_of(tab_ref[base + spot] * rows, 8), rows)
+                    for number in range(len(widths)):
+                        copies.append((bufs[1 + number].at[spot], outs[number].at[at]))
+                return copies
+
+            return [(ins[part], bufs[0].at[pl.ds(part * count, count)])], work
+
+        return [], [step(part) for part in range(2)]
+
+    return Job(
+        [one, two],
+        [((nb * rows, width), F32) for width in widths],
+        [pltpu.VMEM((nb, rows, cols), BF16)]
+        + [pltpu.VMEM((nb, rows, width), F32) for width in widths],
+        plan,
+        then,
+    )
 
 
 def later(value, dep):
@@ -603,8 +763,8 @@
 
 
 class Sum:
-    def __init__(self, plan, call, keep, send):
-        self.plan, self.call = plan, call
+    def __init__(self, plan, keep, send):
+        self.plan = plan
         self.parts, self.count, self.place = [keep], keep.shape[0], 0
         self.move(send)
 
@@ -613,86 +773,23 @@
         self.parts.append(got)
         self.place += 1
 
-    def add(self, vec=None):
+    def add(self):
         self.count //= 2
-        count = self.count
-        _, rows, cols = self.parts[0].shape
-        block = max(1, count // 4)
-        base = count // block
-        spec = pl.BlockSpec((block, rows, cols), lambda i, *_: (base + i, 0, 0))
-        ins = [(part, spec) for part in self.parts]
-        outs = [
-            (pl.BlockSpec((block, rows, cols), lambda i, *_: (i, 0, 0)), (count, rows, cols), BF16)
-        ]
-        if vec is not None:
-            ins += [(value, full(value.shape)) for value in vec]
-            outs.append((full(vec[0].shape), vec[0].shape, F32))
-        size = count * rows * cols
-        got = self.call(
-            functools.partial(add_kernel, len(self.parts)),
-            (count // block,),
-            [],
-            ins,
-            outs,
-            [],
-            spent(1.5),
-            "add",
-        )
-        self.move(got[0])
-        return got[1] if vec is not None else None
+        return add_job(list(self.parts), self.count, self.move)
 
 
 class Spread:
-    def __init__(self, plan, call, block):
-        self.plan, self.call, self.blocks, self.place = plan, call, block, 0
-        self.move()
-
-    def move(self):
-        self.got = self.plan.exchange(self.blocks, *(order[self.place] for order in self.plan.gather))
+    def __init__(self, plan, block):
+        self.plan, self.blocks, self.place, self.age = plan, block, 0, 0
+        self.move(block)
+
+    def move(self, blocks):
+        self.blocks = blocks
+        self.got = self.plan.exchange(blocks, *(order[self.place] for order in self.plan.gather))
         self.place += 1
 
     def join(self):
-        shape = self.blocks.shape
-        self.blocks = self.call(
-            join_kernel,
-            (1,),
-            [],
-            [(self.blocks, full(shape)), (self.got, full(shape))],
-            [(full((2 * shape[0],) + shape[1:]), (2 * shape[0],) + shape[1:], BF16)],
-            [],
-            spent(0.3),
-            "join",
-        )[0]
-        self.move()
-
-    def put(self, spots, widths, before=None):
-        blocks = self.blocks if before is None else self.got
-        count, rows, cols = blocks.shape
-        base = 0 if before is None else count
-        nb = self.plan.nb
-        ins = [(blocks, pl.BlockSpec((1, rows, cols), lambda i, *_: (i, 0, 0)))]
-        aliases = None
-        if before is not None:
-            ins += [(value, ANYWHERE) for value in before]
-            aliases = {1 + k: k for k in range(len(widths))}
-        return self.call(
-            functools.partial(place_kernel, len(widths)),
-            (count,),
-            [spots],
-            ins,
-            [
-                (
-                    pl.BlockSpec((rows, width), lambda i, spots_ref: (spots_ref[base + i], 0)),
-                    (nb * rows, width),
-                    F32,
-                )
-                for width in widths
-            ],
-            [],
-            spent(0.1),
-            "place",
-            aliases=aliases,
-        )
+        return join_job(self.blocks, self.got, self.move)
 
 
 def shards(
@@ -722,11 +819,27 @@
     nf, nb, nd = plan.nf, plan.nb, plan.nd
     fi = lax.axis_index("fsdp").astype(jnp.int32)
     bi = lax.axis_index("batch").astype(jnp.int32)
-    halves = jnp.stack([bi & 1, (bi >> 1) & 1])
-    place = jnp.stack([fi, halves[fi & 1], halves[1 - (fi & 1)], bi])
-    owners = plan.owners(fi, bi)
-    spots = plan.gathered(fi, bi)
+    tab = lax.dynamic_index_in_dim(jnp.asarray(plan.table()), bi * nf + fi, 0, keepdims=False)
+    place = owners = tab
     call = Chain()
+
+    def run(micros, *jobs):
+        jobs = [job for job in jobs if job is not None]
+        if not jobs:
+            return
+        got = call(
+            functools.partial(run_kernel, jobs),
+            (),
+            [tab],
+            [(value, HBM) for job in jobs for value in job.ins],
+            [(HBM, dims, kind) for job in jobs for dims, kind in job.outs],
+            [buf for job in jobs for buf in job.scratch] + [pltpu.SemaphoreType.DMA((256,))],
+            spent(micros),
+            "turn",
+        )
+        for job in jobs:
+            job.then(*got[: len(job.outs)])
+            got = got[len(job.outs) :]
 
     def pair_spec(rows, cols):
         return pl.BlockSpec((1, rows, cols), lambda i, *_: (i, 0, 0))
@@ -805,7 +918,7 @@
 
     set_b = cast([w_out, w_fc1])
     near_a = set_a[2]
-    set_a = last_piece(spread_pieces(set_a))
+    set_a = last_piece(spread_pieces(set_a, set_b[0]))
     set_c = cast([w_fc2], [near_a])
 
     n1, qkv = call(
@@ -872,9 +985,9 @@
     def grad_sum(outs):
         if len(outs) == 1:
             rows, cols = outs[0].shape
-            blocks = jnp.take(outs[0].reshape(nd, rows // nd, cols), owners, axis=0)
+            blocks = jnp.take(outs[0].reshape(nd, rows // nd, cols), tab[OWN : OWN + nd], axis=0)
             outs = [blocks[: nd // 2], blocks[nd // 2 :]]
-        return Sum(plan, call, *outs)
+        return Sum(plan, *outs)
 
     set_c = spread_pieces(set_c, n2)
 
@@ -908,7 +1021,7 @@
         spent(7),
         "df",
     )
-    sum_2.add()
+    run(3, sum_2.add())
 
     some = 2 if pairs % 2 == 0 else 1
     some_spec = pl.BlockSpec((some, slots, D), lambda i, *_: (i, 0, 0))
@@ -953,7 +1066,7 @@
         "gw1o",
     )
     sum_1 = grad_sum(got)
-    sum_2.add()
+    run(2, sum_2.add())
 
     part_pairs = pairs // 2 if pairs % 2 == 0 else pairs
     back = None
@@ -981,8 +1094,7 @@
             aliases=None if back is None else {2: 0, 3: 1},
         )
         if number == 0:
-            sum_1.add()
-        sum_2.add()
+            run(3, sum_1.add(), sum_2.add())
     dq, dkv, attn_sum = back
 
     got = call(
@@ -1003,68 +1115,57 @@
         "gqkv",
     )
     sum_3 = grad_sum(got)
-    while sum_2.count > 1:
-        sum_2.add()
-    sum_1.add()
+    run(8, sum_1.add(), sum_2.add())
+    run(3, sum_3.add())
 
     fallback = (D // nd) % 8 != 0 or (FF // nd) % 8 != 0
-
-    def finish(total, which, masters, moments):
+    places = OWN + nd
+    moved, states = {}, {}
+
+    def finish(name, total, which, masters, moments):
+        def then(block, *new_states):
+            moved[name] = Spread(plan, block)
+            states[name] = new_states
+
+        if not fallback:
+            return finish_job(total.parts, which, masters, moments, then)
         _, rows, cols = total.parts[0].shape
-        if fallback:
-            grad = sum(part[0].astype(F32) for part in total.parts)
-            start, news, states = 0, [], []
-            for kind, master, (first, second) in zip(which, masters, moments):
-                width = master.shape[1]
-                own = lax.dynamic_slice_in_dim(master, bi * rows, rows, 0)
-                new_w, new_m, new_v = adamw(
-                    own,
-                    grad[:, start : start + width],
-                    first,
-                    second,
-                    STEP_RATES[kind],
-                    DECAY_RATES[kind],
-                )
-                news.append(new_w.astype(BF16))
-                states += [new_m, new_v]
-                start += width
-            block = jnp.concatenate(news, axis=1)[None]
-        else:
-            own = pl.BlockSpec((1, rows, cols), lambda i, *_: (0, 0, 0))
-            ins = [(part, own) for part in total.parts]
-            outs = [(full((1, rows, cols)), (1, rows, cols), BF16)]
-            for master, pair in zip(masters, moments):
-                width = master.shape[1]
-                ins.append((master, pl.BlockSpec((rows, width), lambda i, place_ref: (place_ref[3], 0))))
-                ins += [(value, full(value.shape)) for value in pair]
-                outs += [(full((rows, width)), (rows, width), F32)] * 2
-            block, *states = call(
-                functools.partial(finish_kernel, len(total.parts), which),
-                (1,),
-                [place],
-                ins,
-                outs,
-                [],
-                spent(2),
-                "finish",
+        grad = sum(part[0].astype(F32) for part in total.parts)
+        start, news, made = 0, [], []
+        for kind, master, (first, second) in zip(which, masters, moments):
+            width = master.shape[1]
+            own = lax.dynamic_slice_in_dim(master, bi * rows, rows, 0)
+            new_w, new_m, new_v = adamw(
+                own,
+                grad[:, start : start + width],
+                first,
+                second,
+                STEP_RATES[kind],
+                DECAY_RATES[kind],
             )
-        return Spread(plan, call, block), states
-
-    def put(moved, widths, before=None):
+            news.append(new_w.astype(BF16))
+            made += [new_m, new_v]
+            start += width
+        then(jnp.concatenate(news, axis=1)[None], *made)
+        return None
+
+    news = {}
+
+    def put(name, widths):
+        blocks, got = moved[name].blocks, moved[name].got
+
+        def then(*outs):
+            news[name] = outs
+
         if not fallback:
-            return moved.put(spots, widths, before)
-        if before is None:
-            return moved.blocks
-        blocks = jnp.concatenate([before, moved.got], axis=0)
+            return place_job(blocks, got, places, widths, then)
+        blocks = jnp.concatenate([blocks, got], axis=0)
         count, rows, cols = blocks.shape
-        order = jnp.zeros(count, jnp.int32).at[spots].set(jnp.arange(count, dtype=jnp.int32))
+        order = jnp.zeros(count, jnp.int32).at[tab[places:]].set(jnp.arange(count, dtype=jnp.int32))
         blocks = jnp.take(blocks, order, axis=0).reshape(count * rows, cols).astype(F32)
         cuts = np.cumsum([0] + list(widths))
-        return [blocks[:, a:b] for a, b in zip(cuts[:-1], cuts[1:])]
-
-    last = plan.bbits
-    moved_2, (new_m2, new_v2) = finish(sum_2, (3,), (w_fc2,), ((m_fc2, v_fc2),))
-    sum_3.add()
+        then(*[blocks[:, a:b] for a, b in zip(cuts[:-1], cuts[1:])])
+        return None
 
     grad_tokens, vec_sum = call(
         functools.partial(grad_in_kernel, rows_d),
@@ -1097,18 +1198,35 @@
     vec_got = plan.exchange(vec_sum, vec_gens[0])
     vec_place = 1
 
-    def vec_step(total):
-        nonlocal vec_sum, vec_got, vec_place
-        if vec_place > len(vec_gens):
-            total.add()
-            return
-        vec_sum = total.add((vec_sum, vec_got))
-        vec_got = plan.exchange(vec_sum, vec_gens[vec_place]) if vec_place < len(vec_gens) else None
-        vec_place += 1
-
-    moved_2.join()
-    sum_1.add()
-    vec_step(sum_3)
+    def vec_step():
+        if vec_place >= len(vec_gens):
+            return None
+
+        def then(total):
+            nonlocal vec_sum, vec_got, vec_place
+            vec_sum = total
+            vec_got = plan.exchange(total, vec_gens[vec_place])
+            vec_place += 1
+
+        return plus_job(vec_sum, vec_got, then)
+
+    def step_of(name, total, *rest):
+        if total.count > 1:
+            return total.add()
+        if name not in moved:
+            return finish(name, total, *rest)
+        if moved[name].place < plan.bbits:
+            return moved[name].join()
+        return None
+
+    args_2 = ("2", sum_2, (3,), (w_fc2,), ((m_fc2, v_fc2),))
+    args_1 = ("1", sum_1, (2, 1), (w_fc1, w_out), ((m_fc1, v_fc1), (m_out, v_out)))
+    args_3 = ("3", sum_3, (0,), (w_qkv,), ((m_qkv, v_qkv),))
+
+    def is_done(name):
+        return name in moved and moved[name].place >= plan.bbits
+
+    run(4, step_of(*args_3), step_of(*args_1), step_of(*args_2))
 
     (layer_out,) = call(
         functools.partial(out_kernel, rows_f),
@@ -1127,45 +1245,46 @@
         "out",
     )
 
-    while sum_1.count > 1:
-        sum_1.add()
-    vec_step(sum_3)
-    while moved_2.place < last:
-        moved_2.join()
-    put_2 = put(moved_2, (D,))
-    while sum_3.count > 1:
-        vec_step(sum_3)
-    moved_1, (new_m1, new_v1, new_mo, new_vo) = finish(
-        sum_1, (2, 1), (w_fc1, w_out), ((m_fc1, v_fc1), (m_out, v_out))
-    )
-    moved_3, (new_mq, new_vq) = finish(sum_3, (0,), (w_qkv,), ((m_qkv, v_qkv),))
-    (new_2,) = put(moved_2, (D,), put_2)
-    while moved_3.place < last:
-        moved_1.join()
-        moved_3.join()
-    put_1 = put(moved_1, (FF, D))
-    put_3 = put(moved_3, (3 * D,))
-    new_1, new_o = put(moved_1, (FF, D), put_1)
-    (new_q,) = put(moved_3, (3 * D,), put_3)
+    placed = set()
+    widths = {"2": (D,), "1": (FF, D), "3": (3 * D,)}
+    while not is_done("3"):
+        puts = []
+        for name in ("2", "1"):
+            if is_done(name) and name not in placed and moved[name].age > 0:
+                placed.add(name)
+                puts.append(put(name, widths[name]))
+        for one in moved.values():
+            one.age += one.place >= plan.bbits
+        run(2, step_of(*args_3), step_of(*args_1), step_of(*args_2), vec_step(), *puts)
+    for name in ("2", "1"):
+        if name not in placed:
+            while not is_done(name):
+                run(1, step_of(*{"2": args_2, "1": args_1}[name]))
+            run(0.2, put(name, widths[name]))
+    run(1, put("3", widths["3"]))
 
     while vec_place <= len(vec_gens):
         vec_sum = vec_sum + vec_got
         vec_got = plan.exchange(vec_sum, vec_gens[vec_place]) if vec_place < len(vec_gens) else None
         vec_place += 1
-    states = jnp.concatenate([m_vec, v_vec], axis=0)[None]
+    held = jnp.concatenate([m_vec, v_vec], axis=0)[None]
     for rank in range(plan.bbits):
-        got = plan.exchange(states, *(order[rank] for order in plan.gather))
-        states = jnp.concatenate([states, got], axis=0)
-    order = jnp.zeros(nb, jnp.int32).at[spots].set(jnp.arange(nb, dtype=jnp.int32))
+        got = plan.exchange(held, *(order[rank] for order in plan.gather))
+        held = jnp.concatenate([held, got], axis=0)
+    order = jnp.zeros(nb, jnp.int32).at[tab[places:]].set(jnp.arange(nb, dtype=jnp.int32))
     own_cols = D // nd
-    states = jnp.transpose(jnp.take(states, order, axis=0), (1, 0, 2)).reshape(2 * NVEC, nb * own_cols)
+    held = jnp.transpose(jnp.take(held, order, axis=0), (1, 0, 2)).reshape(2 * NVEC, nb * own_cols)
     grad_vec = lax.dynamic_slice_in_dim(vec_sum[:NVEC], fi * nb * own_cols, nb * own_cols, 1)
     vec_new, all_m, all_v = adamw(
-        vectors, grad_vec, states[:NVEC], states[NVEC:], STEP_RATES[4], DECAY_RATES[4]
+        vectors, grad_vec, held[:NVEC], held[NVEC:], STEP_RATES[4], DECAY_RATES[4]
     )
     new_mv = lax.dynamic_slice_in_dim(all_m, bi * own_cols, own_cols, 1)
     new_vv = lax.dynamic_slice_in_dim(all_v, bi * own_cols, own_cols, 1)
 
+    (new_2,), (new_1, new_o), (new_q,) = news["2"], news["1"], news["3"]
+    new_m2, new_v2 = states["2"]
+    new_m1, new_v1, new_mo, new_vo = states["1"]
+    new_mq, new_vq = states["3"]
     return (
         layer_out,
         grad_tokens,

time: 336 us -> 416 us (1.24)
  Pallas kernels: 236 us -> 313 us
  waiting for transfers between devices: 20.8 us -> 26.5 us
  starting transfers between devices: 44.9 us -> 49.2 us
    pallas_call x43 -> x29, Pallas kernels: 236 us -> 313 us  [__call__(): pl.pallas_call(body, grid_spec=pltpu.PrefetchScalarGridSpec(num_scalar_pr...]
    ppermute x50, waiting for transfers between devices: 20.8 us -> 26.5 us  [exchange(): return lax.ppermute(value, ('batch', 'fsdp'), pairs)]
    ppermute x50, starting transfers between devices: 44.9 us -> 49.2 us  [exchange(): return lax.ppermute(value, ('batch', 'fsdp'), pairs)]
    unnamed x92 -> x82, local copies, waits for them, and re-layouts: 22 us -> 18.1 us
  transfers between devices with their start and end apart: 50 -> 50, of which waited for: 9 -> 16; matrix products, arithmetic and copies ran while one was open for 2% -> 1% of each run, Pallas kernels for 69% -> 60%
where the time goes in v3:
time: 416 us; the launch traced here: 415 us
  Pallas kernels  313 us (75%)
  starting transfers between devices  49.2 us (12%)
  waiting for transfers between devices  26.5 us (6%)
  local copies, waits for them, and re-layouts  21.5 us (5%)
    pallas_call x29, Pallas kernels, __call__(): pl.pallas_call(body, grid_spec=pltpu.PrefetchScalarGridSpec(num_scalar_pr...  313 us
    ppermute x50, starting transfers between devices, exchange(): return lax.ppermute(value, ('batch', 'fsdp'), pairs)  49.2 us
    ppermute x50, waiting for transfers between devices, exchange(): return lax.ppermute(value, ('batch', 'fsdp'), pairs)  26.5 us
    unnamed x82, local copies, waits for them, and re-layouts  18.1 us
  transfers between devices with their start and end apart: 50, of which 16 were waited for; matrix products, arithmetic and copies ran while one was open for 1% of the time, Pallas kernels for 60%

profile of v3, /device:TPU:0, one launch (start us, length us, event | category | flops | bytes accessed | tf_op | source)
XLA Modules:
  0.0 414.6 jit_solution(1267028158712308046)
XLA Ops:
  7.9 6.0 %order.1 = (bf16[4,256,256]{2,1,0:T(8,128)(2,1)}, bf16[4,256,768]{2,1,0:T(8,128)(2,1)}, f32[4,256,128]{2,1,0:T(8,128)}, bf16[4,128,768]{2,1,0:T(8,128)(2,1)}) custom-call(s32[4]{0:T(128)} %refs_0_.1, s32[4,1,128]{2,1,0:T(1,128)} %bitcast.15, bf16[4,256,768]{2,1,0:T(8,128)(2,1)} %refs_2_.2, bf16[4,256,768]{2,1,0:T(8,128)(2,1)} %refs_3_.1, ...), custom_call_target="tpu_custom_call" | custom-call | flops 17999998976 | bytes 60000000 | tf_op jit(solution)/shard_map/order/pallas_call | solution.py:745
  13.9 3.8 cast.4
  26.6 3.4 cast.5
  31.0 10.6 %qkv.1 = (bf16[4,256,768]{2,1,0:T(8,128)(2,1)}, bf16[4,256,2304]{2,1,0:T(8,128)(2,1)}) custom-call(s32[44]{0:T(128)} %get-tuple-element.175.refs_0_, bf16[4,256,768]{2,1,0:T(8,128)(2,1)} %get-tuple-element.92.refs_1_, f32[4,256,128]{2,1,0:T(8,128)} %get-tuple-element.93.refs_2_, f32[16,768]{1,0:T(8,128)} %fusion.7.refs_3_.refs_4_, ...), custom_call_target="tpu_custom_call" | custom-call | flops 3000000000 | bytes 10000000 | tf_op jit(solution)/shard_map/qkv/pallas_call | solution.py:745
  44.1 15.7 %mix.1.refs_3_.refs_11_ = bf16[4,256,768]{2,1,0:T(8,128)(2,1)} custom-call(bf16[4,256,2304]{2,1,0:T(8,128)(2,1)} %get-tuple-element.100.refs_0_.refs_2_, bf16[96,3840]{1,0:T(8,128)(2,1)} %copy-done, bf16[4,256,2304]{2,1,0:T(8,128)(2,1)} %get-tuple-element.100.refs_0_.refs_2_), custom_call_target="tpu_custom_call" | custom-call | flops 3000000000 | bytes 10000000 | tf_op jit(solution)/shard_map/mix/pallas_call | solution.py:745
  62.3 17.9 %fc1.1 = (f32[4,256,768]{2,1,0:T(8,128)}, bf16[4,256,768]{2,1,0:T(8,128)(2,1)}, bf16[4,256,3072]{2,1,0:T(8,128)(2,1)}, bf16[4,128,3072]{2,1,0:T(8,128)(2,1)}) custom-call(s32[44]{0:T(128)} %get-tuple-element.175.refs_0_, bf16[4,256,768]{2,1,0:T(8,128)(2,1)} %get-tuple-element.92.refs_1_, f32[4,256,128]{2,1,0:T(8,128)} %get-tuple-element.93.refs_2_, ...), custom_call_target="tpu_custom_call" | custom-call | flops 54000001024 | bytes 180000000 | tf_op jit(solution)/shard_map/fc1/pallas_call | solution.py:745
  81.8 8.7 %gw2.1 = (bf16[16,96,768]{2,1,0:T(8,128)(2,1)}, bf16[16,96,768]{2,1,0:T(8,128)(2,1)}, f32[1,768]{1,0:T(1,128)}) custom-call(s32[44]{0:T(128)} %get-tuple-element.175.refs_0_, bf16[4,256,3072]{2,1,0:T(8,128)(2,1)} %get-tuple-element.104.refs_1_, bf16[4,128,768]{2,1,0:T(8,128)(2,1)} %get-tuple-element.95.refs_3_.refs_2_.refs_1_, ...), custom_call_target="tpu_custom_call" | custom-call | flops 24000000000 | bytes 80000000 | tf_op jit(solution)/shard_map/gw2/pallas_call | solution.py:745
  93.0 9.5 %df.1 = (bf16[512,3072]{1,0:T(8,128)(2,1)}, f32[1,3072]{1,0:T(1,128)}) custom-call(s32[44]{0:T(128)} %get-tuple-element.175.refs_0_, bf16[4,128,768]{2,1,0:T(8,128)(2,1)} %get-tuple-element.95.refs_3_.refs_2_.refs_1_, bf16[4,128,3072]{2,1,0:T(8,128)(2,1)} %get-tuple-element.110.refs_3_.refs_2_, bf16[768,768]{1,0:T(8,128)(2,1)} %get-tuple-element.107.refs_3_.refs_5_, ...), custom_call_target="tpu_custom_call" | custom-call | flops 20999999488 | bytes 70000000 | tf_op jit(solution)/shard_map/df/pallas_call | solution.py:745
  103.9 5.5 %turn.13.refs_11_ = bf16[8,96,768]{2,1,0:T(8,128)(2,1)} custom-call(s32[44]{0:T(128)} %get-tuple-element.175.refs_0_, bf16[16,96,768]{2,1,0:T(8,128)(2,1)} %get-tuple-element.114.refs_1_.refs_3_.refs_4_.refs_8_, bf16[16,96,768]{2,1,0:T(8,128)(2,1)} %copy-done.9, f32[1,3072]{1,0:T(1,128)} %get-tuple-element.116.refs_3_.refs_10_), custom_call_target="tpu_custom_call" | custom-call | flops 8999999488 | bytes 30000000 | tf_op jit(solution)/shard_map/turn/pallas_call | solution.py:745
  111.0 11.5 %mlp_back.1 = (f32[4,128,768]{2,1,0:T(8,128)}, bf16[4,128,768]{2,1,0:T(8,128)(2,1)}, bf16[4,128,768]{2,1,0:T(8,128)(2,1)}, f32[8,768]{1,0:T(8,128)}) custom-call(s32[44]{0:T(128)} %get-tuple-element.175.refs_0_, bf16[512,3072]{1,0:T(8,128)(2,1)} %get-tuple-element.113.refs_1_.refs_2_, bf16[4,128,768]{2,1,0:T(8,128)(2,1)} %get-tuple-element.95.refs_3_.refs_2_.refs_1_, ...), custom_call_target="tpu_custom_call" | custom-call | flops 30000001024 | bytes 100000000 | tf_op jit(solution)/shard_map/mlp_back/pallas_call | solution.py:745
  122.4 9.7 %gw1o.1 = (bf16[16,24,3840]{2,1,0:T(8,128)(2,1)}, bf16[16,24,3840]{2,1,0:T(8,128)(2,1)}) custom-call(s32[44]{0:T(128)} %get-tuple-element.175.refs_0_, bf16[4,256,768]{2,1,0:T(8,128)(2,1)} %get-tuple-element.108.refs_1_, bf16[512,3072]{1,0:T(8,128)(2,1)} %get-tuple-element.113.refs_1_.refs_2_, bf16[4,256,768]{2,1,0:T(8,128)(2,1)} %mix.1.refs_3_.refs_11_, ...), custom_call_target="tpu_custom_call" | custom-call | flops 27000000512 | bytes 90000000 | tf_op jit(solution)/shard_map/gw1o/pallas_call | solution.py:745
  132.1 5.2 %turn.14.refs_2_ = bf16[4,96,768]{2,1,0:T(8,128)(2,1)} custom-call(s32[44]{0:T(128)} %get-tuple-element.175.refs_0_, bf16[16,96,768]{2,1,0:T(8,128)(2,1)} %get-tuple-element.114.refs_1_.refs_3_.refs_4_.refs_8_, bf16[16,96,768]{2,1,0:T(8,128)(2,1)} %copy-done.9, bf16[8,96,768]{2,1,0:T(8,128)(2,1)} %collective-permute-done.19.refs_3_.refs_5_.refs_6_.refs_10_, ...), custom_call_target="tpu_custom_call" | custom-call | flops 6000000000 | bytes 20000000 | tf_op jit(solution)/shard_map/turn/pallas_call | solution.py:745
  138.8 15.2 %attn_back.2 = (bf16[4,128,768]{2,1,0:T(8,128)(2,1)}, bf16[4,256,1536]{2,1,0:T(8,128)(2,1)}, f32[8,768]{1,0:T(8,128)}) custom-call(bf16[4,256,2304]{2,1,0:T(8,128)(2,1)} %get-tuple-element.100.refs_0_.refs_2_, bf16[4,128,768]{2,1,0:T(8,128)(2,1)} %get-tuple-element.117.refs_1_, bf16[4,96,768]{2,1,0:T(8,128)(2,1)} %turn.14.refs_2_), custom_call_target="tpu_custom_call" | custom-call | flops 35999997952 | bytes 120000000 | tf_op jit(solution)/shard_map/attn_back/pallas_call | solution.py:745
  155.9 5.9 %turn.15 = (bf16[8,24,3840]{2,1,0:T(8,128)(2,1)}, bf16[2,96,768]{2,1,0:T(8,128)(2,1)}) custom-call(s32[44]{0:T(128)} %get-tuple-element.175.refs_0_, bf16[16,24,3840]{2,1,0:T(8,128)(2,1)} %get-tuple-element.124.refs_1_.refs_4_.refs_5_.refs_6_, bf16[16,24,3840]{2,1,0:T(8,128)(2,1)} %copy-done.8, ...), custom_call_target="tpu_custom_call" | custom-call | flops 8999999488 | bytes 30000000 | tf_op jit(solution)/shard_map/turn/pallas_call | solution.py:745
  163.7 15.3 %attn_back.3 = (bf16[4,128,768]{2,1,0:T(8,128)(2,1)}, bf16[4,256,1536]{2,1,0:T(8,128)(2,1)}, f32[8,768]{1,0:T(8,128)}) custom-call(bf16[4,256,2304]{2,1,0:T(8,128)(2,1)} %get-tuple-element.100.refs_0_.refs_2_, bf16[4,128,768]{2,1,0:T(8,128)(2,1)} %get-tuple-element.117.refs_1_, ...), custom_call_target="tpu_custom_call", output_to_operand_aliasing={{0}: (2, {}), {1}: (3, {})} | custom-call | flops 35999997952 | bytes 120000000 | tf_op jit(solution)/shard_map/attn_back/pallas_call | solution.py:745
  178.9 9.0 %gqkv.1 = (bf16[16,24,2304]{2,1,0:T(8,128)(2,1)}, bf16[16,24,2304]{2,1,0:T(8,128)(2,1)}) custom-call(s32[44]{0:T(128)} %get-tuple-element.175.refs_0_, bf16[4,256,768]{2,1,0:T(8,128)(2,1)} %get-tuple-element.101.refs_1_, bf16[4,128,768]{2,1,0:T(8,128)(2,1)} %get-tuple-element.126.refs_2_.refs_4_, bf16[4,256,1536]{2,1,0:T(8,128)(2,1)} %get-tuple-element.127.refs_3_.refs_5_, ...), custom_call_target="tpu_custom_call" | custom-call | flops 27000000512 | bytes 90000000 | tf_op jit(solution)/shard_map/gqkv/pallas_call | solution.py:745
  189.9 5.5 %turn.16 = (bf16[4,24,3840]{2,1,0:T(8,128)(2,1)}, bf16[1,96,768]{2,1,0:T(8,128)(2,1)}) custom-call(s32[44]{0:T(128)} %get-tuple-element.175.refs_0_, bf16[16,24,3840]{2,1,0:T(8,128)(2,1)} %get-tuple-element.124.refs_1_.refs_4_.refs_5_.refs_6_, bf16[16,24,3840]{2,1,0:T(8,128)(2,1)} %copy-done.8, bf16[8,24,3840]{2,1,0:T(8,128)(2,1)} %copy-done.12, ...), custom_call_target="tpu_custom_call" | custom-call | flops 24000000000 | bytes 80000000 | tf_op jit(solution)/shard_map/turn/pallas_call | solution.py:745
  196.2 3.2 collective-permute-start.27
  200.8 5.5 %turn.17.refs_18_ = bf16[8,24,2304]{2,1,0:T(8,128)(2,1)} custom-call(s32[44]{0:T(128)} %get-tuple-element.175.refs_0_, bf16[16,24,2304]{2,1,0:T(8,128)(2,1)} %get-tuple-element.129.refs_1_, bf16[16,24,2304]{2,1,0:T(8,128)(2,1)} %copy-done.10, bf16[1,96,768]{2,1,0:T(8,128)(2,1)} %get-tuple-element.132.refs_3_), custom_call_target="tpu_custom_call" | custom-call | flops 8999999488 | bytes 30000000 | tf_op jit(solution)/shard_map/turn/pallas_call | solution.py:745
  207.2 15.1 %grad_in.1 = (f32[4,256,768]{2,1,0:T(8,128)}, f32[16,768]{1,0:T(8,128)}) custom-call(s32[44]{0:T(128)} %get-tuple-element.175.refs_0_, bf16[4,256,768]{2,1,0:T(8,128)(2,1)} %get-tuple-element.92.refs_1_, f32[4,256,128]{2,1,0:T(8,128)} %get-tuple-element.93.refs_2_, f32[16,768]{1,0:T(8,128)} %fusion.7.refs_3_.refs_4_, ...), custom_call_target="tpu_custom_call" | custom-call | flops 44999999488 | bytes 150000000 | tf_op jit(solution)/shard_map/grad_in/pallas_call | solution.py:745
  224.0 6.7 %turn.18 = (bf16[4,24,2304]{2,1,0:T(8,128)(2,1)}, bf16[2,24,3840]{2,1,0:T(8,128)(2,1)}, bf16[1,96,768]{2,1,0:T(8,128)(2,1)}, f32[96,768]{1,0:T(8,128)}, f32[96,768]{1,0:T(8,128)}) custom-call(s32[44]{0:T(128)} %get-tuple-element.175.refs_0_, bf16[16,24,2304]{2,1,0:T(8,128)(2,1)} %get-tuple-element.129.refs_1_, bf16[16,24,2304]{2,1,0:T(8,128)(2,1)} %copy-done.10, ...), custom_call_target="tpu_custom_call" | custom-call | flops 12000000000 | bytes 40000000 | tf_op jit(solution)/shard_map/turn/pallas_call | solution.py:745
  232.9 13.0 %out.1.refs_14_ = bf16[4,256,768]{2,1,0:T(8,128)(2,1)} custom-call(s32[44]{0:T(128)} %get-tuple-element.175.refs_0_, bf16[4,256,3072]{2,1,0:T(8,128)(2,1)} %get-tuple-element.104.refs_1_, f32[4,256,768]{2,1,0:T(8,128)} %get-tuple-element.105.refs_3_.refs_2_, f32[16,768]{1,0:T(8,128)} %fusion.7.refs_3_.refs_4_, ...), custom_call_target="tpu_custom_call" | custom-call | flops 38999998464 | bytes 130000000 | tf_op jit(solution)/shard_map/out/pallas_call | solution.py:745
  247.6 13.0 %turn.19 = (bf16[2,24,2304]{2,1,0:T(8,128)(2,1)}, bf16[1,24,3840]{2,1,0:T(8,128)(2,1)}, bf16[2,96,768]{2,1,0:T(8,128)(2,1)}, f32[16,768]{1,0:T(8,128)}) custom-call(s32[44]{0:T(128)} %get-tuple-element.175.refs_0_, bf16[16,24,2304]{2,1,0:T(8,128)(2,1)} %get-tuple-element.129.refs_1_, bf16[16,24,2304]{2,1,0:T(8,128)(2,1)} %copy-done.10, ...), custom_call_target="tpu_custom_call" | custom-call | flops 6000000000 | bytes 20000000 | tf_op jit(solution)/shard_map/turn/pallas_call | solution.py:745
  270.7 5.0 %collective-permute-done.33.refs_11_ = bf16[1,24,3840]{2,1,0:T(8,128)(2,1)S(1)} collective-permute-done((bf16[1,24,3840]{2,1,0:T(8,128)(2,1)}, bf16[1,24,3840]{2,1,0:T(8,128)(2,1)S(1)}, u32[]{:S(2)}, u32[]{:S(2)}) %collective-permute-start.33) | collective-permute-done | bytes 184352 | tf_op jit(solution)/shard_map/ppermute | solution.py:111
  277.2 22.0 %turn.20 = (bf16[1,24,2304]{2,1,0:T(8,128)(2,1)}, bf16[1,24,3840]{2,1,0:T(8,128)(2,1)}, f32[24,3072]{1,0:T(8,128)}, f32[24,3072]{1,0:T(8,128)}, f32[24,768]{1,0:...) custom-call(s32[44]{0:T(128)} %get-tuple-element.175.refs_0_, ...), custom_call_target="tpu_custom_call" | custom-call | flops 6000000000 | bytes 20000000 | tf_op jit(solution)/shard_map/turn/pallas_call | solution.py:745
  307.4 3.8 collective-permute-done.36.refs_6_
  312.5 15.2 %turn.21 = (bf16[1,24,2304]{2,1,0:T(8,128)(2,1)}, f32[24,2304]{1,0:T(8,128)}, f32[24,2304]{1,0:T(8,128)}, bf16[2,24,3840]{2,1,0:T(8,128)(2,1)}, f32[16,768]{1,0:T(8,128)}) custom-call(s32[44]{0:T(128)} %get-tuple-element.175.refs_0_, bf16[16,24,2304]{2,1,0:T(8,128)(2,1)} %get-tuple-element.129.refs_1_, bf16[16,24,2304]{2,1,0:T(8,128)(2,1)} %copy-done.10, ...), custom_call_target="tpu_custom_call" | custom-call | flops 6000000000 | bytes 20000000 | tf_op jit(solution)/shard_map/turn/pallas_call | solution.py:745
  339.2 33.1 %turn.22 = (bf16[2,24,2304]{2,1,0:T(8,128)(2,1)}, bf16[4,24,3840]{2,1,0:T(8,128)(2,1)}, f32[16,768]{1,0:T(8,128)}, f32[768,768]{1,0:T(8,128)}) custom-call(s32[44]{0:T(128)} %get-tuple-element.175.refs_0_, bf16[1,24,2304]{2,1,0:T(8,128)(2,1)} %get-tuple-element.148.refs_1_, bf16[1,24,2304]{2,1,0:T(8,128)(2,1)} %copy-done.34, ...), custom_call_target="tpu_custom_call" | custom-call | flops 6000000000 | bytes 20000000 | tf_op jit(solution)/shard_map/turn/pallas_call | solution.py:745
  376.4 3.6 collective-permute-done.43.refs_2_
  380.7 17.6 %turn.23.refs_3_.refs_1_ = bf16[4,24,2304]{2,1,0:T(8,128)(2,1)} custom-call(s32[44]{0:T(128)} %get-tuple-element.175.refs_0_, bf16[2,24,2304]{2,1,0:T(8,128)(2,1)} %get-tuple-element.152.refs_1_, bf16[2,24,2304]{2,1,0:T(8,128)(2,1)} %copy-done.29, f32[768,768]{1,0:T(8,128)} %get-tuple-element.85.refs_3_), custom_call_target="tpu_custom_call" | custom-call | flops 6000000000 | bytes 20000000 | tf_op jit(solution)/shard_map/turn/pallas_call | solution.py:745
  402.6 5.7 %turn.24 = (f32[192,3072]{1,0:T(8,128)}, f32[192,768]{1,0:T(8,128)}) custom-call(s32[44]{0:T(128)} %get-tuple-element.175.refs_0_, bf16[4,24,3840]{2,1,0:T(8,128)(2,1)} %get-tuple-element.154.refs_1_, bf16[4,24,3840]{2,1,0:T(8,128)(2,1)} %copy-done.17, bf16[4,24,2304]{2,1,0:T(8,128)(2,1)} %turn.23.refs_3_.refs_1_), custom_call_target="tpu_custom_call" | custom-call | flops 600000000 | bytes 2000000 | tf_op jit(solution)/shard_map/turn/pallas_call | solution.py:745
  409.1 5.2 %turn.25 = f32[192,2304]{1,0:T(8,128)} custom-call(s32[44]{0:T(128)} %get-tuple-element.175.refs_0_, bf16[4,24,2304]{2,1,0:T(8,128)(2,1)} %turn.23.refs_3_.refs_1_, bf16[4,24,2304]{2,1,0:T(8,128)(2,1)} %copy-done.23, f32[192,768]{1,0:T(8,128)} %get-tuple-element.79.refs_3_), custom_call_target="tpu_custom_call" | custom-call | flops 3000000000 | bytes 10000000 | tf_op jit(solution)/shard_map/turn/pallas_call | solution.py:745
  (201 shorter events, 87.1 us)
Async XLA Ops:
  5.0 13.3 %collective-permute-start.4 = (bf16[96,2304]{1,0:T(8,128)(2,1)}, bf16[96,2304]{1,0:T(8,128)(2,1)S(1)}, u32[]{:S(2)}, u32[]{:S(2)}) collective-permute-start(bf16[96,2304]{1,0:T(8,128)(2,1)} %get-tuple-element.91.refs_4_), channel_id=1, source_target_pairs={{0,2},{1,3},{2,0},{3,1},{4,6},{5,7},{6,4},{7,5},{8,10},{9,11},{10,... | collective-permute-start | bytes 1327112 | tf_op jit(solution)/shard_map/ppermute | solution.py:111
  22.8 19.1 %collective-permute-start.8 = (bf16[96,3840]{1,0:T(8,128)(2,1)}, bf16[96,3840]{1,0:T(8,128)(2,1)S(1)}, u32[]{:S(2)}, u32[]{:S(2)}) collective-permute-start(bf16[96,3840]{1,0:T(8,128)(2,1)} %get-tuple-element.98.refs_3_), channel_id=1, source_target_pairs={{0,2},{1,3},{2,0},{3,1},{4,6},{5,7},{6,4},{7,5},{8,10},{9,11},{10,... | collective-permute-start | bytes 2211848 | tf_op jit(solution)/shard_map/ppermute | solution.py:111
  41.9 17.9 %collective-permute-start.10 = (bf16[96,3840]{1,0:T(8,128)(2,1)S(1)}, bf16[96,3840]{1,0:T(8,128)(2,1)}, u32[]{:S(2)}, u32[]{:S(2)}) collective-permute-start(bf16[96,3840]{1,0:T(8,128)(2,1)S(1)} %collective-permute-done.8.refs_1_.refs_7_), channel_id=1, source_target_pairs={{0,4},{1,9},{2,6},{3,11},{4,0},{5,13},{6,2},{7,15},{8,12},{9,1},{1... | collective-permute-start | bytes 2211848 | tf_op jit(solution)/shard_map/ppermute | solution.py:111
  43.5 18.0 %collective-permute-start.9 = (bf16[192,3840]{1,0:T(8,128)(2,1)S(1)}, bf16[192,3840]{1,0:T(8,128)(2,1)}, u32[]{:S(2)}, u32[]{:S(2)}) collective-permute-start(bf16[192,3840]{1,0:T(8,128)(2,1)S(1)} %copy-done.11), channel_id=1, source_target_pairs={{0,1},{1,0},{2,3},{3,2},{4,5},{5,4},{6,7},{7,6},{8,9},{9,8},{10,11... | collective-permute-start | bytes 4423688 | tf_op jit(solution)/shard_map/ppermute | solution.py:111
  43.8 17.7 %collective-permute-start.11 = (bf16[96,3840]{1,0:T(8,128)(2,1)S(1)}, bf16[96,3840]{1,0:T(8,128)(2,1)}, u32[]{:S(2)}, u32[]{:S(2)}) collective-permute-start(bf16[96,3840]{1,0:T(8,128)(2,1)S(1)} %collective-permute-done.8.refs_1_.refs_7_), channel_id=1, source_target_pairs={{0,1},{1,0},{2,3},{3,2},{4,5},{5,4},{6,7},{7,6},{8,9},{9,8},{10,11... | collective-permute-start | bytes 2211848 | tf_op jit(solution)/shard_map/ppermute | solution.py:111
  60.0 20.2 %collective-permute-start.14 = (bf16[384,768]{1,0:T(8,128)(2,1)}, bf16[384,768]{1,0:T(8,128)(2,1)}, u32[]{:S(2)}, u32[]{:S(2)}) collective-permute-start(bf16[384,768]{1,0:T(8,128)(2,1)} %get-tuple-element.99.refs_10_), channel_id=1, source_target_pairs={{0,2},{1,3},{2,0},{3,1},{4,6},{5,7},{6,4},{7,5},{8,10},{9,11},{10,... | collective-permute-start | bytes 1769480 | tf_op jit(solution)/shard_map/ppermute | solution.py:111
  61.5 31.0 %collective-permute-start.13 = (bf16[768,768]{1,0:T(8,128)(2,1)S(1)}, bf16[768,768]{1,0:T(8,128)(2,1)}, u32[]{:S(2)}, u32[]{:S(2)}) collective-permute-start(bf16[768,768]{1,0:T(8,128)(2,1)S(1)} %copy-done.13), channel_id=1, source_target_pairs={{0,1},{1,0},{2,3},{3,2},{4,5},{5,4},{6,7},{7,6},{8,9},{9,8},{10,11... | collective-permute-start | bytes 3538952 | tf_op jit(solution)/shard_map/ppermute | solution.py:111
  80.2 10.3 %collective-permute-start.15 = (bf16[384,768]{1,0:T(8,128)(2,1)}, bf16[384,768]{1,0:T(8,128)(2,1)}, u32[]{:S(2)}, u32[]{:S(2)}) collective-permute-start(bf16[384,768]{1,0:T(8,128)(2,1)} %collective-permute-done.14.refs_5_.refs_7_), channel_id=1, source_target_pairs={{0,4},{1,9},{2,6},{3,11},{4,0},{5,13},{6,2},{7,15},{8,12},{9,1},{1... | collective-permute-start | bytes 1769480 | tf_op jit(solution)/shard_map/ppermute | solution.py:111
  81.8 10.7 %collective-permute-start.16 = (bf16[384,768]{1,0:T(8,128)(2,1)}, bf16[384,768]{1,0:T(8,128)(2,1)}, u32[]{:S(2)}, u32[]{:S(2)}) collective-permute-start(bf16[384,768]{1,0:T(8,128)(2,1)} %collective-permute-done.14.refs_5_.refs_7_), channel_id=1, source_target_pairs={{0,1},{1,0},{2,3},{3,2},{4,5},{5,4},{6,7},{7,6},{8,9},{9,8},{10,11... | collective-permute-start | bytes 1769480 | tf_op jit(solution)/shard_map/ppermute | solution.py:111
  91.0 11.5 %collective-permute-start.18 = (bf16[16,96,768]{2,1,0:T(8,128)(2,1)}, bf16[16,96,768]{2,1,0:T(8,128)(2,1)S(1)}, u32[]{:S(2)}, u32[]{:S(2)}) collective-permute-start(bf16[16,96,768]{2,1,0:T(8,128)(2,1)} %get-tuple-element.115), channel_id=1, source_target_pairs={{0,1},{1,0},{2,3},{3,2},{4,5},{5,4},{6,7},{7,6},{8,9},{9,8},{10,11... | collective-permute-start | bytes 7077896 | tf_op jit(solution)/shard_map/ppermute | solution.py:111
  109.4 22.7 %collective-permute-start.19 = (bf16[8,96,768]{2,1,0:T(8,128)(2,1)}, bf16[8,96,768]{2,1,0:T(8,128)(2,1)}, u32[]{:S(2)}, u32[]{:S(2)}) collective-permute-start(bf16[8,96,768]{2,1,0:T(8,128)(2,1)} %turn.13.refs_11_), channel_id=1, source_target_pairs={{0,2},{1,5},{2,0},{3,7},{4,6},{5,1},{6,4},{7,3},{8,10},{9,13},{10,... | collective-permute-start | bytes 3538952 | tf_op jit(solution)/shard_map/ppermute | solution.py:111
  132.1 22.0 %collective-permute-start.20 = (bf16[16,24,3840]{2,1,0:T(8,128)(2,1)}, bf16[16,24,3840]{2,1,0:T(8,128)(2,1)S(1)}, u32[]{:S(2)}, u32[]{:S(2)}) collective-permute-start(bf16[16,24,3840]{2,1,0:T(8,128)(2,1)} %get-tuple-element.120.refs_4_), channel_id=1, source_target_pairs={{0,1},{1,0},{2,3},{3,2},{4,5},{5,4},{6,7},{7,6},{8,9},{9,8},{10,11... | collective-permute-start | bytes 8847368 | tf_op jit(solution)/shard_map/ppermute | solution.py:111
  137.3 16.8 %collective-permute-start.21 = (bf16[4,96,768]{2,1,0:T(8,128)(2,1)}, bf16[4,96,768]{2,1,0:T(8,128)(2,1)S(1)}, u32[]{:S(2)}, u32[]{:S(2)}) collective-permute-start(bf16[4,96,768]{2,1,0:T(8,128)(2,1)} %turn.14.refs_2_), channel_id=1, source_target_pairs={{0,8},{1,3},{2,10},{3,1},{4,12},{5,7},{6,14},{7,5},{8,0},{9,11},{1... | collective-permute-start | bytes 1769480 | tf_op jit(solution)/shard_map/ppermute | solution.py:111
  161.7 26.2 %collective-permute-start.23 = (bf16[8,24,3840]{2,1,0:T(8,128)(2,1)}, bf16[8,24,3840]{2,1,0:T(8,128)(2,1)S(1)}, u32[]{:S(2)}, u32[]{:S(2)}) collective-permute-start(bf16[8,24,3840]{2,1,0:T(8,128)(2,1)} %get-tuple-element.131), channel_id=1, source_target_pairs={{0,2},{1,5},{2,0},{3,7},{4,6},{5,1},{6,4},{7,3},{8,10},{9,13},{10,... | collective-permute-start | bytes 4423688 | tf_op jit(solution)/shard_map/ppermute | solution.py:111
  162.6 25.3 %collective-permute-start.24 = (bf16[2,96,768]{2,1,0:T(8,128)(2,1)}, bf16[2,96,768]{2,1,0:T(8,128)(2,1)S(1)}, u32[]{:S(2)}, u32[]{:S(2)}) collective-permute-start(bf16[2,96,768]{2,1,0:T(8,128)(2,1)} %get-tuple-element.125.refs_5_), channel_id=1, source_target_pairs={{0,4},{1,9},{2,6},{3,11},{4,0},{5,13},{6,2},{7,15},{8,12},{9,1},{1... | collective-permute-start | bytes 884744 | tf_op jit(solution)/shard_map/ppermute | solution.py:111
  187.9 11.5 %collective-permute-start.22 = (bf16[16,24,2304]{2,1,0:T(8,128)(2,1)}, bf16[16,24,2304]{2,1,0:T(8,128)(2,1)S(1)}, u32[]{:S(2)}, u32[]{:S(2)}) collective-permute-start(bf16[16,24,2304]{2,1,0:T(8,128)(2,1)} %get-tuple-element.130.refs_9_), channel_id=1, source_target_pairs={{0,1},{1,0},{2,3},{3,2},{4,5},{5,4},{6,7},{7,6},{8,9},{9,8},{10,11... | collective-permute-start | bytes 5308424 | tf_op jit(solution)/shard_map/ppermute | solution.py:111
  195.3 27.1 %collective-permute-start.26 = (bf16[4,24,3840]{2,1,0:T(8,128)(2,1)}, bf16[4,24,3840]{2,1,0:T(8,128)(2,1)}, u32[]{:S(2)}, u32[]{:S(2)}) collective-permute-start(bf16[4,24,3840]{2,1,0:T(8,128)(2,1)} %get-tuple-element.133), channel_id=1, source_target_pairs={{0,8},{1,3},{2,10},{3,1},{4,12},{5,7},{6,14},{7,5},{8,0},{9,11},{1... | collective-permute-start | bytes 2211848 | tf_op jit(solution)/shard_map/ppermute | solution.py:111
  196.2 26.2 %collective-permute-start.27 = (bf16[1,96,768]{2,1,0:T(8,128)(2,1)}, bf16[1,96,768]{2,1,0:T(8,128)(2,1)S(1)}, u32[]{:S(2)}, u32[]{:S(2)}) collective-permute-start(bf16[1,96,768]{2,1,0:T(8,128)(2,1)} %get-tuple-element.132.refs_3_), channel_id=1, source_target_pairs={{0,24},{1,25},{2,26},{3,27},{4,28},{5,29},{6,30},{7,31},{8,16},{9,... | collective-permute-start | bytes 442376 | tf_op jit(solution)/shard_map/ppermute | solution.py:111
  206.2 16.2 %collective-permute-start.25 = (bf16[8,24,2304]{2,1,0:T(8,128)(2,1)}, bf16[8,24,2304]{2,1,0:T(8,128)(2,1)S(1)}, u32[]{:S(2)}, u32[]{:S(2)}) collective-permute-start(bf16[8,24,2304]{2,1,0:T(8,128)(2,1)} %turn.17.refs_18_), channel_id=1, source_target_pairs={{0,2},{1,5},{2,0},{3,7},{4,6},{5,1},{6,4},{7,3},{8,10},{9,13},{10,... | collective-permute-start | bytes 2654216 | tf_op jit(solution)/shard_map/ppermute | solution.py:111
  222.3 23.7 %collective-permute-start.31 = (f32[16,768]{1,0:T(8,128)}, f32[16,768]{1,0:T(8,128)S(1)}, u32[]{:S(2)}, u32[]{:S(2)}) collective-permute-start(f32[16,768]{1,0:T(8,128)} %get-tuple-element.135.refs_17_.refs_12_), channel_id=1, source_target_pairs={{0,1},{1,0},{2,3},{3,2},{4,5},{5,4},{6,7},{7,6},{8,9},{9,8},{10,11... | collective-permute-start | bytes 147464 | tf_op jit(solution)/shard_map/ppermute | solution.py:111
  230.7 15.7 %collective-permute-start.28 = (bf16[4,24,2304]{2,1,0:T(8,128)(2,1)}, bf16[4,24,2304]{2,1,0:T(8,128)(2,1)S(1)}, u32[]{:S(2)}, u32[]{:S(2)}) collective-permute-start(bf16[4,24,2304]{2,1,0:T(8,128)(2,1)} %get-tuple-element.138), channel_id=1, source_target_pairs={{0,8},{1,3},{2,10},{3,1},{4,12},{5,7},{6,14},{7,5},{8,0},{9,11},{1... | collective-permute-start | bytes 1327112 | tf_op jit(solution)/shard_map/ppermute | solution.py:111
  231.0 15.0 %collective-permute-start.29 = (bf16[2,24,3840]{2,1,0:T(8,128)(2,1)}, bf16[2,24,3840]{2,1,0:T(8,128)(2,1)S(1)}, u32[]{:S(2)}, u32[]{:S(2)}) collective-permute-start(bf16[2,24,3840]{2,1,0:T(8,128)(2,1)} %get-tuple-element.139), channel_id=1, source_target_pairs={{0,4},{1,9},{2,6},{3,11},{4,0},{5,13},{6,2},{7,15},{8,12},{9,1},{1... | collective-permute-start | bytes 1105928 | tf_op jit(solution)/shard_map/ppermute | solution.py:111
  232.1 13.9 %collective-permute-start.30 = (bf16[1,96,768]{2,1,0:T(8,128)(2,1)}, bf16[1,96,768]{2,1,0:T(8,128)(2,1)S(1)}, u32[]{:S(2)}, u32[]{:S(2)}) collective-permute-start(bf16[1,96,768]{2,1,0:T(8,128)(2,1)} %get-tuple-element.140.refs_10_), channel_id=1, source_target_pairs={{0,24},{1,25},{2,26},{3,27},{4,28},{5,29},{6,30},{7,31},{8,16},{9,... | collective-permute-start | bytes 442376 | tf_op jit(solution)/shard_map/ppermute | solution.py:111
  260.6 15.2 %collective-permute-start.34 = (bf16[2,96,768]{2,1,0:T(8,128)(2,1)}, bf16[2,96,768]{2,1,0:T(8,128)(2,1)S(1)}, u32[]{:S(2)}, u32[]{:S(2)}) collective-permute-start(bf16[2,96,768]{2,1,0:T(8,128)(2,1)} %get-tuple-element.143.refs_18_), channel_id=1, source_target_pairs={{0,8},{1,5},{2,10},{3,7},{4,12},{5,1},{6,14},{7,3},{8,0},{9,13},{1... | collective-permute-start | bytes 884744 | tf_op jit(solution)/shard_map/ppermute | solution.py:111
  261.9 42.3 %collective-permute-start.46 = (f32[1,28,24]{1,2,0:T(8,128)S(1)}, f32[1,28,24]{1,2,0:T(8,128)S(1)}, u32[]{:S(2)}, u32[]{:S(2)}) collective-permute-start(f32[1,28,24]{1,2,0:T(8,128)S(1)} %maximum_bitcast_fusion), channel_id=1, source_target_pairs={{0,24},{1,25},{2,26},{3,27},{4,28},{5,29},{6,30},{7,31},{8,16},{9,... | collective-permute-start | bytes 8072 | tf_op jit(solution)/shard_map/ppermute | solution.py:111
  264.8 11.0 %collective-permute-start.32 = (bf16[2,24,2304]{2,1,0:T(8,128)(2,1)}, bf16[2,24,2304]{2,1,0:T(8,128)(2,1)S(1)}, u32[]{:S(2)}, u32[]{:S(2)}) collective-permute-start(bf16[2,24,2304]{2,1,0:T(8,128)(2,1)} %get-tuple-element.141), channel_id=1, source_target_pairs={{0,4},{1,9},{2,6},{3,11},{4,0},{5,13},{6,2},{7,15},{8,12},{9,1},{1... | collective-permute-start | bytes 663560 | tf_op jit(solution)/shard_map/ppermute | solution.py:111
  299.2 12.0 %collective-permute-start.37 = (bf16[1,24,3840]{2,1,0:T(8,128)(2,1)}, bf16[1,24,3840]{2,1,0:T(8,128)(2,1)S(1)}, u32[]{:S(2)}, u32[]{:S(2)}) collective-permute-start(bf16[1,24,3840]{2,1,0:T(8,128)(2,1)} %get-tuple-element.146.refs_10_), channel_id=1, source_target_pairs={{0,24},{1,25},{2,26},{3,27},{4,28},{5,29},{6,30},{7,31},{8,16},{9,... | collective-permute-start | bytes 552968 | tf_op jit(solution)/shard_map/ppermute | solution.py:111
  300.3 10.9 %collective-permute-start.36 = (bf16[1,24,2304]{2,1,0:T(8,128)(2,1)}, bf16[1,24,2304]{2,1,0:T(8,128)(2,1)S(1)}, u32[]{:S(2)}, u32[]{:S(2)}) collective-permute-start(bf16[1,24,2304]{2,1,0:T(8,128)(2,1)} %get-tuple-element.145), channel_id=1, source_target_pairs={{0,24},{1,25},{2,26},{3,27},{4,28},{5,29},{6,30},{7,31},{8,16},{9,... | collective-permute-start | bytes 331784 | tf_op jit(solution)/shard_map/ppermute | solution.py:111
  304.1 25.1 %collective-permute-start.47 = (f32[2,28,24]{1,2,0:T(8,128)S(1)}, f32[2,28,24]{1,2,0:T(8,128)S(1)}, u32[]{:S(2)}, u32[]{:S(2)}) collective-permute-start(f32[2,28,24]{1,2,0:T(8,128)S(1)} %pad_maximum_fusion.2), channel_id=1, source_target_pairs={{0,8},{1,5},{2,10},{3,7},{4,12},{5,1},{6,14},{7,3},{8,0},{9,13},{1... | collective-permute-start | bytes 16136 | tf_op jit(solution)/shard_map/ppermute | solution.py:111
  304.2 33.4 %collective-permute-start.42 = (bf16[4,96,768]{2,1,0:T(8,128)(2,1)}, bf16[4,96,768]{2,1,0:T(8,128)(2,1)S(1)}, u32[]{:S(2)}, u32[]{:S(2)}) collective-permute-start(bf16[4,96,768]{2,1,0:T(8,128)(2,1)} %get-tuple-element.151.refs_7_), channel_id=1, source_target_pairs={{0,4},{1,9},{2,6},{3,11},{4,0},{5,13},{6,2},{7,15},{8,12},{9,1},{1... | collective-permute-start | bytes 1769480 | tf_op jit(solution)/shard_map/ppermute | solution.py:111
  373.6 28.1 %collective-permute-start.45 = (bf16[4,24,3840]{2,1,0:T(8,128)(2,1)}, bf16[4,24,3840]{2,1,0:T(8,128)(2,1)S(1)}, u32[]{:S(2)}, u32[]{:S(2)}) collective-permute-start(bf16[4,24,3840]{2,1,0:T(8,128)(2,1)} %get-tuple-element.154.refs_1_), channel_id=1, source_target_pairs={{0,4},{1,9},{2,6},{3,11},{4,0},{5,13},{6,2},{7,15},{8,12},{9,1},{1... | collective-permute-start | bytes 2211848 | tf_op jit(solution)/shard_map/ppermute | solution.py:111
  375.0 24.6 %collective-permute-start.49 = (f32[16,768]{1,0:T(8,128)}, f32[16,768]{1,0:T(8,128)S(1)}, u32[]{:S(2)}, u32[]{:S(2)}) collective-permute-start(f32[16,768]{1,0:T(8,128)} %get-tuple-element.164), channel_id=1, source_target_pairs={{0,24},{1,25},{2,26},{3,27},{4,28},{5,29},{6,30},{7,31},{8,16},{9,... | collective-permute-start | bytes 147464 | tf_op jit(solution)/shard_map/ppermute | solution.py:111
  (58 other events, 279.9 us)

commit v4 on v2

--- a/solution.py
+++ b/solution.py
@@ -116,20 +116,22 @@
             masks = np.concatenate([masks, masks ^ mask])
         return masks
 
-    def owners(self, fi, bi):
-        mine = bi * self.nf + fi
-        even, odd = (jnp.asarray(self.spans(order[1:]), jnp.int32) for order in self.scatter)
-        is_even = (fi & 1) == 0
-        keep = mine ^ jnp.where(is_even, even, odd)
-        send = (mine ^ 1) ^ jnp.where(is_even, odd, even)
-        index = jnp.concatenate([keep, send])
-        return (index & (self.nf - 1)) * self.nb + (index >> self.fbits)
-
-    def gathered(self, fi, bi):
-        even, odd = (
-            jnp.asarray(self.spans(gens[::-1]) >> self.fbits, jnp.int32) for gens in self.gather
-        )
-        return bi ^ jnp.where((fi & 1) == 0, even, odd)
+    def table(self):
+        rows = []
+        for index in range(self.nd):
+            core, fi, bi = index & 1, index & (self.nf - 1), index >> self.fbits
+            halves = (bi & 1, (bi >> 1) & 1)
+            keep = index ^ self.spans(self.scatter[core][1:])
+            send = (index ^ 1) ^ self.spans(self.scatter[1 - core][1:])
+            order = np.concatenate([keep, send])
+            owners = (order & (self.nf - 1)) * self.nb + (order >> self.fbits)
+            places = bi ^ (self.spans(self.gather[core][::-1]) >> self.fbits)
+            own = np.asarray([fi, halves[core], halves[1 - core], bi])
+            rows.append(np.concatenate([own, owners, places]))
+        return np.stack(rows).astype(np.int32)
+
+
+OWN = 4
 
 
 PIECES = ((0, None), (1, None), (2, 0), (2, 1), (3, 2), (3, 3))
@@ -294,7 +296,7 @@
     half, block, _ = send_ref.shape
     for out_ref, base in ((send_ref, half), (keep_ref, 0)):
         for spot in range(half):
-            start = pl.multiple_of(owners_ref[base + spot] * block, 8)
+            start = pl.multiple_of(owners_ref[OWN + base + spot] * block, 8)
             out_ref[spot] = acc_ref[pl.ds(start, block), :].astype(BF16)
 
 
@@ -516,50 +518,28 @@
     out_ref[0] = dot(perm_ref[0], y.astype(BF16)).astype(BF16)
 
 
-def add_kernel(count, *refs):
-    ins, outs = refs[: -1 - (len(refs) > count + 1)], refs[-1 - (len(refs) > count + 1) :]
-    total = ins[0][...].astype(F32)
-    for ref in ins[1:count]:
-        total = total + ref[...].astype(F32)
-    outs[0][...] = total.astype(BF16)
-    if len(outs) > 1:
-        outs[1][...] = ins[count][...] + ins[count + 1][...]
-
-
-def finish_kernel(count, which, place_ref, *refs):
-    parts = refs[:count]
-    number = len(which)
-    states = refs[count : count + 3 * number]
-    new_ref = refs[count + 3 * number]
-    moments = refs[count + 3 * number + 1 :]
-    total = parts[0][0].astype(F32)
-    for ref in parts[1:]:
-        total = total + ref[0].astype(F32)
-    start = 0
-    for spot, kind in enumerate(which):
-        master, first, second = states[3 * spot : 3 * spot + 3]
-        cols = slice(start, start + master.shape[1])
-        new_w, new_m, new_v = adamw(
-            master[...], total[:, cols], first[...], second[...], STEP_RATES[kind], DECAY_RATES[kind]
-        )
-        new_ref[0, :, cols] = new_w.astype(BF16)
-        moments[2 * spot][...] = new_m
-        moments[2 * spot + 1][...] = new_v
-        start += master.shape[1]
-
-
-def join_kernel(one_ref, two_ref, out_ref):
-    count = one_ref.shape[0]
-    out_ref[:count] = one_ref[...]
-    out_ref[count:] = two_ref[...]
-
-
-def place_kernel(number, spots_ref, blocks_ref, *refs):
-    start = 0
-    for out_ref in refs[-number:]:
-        width = out_ref.shape[1]
-        out_ref[...] = blocks_ref[0, :, start : start + width].astype(F32)
-        start += width
+def place_kernel(number, base, spots_ref, one_ref, two_ref, *refs):
+    step = pl.program_id(0)
+    count, rows, _ = one_ref.shape
+
+    def put(out_ref):
+        for spot in range(2 * count):
+            source = one_ref if spot < count else two_ref
+            at = pl.ds(pl.multiple_of(spots_ref[base + spot] * rows, 8), rows)
+            out_ref[at, :] = source[spot % count].astype(F32)
+
+    if number == 1:
+        put(refs[0])
+        return
+    last = pl.num_programs(0) - 1
+
+    @pl.when(step < last)
+    def _():
+        put(refs[0])
+
+    @pl.when(step == last)
+    def _():
+        put(refs[1])
 
 
 def later(value, dep):
@@ -568,12 +548,20 @@
 
 class Chain:
     def __init__(self):
-        self.last = None
+        self.last, self.waiting = None, []
+
+    def pin(self, values):
+        return lax.optimization_barrier((list(values), self.last))[0]
+
+    def hold(self, value):
+        self.waiting.append(value)
+        return value
 
     def __call__(
         self, kernel, grid, scalars, ins, outs, scratch, estimate, name, after=(), aliases=None
     ):
-        deps = list(after)
+        deps = list(after) + self.waiting
+        self.waiting = []
         if self.last is not None:
             deps.append(self.last)
         fixed = len(scalars) + len(ins)
@@ -613,85 +601,54 @@
         self.parts.append(got)
         self.place += 1
 
-    def add(self, vec=None):
+    def total(self, low, high):
+        parts = self.call.pin(self.parts)
+        total = parts[0][low:high].astype(F32)
+        for part in parts[1:]:
+            total = total + part[low:high].astype(F32)
+        return total
+
+    def add(self):
         self.count //= 2
-        count = self.count
-        _, rows, cols = self.parts[0].shape
-        block = max(1, count // 4)
-        base = count // block
-        spec = pl.BlockSpec((block, rows, cols), lambda i, *_: (base + i, 0, 0))
-        ins = [(part, spec) for part in self.parts]
-        outs = [
-            (pl.BlockSpec((block, rows, cols), lambda i, *_: (i, 0, 0)), (count, rows, cols), BF16)
-        ]
-        if vec is not None:
-            ins += [(value, full(value.shape)) for value in vec]
-            outs.append((full(vec[0].shape), vec[0].shape, F32))
-        size = count * rows * cols
-        got = self.call(
-            functools.partial(add_kernel, len(self.parts)),
-            (count // block,),
-            [],
-            ins,
-            outs,
-            [],
-            spent(1.5),
-            "add",
-        )
-        self.move(got[0])
-        return got[1] if vec is not None else None
+        total = self.total(self.count, 2 * self.count)
+        self.sent = self.call.hold(total.astype(BF16))
+        self.move(self.sent)
 
 
 class Spread:
     def __init__(self, plan, call, block):
-        self.plan, self.call, self.blocks, self.place = plan, call, block, 0
-        self.move()
-
-    def move(self):
-        self.got = self.plan.exchange(self.blocks, *(order[self.place] for order in self.plan.gather))
+        self.plan, self.call, self.place = plan, call, 0
+        self.move(block)
+
+    def move(self, blocks):
+        self.blocks = self.call.hold(blocks)
+        self.got = self.plan.exchange(blocks, *(order[self.place] for order in self.plan.gather))
         self.place += 1
 
     def join(self):
-        shape = self.blocks.shape
-        self.blocks = self.call(
-            join_kernel,
-            (1,),
-            [],
-            [(self.blocks, full(shape)), (self.got, full(shape))],
-            [(full((2 * shape[0],) + shape[1:]), (2 * shape[0],) + shape[1:], BF16)],
-            [],
-            spent(0.3),
-            "join",
-        )[0]
-        self.move()
-
-    def put(self, spots, widths, before=None):
-        blocks = self.blocks if before is None else self.got
-        count, rows, cols = blocks.shape
-        base = 0 if before is None else count
-        nb = self.plan.nb
-        ins = [(blocks, pl.BlockSpec((1, rows, cols), lambda i, *_: (i, 0, 0)))]
-        aliases = None
-        if before is not None:
-            ins += [(value, ANYWHERE) for value in before]
-            aliases = {1 + k: k for k in range(len(widths))}
+        self.move(jnp.concatenate(self.call.pin([self.blocks, self.got]), axis=0))
+
+    def put(self, base, tab, widths):
+        count, rows, cols = self.blocks.shape
+        step = D if len(widths) > 1 or cols > D else D // 3
+        last = widths[0] // step - 1
+        ins = [
+            (value, pl.BlockSpec((count, rows, step), lambda i, *_: (0, 0, i)))
+            for value in (self.blocks, self.got)
+        ]
+        maps = [lambda i, *_: (0, jnp.minimum(i, last)), lambda i, *_: (0, 0)]
         return self.call(
-            functools.partial(place_kernel, len(widths)),
-            (count,),
-            [spots],
+            functools.partial(place_kernel, len(widths), base),
+            (cols // step,),
+            [tab],
             ins,
             [
-                (
-                    pl.BlockSpec((rows, width), lambda i, spots_ref: (spots_ref[base + i], 0)),
-                    (nb * rows, width),
-                    F32,
-                )
-                for width in widths
+                (pl.BlockSpec((2 * count * rows, step), idx), (2 * count * rows, width), F32)
+                for idx, width in zip(maps, widths)
             ],
             [],
-            spent(0.1),
+            spent(1),
             "place",
-            aliases=aliases,
         )
 
 
@@ -722,11 +679,10 @@
     nf, nb, nd = plan.nf, plan.nb, plan.nd
     fi = lax.axis_index("fsdp").astype(jnp.int32)
     bi = lax.axis_index("batch").astype(jnp.int32)
-    halves = jnp.stack([bi & 1, (bi >> 1) & 1])
-    place = jnp.stack([fi, halves[fi & 1], halves[1 - (fi & 1)], bi])
-    owners = plan.owners(fi, bi)
-    spots = plan.gathered(fi, bi)
+    tab = lax.dynamic_index_in_dim(jnp.asarray(plan.table()), bi * nf + fi, 0, keepdims=False)
+    place = owners = tab
     call = Chain()
+
 
     def pair_spec(rows, cols):
         return pl.BlockSpec((1, rows, cols), lambda i, *_: (i, 0, 0))
@@ -805,7 +761,7 @@
 
     set_b = cast([w_out, w_fc1])
     near_a = set_a[2]
-    set_a = last_piece(spread_pieces(set_a))
+    set_a = last_piece(spread_pieces(set_a, set_b[0]))
     set_c = cast([w_fc2], [near_a])
 
     n1, qkv = call(
@@ -872,7 +828,7 @@
     def grad_sum(outs):
         if len(outs) == 1:
             rows, cols = outs[0].shape
-            blocks = jnp.take(outs[0].reshape(nd, rows // nd, cols), owners, axis=0)
+            blocks = jnp.take(outs[0].reshape(nd, rows // nd, cols), tab[OWN : OWN + nd], axis=0)
             outs = [blocks[: nd // 2], blocks[nd // 2 :]]
         return Sum(plan, call, *outs)
 
@@ -1003,67 +959,41 @@
         "gqkv",
     )
     sum_3 = grad_sum(got)
-    while sum_2.count > 1:
-        sum_2.add()
     sum_1.add()
 
     fallback = (D // nd) % 8 != 0 or (FF // nd) % 8 != 0
+    places = OWN + nd
 
     def finish(total, which, masters, moments):
         _, rows, cols = total.parts[0].shape
-        if fallback:
-            grad = sum(part[0].astype(F32) for part in total.parts)
-            start, news, states = 0, [], []
-            for kind, master, (first, second) in zip(which, masters, moments):
-                width = master.shape[1]
-                own = lax.dynamic_slice_in_dim(master, bi * rows, rows, 0)
-                new_w, new_m, new_v = adamw(
-                    own,
-                    grad[:, start : start + width],
-                    first,
-                    second,
-                    STEP_RATES[kind],
-                    DECAY_RATES[kind],
-                )
-                news.append(new_w.astype(BF16))
-                states += [new_m, new_v]
-                start += width
-            block = jnp.concatenate(news, axis=1)[None]
-        else:
-            own = pl.BlockSpec((1, rows, cols), lambda i, *_: (0, 0, 0))
-            ins = [(part, own) for part in total.parts]
-            outs = [(full((1, rows, cols)), (1, rows, cols), BF16)]
-            for master, pair in zip(masters, moments):
-                width = master.shape[1]
-                ins.append((master, pl.BlockSpec((rows, width), lambda i, place_ref: (place_ref[3], 0))))
-                ins += [(value, full(value.shape)) for value in pair]
-                outs += [(full((rows, width)), (rows, width), F32)] * 2
-            block, *states = call(
-                functools.partial(finish_kernel, len(total.parts), which),
-                (1,),
-                [place],
-                ins,
-                outs,
-                [],
-                spent(2),
-                "finish",
+        grad = total.total(0, 1)[0]
+        start, news, made = 0, [], []
+        for kind, master, (first, second) in zip(which, masters, moments):
+            width = master.shape[1]
+            own = lax.dynamic_slice_in_dim(master, bi * rows, rows, 0)
+            new_w, new_m, new_v = adamw(
+                own,
+                grad[:, start : start + width],
+                first,
+                second,
+                STEP_RATES[kind],
+                DECAY_RATES[kind],
             )
-        return Spread(plan, call, block), states
-
-    def put(moved, widths, before=None):
+            news.append(new_w.astype(BF16))
+            made += [new_m, new_v]
+            start += width
+        return Spread(plan, call, jnp.concatenate(news, axis=1)[None]), made
+
+    def put(moved, widths):
         if not fallback:
-            return moved.put(spots, widths, before)
-        if before is None:
-            return moved.blocks
-        blocks = jnp.concatenate([before, moved.got], axis=0)
+            return moved.put(places, tab, widths)
+        blocks = jnp.concatenate([moved.blocks, moved.got], axis=0)
         count, rows, cols = blocks.shape
-        order = jnp.zeros(count, jnp.int32).at[spots].set(jnp.arange(count, dtype=jnp.int32))
+        order = jnp.zeros(count, jnp.int32).at[tab[places:]].set(jnp.arange(count, dtype=jnp.int32))
         blocks = jnp.take(blocks, order, axis=0).reshape(count * rows, cols).astype(F32)
         cuts = np.cumsum([0] + list(widths))
         return [blocks[:, a:b] for a, b in zip(cuts[:-1], cuts[1:])]
 
-    last = plan.bbits
-    moved_2, (new_m2, new_v2) = finish(sum_2, (3,), (w_fc2,), ((m_fc2, v_fc2),))
     sum_3.add()
 
     grad_tokens, vec_sum = call(
@@ -1095,20 +1025,13 @@
 
     vec_gens = [1, 2] + plan.batch
     vec_got = plan.exchange(vec_sum, vec_gens[0])
-    vec_place = 1
-
-    def vec_step(total):
-        nonlocal vec_sum, vec_got, vec_place
-        if vec_place > len(vec_gens):
-            total.add()
-            return
-        vec_sum = total.add((vec_sum, vec_got))
-        vec_got = plan.exchange(vec_sum, vec_gens[vec_place]) if vec_place < len(vec_gens) else None
-        vec_place += 1
-
-    moved_2.join()
+
+    last = plan.bbits
+    sum_3.add()
     sum_1.add()
-    vec_step(sum_3)
+    while sum_2.count > 1:
+        sum_2.add()
+    moved_2, (new_m2, new_v2) = finish(sum_2, (3,), (w_fc2,), ((m_fc2, v_fc2),))
 
     (layer_out,) = call(
         functools.partial(out_kernel, rows_f),
@@ -1127,36 +1050,58 @@
         "out",
     )
 
-    while sum_1.count > 1:
-        sum_1.add()
-    vec_step(sum_3)
+    vec_place = 1
+
+    def vec_step():
+        nonlocal vec_sum, vec_got, vec_place
+        if vec_place > len(vec_gens):
+            return
+        one, two = call.pin([vec_sum, vec_got])
+        vec_sum = one + two
+        if vec_place < len(vec_gens):
+            vec_got = plan.exchange(vec_sum, vec_gens[vec_place])
+        vec_place += 1
+
+    moved_1 = moved_3 = None
+    while moved_3 is None or moved_3.place < last:
+        token = None
+        if sum_3.count > 1:
+            sum_3.add()
+            token = sum_3.sent
+        elif moved_3 is None:
+            moved_3, (new_mq, new_vq) = finish(sum_3, (0,), (w_qkv,), ((m_qkv, v_qkv),))
+            token = moved_3.blocks
+        else:
+            moved_3.join()
+            token = moved_3.blocks
+        if sum_1.count > 1:
+            sum_1.add()
+        elif moved_1 is None:
+            moved_1, (new_m1, new_v1, new_mo, new_vo) = finish(
+                sum_1, (2, 1), (w_fc1, w_out), ((m_fc1, v_fc1), (m_out, v_out))
+            )
+        elif moved_1.place < last:
+            moved_1.join()
+        if moved_2.place < last:
+            moved_2.join()
+        vec_step()
+        call.last = token
+    while len(vec_gens) >= vec_place:
+        vec_step()
+    while moved_1.place < last:
+        moved_1.join()
     while moved_2.place < last:
         moved_2.join()
-    put_2 = put(moved_2, (D,))
-    while sum_3.count > 1:
-        vec_step(sum_3)
-    moved_1, (new_m1, new_v1, new_mo, new_vo) = finish(
-        sum_1, (2, 1), (w_fc1, w_out), ((m_fc1, v_fc1), (m_out, v_out))
-    )
-    moved_3, (new_mq, new_vq) = finish(sum_3, (0,), (w_qkv,), ((m_qkv, v_qkv),))
-    (new_2,) = put(moved_2, (D,), put_2)
-    while moved_3.place < last:
-        moved_1.join()
-        moved_3.join()
-    put_1 = put(moved_1, (FF, D))
-    put_3 = put(moved_3, (3 * D,))
-    new_1, new_o = put(moved_1, (FF, D), put_1)
-    (new_q,) = put(moved_3, (3 * D,), put_3)
-
-    while vec_place <= len(vec_gens):
-        vec_sum = vec_sum + vec_got
-        vec_got = plan.exchange(vec_sum, vec_gens[vec_place]) if vec_place < len(vec_gens) else None
-        vec_place += 1
+    call.waiting = []
+    (new_2,) = put(moved_2, (D,))
+    new_1, new_o = put(moved_1, (FF, D))
+    (new_q,) = put(moved_3, (3 * D,))
+
     states = jnp.concatenate([m_vec, v_vec], axis=0)[None]
     for rank in range(plan.bbits):
         got = plan.exchange(states, *(order[rank] for order in plan.gather))
         states = jnp.concatenate([states, got], axis=0)
-    order = jnp.zeros(nb, jnp.int32).at[spots].set(jnp.arange(nb, dtype=jnp.int32))
+    order = jnp.zeros(nb, jnp.int32).at[tab[places:]].set(jnp.arange(nb, dtype=jnp.int32))
     own_cols = D // nd
     states = jnp.transpose(jnp.take(states, order, axis=0), (1, 0, 2)).reshape(2 * NVEC, nb * own_cols)
     grad_vec = lax.dynamic_slice_in_dim(vec_sum[:NVEC], fi * nb * own_cols, nb * own_cols, 1)

time: 336 us -> 302 us (0.90)
  Pallas kernels: 236 us -> 171 us
  other arithmetic: 5.56 us -> 36.9 us
  local copies, waits for them, and re-layouts: 24.7 us -> 10.2 us
  starting transfers between devices: 44.9 us -> 52.9 us
  waiting for transfers between devices: 20.8 us -> 28.2 us
    pallas_call x43 -> x19, Pallas kernels: 236 us -> 171 us  [__call__(): pl.pallas_call(body, grid_spec=pltpu.PrefetchScalarGridSpec(num_scalar_pr...]
    convert_element_type x0 -> x14, other arithmetic: none -> 25.2 us  [the longest x12 21.6 us: add(): self.sent = self.call.hold(total.astype(BF16))]
    unnamed x92 -> x82, local copies, waits for them, and re-layouts: 22 us -> 5.02 us
    ppermute x50, starting transfers between devices: 44.9 us -> 52.9 us  [exchange(): return lax.ppermute(value, ('batch', 'fsdp'), pairs)]
    ppermute x50, waiting for transfers between devices: 20.8 us -> 28.2 us  [exchange(): return lax.ppermute(value, ('batch', 'fsdp'), pairs)]
    broadcast_in_dim x0 -> x3, other arithmetic: none -> 4.71 us  [finish(): return (Spread(plan, call, jnp.concatenate(news, axis=1)[None]), made)]
  transfers between devices with their start and end apart: 50 -> 50, of which waited for: 9 -> 13; matrix products, arithmetic and copies ran while one was open for 2% -> 14% of each run, Pallas kernels for 69% -> 55%
where the time goes in v4:
time: 302 us; the launch traced here: 301 us
  Pallas kernels  171 us (57%)
  starting transfers between devices  52.9 us (18%)
  other arithmetic  36.9 us (12%)
  waiting for transfers between devices  28.2 us (9%)
  local copies, waits for them, and re-layouts  10.2 us (3%)
    pallas_call x19, Pallas kernels, __call__(): pl.pallas_call(body, grid_spec=pltpu.PrefetchScalarGridSpec(num_scalar_pr...  171 us
    ppermute x50, starting transfers between devices, exchange(): return lax.ppermute(value, ('batch', 'fsdp'), pairs)  52.9 us
    ppermute x50, waiting for transfers between devices, exchange(): return lax.ppermute(value, ('batch', 'fsdp'), pairs)  28.2 us
    convert_element_type x12, other arithmetic, add(): self.sent = self.call.hold(total.astype(BF16))  21.6 us
  transfers between devices with their start and end apart: 50, of which 13 were waited for; matrix products, arithmetic and copies ran while one was open for 14% of the time, Pallas kernels for 55%

profile of v4, /device:TPU:0, one launch (start us, length us, event | category | flops | bytes accessed | tf_op | source)
XLA Modules:
  0.0 300.6 jit_solution(13478545116312351319)
XLA Ops:
  1.9 3.1 %cast.3 = (bf16[192,2304]{1,0:T(8,128)(2,1)}, bf16[96,2304]{1,0:T(8,128)(2,1)}) custom-call(s32[44]{0:T(128)} %get-tuple-element.291.refs_0_, f32[192,2304]{1,0:T(8,128)} %refs_1_.3), custom_call_target="tpu_custom_call" | custom-call | flops 6635520000 | bytes 22118400 | tf_op jit(solution)/shard_map/cast/pallas_call | solution.py:573
  5.0 3.0 collective-permute-start.4
  8.0 6.0 %order.1 = (bf16[4,256,256]{2,1,0:T(8,128)(2,1)}, bf16[4,256,768]{2,1,0:T(8,128)(2,1)}, f32[4,256,128]{2,1,0:T(8,128)}, bf16[4,128,768]{2,1,0:T(8,128)(2,1)}) custom-call(s32[4]{0:T(128)} %refs_0_.1, s32[4,1,128]{2,1,0:T(1,128)} %bitcast.33, bf16[4,256,768]{2,1,0:T(8,128)(2,1)} %refs_2_.2, bf16[4,256,768]{2,1,0:T(8,128)(2,1)} %refs_3_.1, ...), custom_call_target="tpu_custom_call" | custom-call | flops 17999998976 | bytes 60000000 | tf_op jit(solution)/shard_map/order/pallas_call | solution.py:573
  14.0 3.8 %cast.4 = (bf16[192,3840]{1,0:T(8,128)(2,1)}, bf16[96,3840]{1,0:T(8,128)(2,1)}) custom-call(s32[44]{0:T(128)} %get-tuple-element.291.refs_0_, f32[192,768]{1,0:T(8,128)} %refs_1_.4, f32[192,3072]{1,0:T(8,128)} %refs_2_.3, bf16[4,128,768]{2,1,0:T(8,128)(2,1)} %get-tuple-element.147.refs_3_.refs_2_.refs_1_), custom_call_target="tpu_custom_call" | custom-call | flops 11059200000 | bytes 36864000 | tf_op jit(solution)/shard_map/cast/pallas_call | solution.py:573
  27.1 3.4 %cast.5 = (bf16[768,768]{1,0:T(8,128)(2,1)}, bf16[384,768]{1,0:T(8,128)(2,1)}) custom-call(s32[44]{0:T(128)} %get-tuple-element.291.refs_0_, f32[768,768]{1,0:T(8,128)} %refs_1_.5, bf16[96,2304]{1,0:T(8,128)(2,1)} %collective-permute-done.4.refs_2_.refs_6_.refs_14_, bf16[96,3840]{1,0:T(8,128)(2,1)} %get-tuple-element.150.refs_3_), custom_call_target="tpu_custom_call" | custom-call | flops 8847360000 | bytes 29491200 | tf_op jit(solution)/shard_map/cast/pallas_call | solution.py:573
  30.5 10.5 %qkv.1 = (bf16[4,256,768]{2,1,0:T(8,128)(2,1)}, bf16[4,256,2304]{2,1,0:T(8,128)(2,1)}) custom-call(s32[44]{0:T(128)} %get-tuple-element.291.refs_0_, bf16[4,256,768]{2,1,0:T(8,128)(2,1)} %get-tuple-element.144.refs_1_, f32[4,256,128]{2,1,0:T(8,128)} %get-tuple-element.145.refs_2_, f32[16,768]{1,0:T(8,128)} %fusion.13.refs_3_.refs_4_, ...), custom_call_target="tpu_custom_call" | custom-call | flops 3000000000 | bytes 10000000 | tf_op jit(solution)/shard_map/qkv/pallas_call | solution.py:573
  43.1 10.4 %mix.1.refs_3_.refs_11_ = bf16[4,256,768]{2,1,0:T(8,128)(2,1)} custom-call(bf16[4,256,2304]{2,1,0:T(8,128)(2,1)} %get-tuple-element.152.refs_0_.refs_2_, bf16[96,3840]{1,0:T(8,128)(2,1)} %copy-done.4, bf16[4,256,2304]{2,1,0:T(8,128)(2,1)} %get-tuple-element.152.refs_0_.refs_2_), custom_call_target="tpu_custom_call" | custom-call | flops 3000000000 | bytes 10000000 | tf_op jit(solution)/shard_map/mix/pallas_call | solution.py:573
  54.1 3.6 %collective-permute-start.42 = (f32[1,28,24]{1,2,0:T(8,128)S(1)}, f32[1,28,24]{1,2,0:T(8,128)S(1)}, u32[]{:S(2)}, u32[]{:S(2)}) collective-permute-start(f32[1,28,24]{1,2,0:T(8,128)S(1)} %maximum_bitcast_fusion.1), channel_id=1, source_target_pairs={{0,24},{1,25},{2,26},{3,27},{4,28},{5,29},{6,30},{7,31},{8,16},{9,... | collective-permute-start | bytes 8072 | tf_op jit(solution)/shard_map/ppermute | solution.py:111
  60.3 17.9 %fc1.1 = (f32[4,256,768]{2,1,0:T(8,128)}, bf16[4,256,768]{2,1,0:T(8,128)(2,1)}, bf16[4,256,3072]{2,1,0:T(8,128)(2,1)}, bf16[4,128,3072]{2,1,0:T(8,128)(2,1)}) custom-call(s32[44]{0:T(128)} %get-tuple-element.291.refs_0_, bf16[4,256,768]{2,1,0:T(8,128)(2,1)} %get-tuple-element.144.refs_1_, f32[4,256,128]{2,1,0:T(8,128)} %get-tuple-element.145.refs_2_, ...), custom_call_target="tpu_custom_call" | custom-call | flops 54000001024 | bytes 180000000 | tf_op jit(solution)/shard_map/fc1/pallas_call | solution.py:573
  79.7 8.1 %gw2.1 = (bf16[16,96,768]{2,1,0:T(8,128)(2,1)}, bf16[16,96,768]{2,1,0:T(8,128)(2,1)}, f32[1,768]{1,0:T(1,128)}) custom-call(s32[44]{0:T(128)} %get-tuple-element.291.refs_0_, bf16[4,256,3072]{2,1,0:T(8,128)(2,1)} %get-tuple-element.156.refs_1_, bf16[4,128,768]{2,1,0:T(8,128)(2,1)} %get-tuple-element.147.refs_3_.refs_2_.refs_1_, ...), custom_call_target="tpu_custom_call" | custom-call | flops 24000000000 | bytes 80000000 | tf_op jit(solution)/shard_map/gw2/pallas_call | solution.py:573
  92.3 9.6 %df.1 = (bf16[512,3072]{1,0:T(8,128)(2,1)}, f32[1,3072]{1,0:T(1,128)}) custom-call(s32[44]{0:T(128)} %get-tuple-element.291.refs_0_, bf16[4,128,768]{2,1,0:T(8,128)(2,1)} %get-tuple-element.147.refs_3_.refs_2_.refs_1_, bf16[4,128,3072]{2,1,0:T(8,128)(2,1)} %get-tuple-element.162.refs_3_.refs_2_, bf16[768,768]{1,0:T(8,128)(2,1)} %get-tuple-element.159.refs_3_.refs_5_, ...), custom_call_target="tpu_custom_call" | custom-call | flops 20999999488 | bytes 70000000 | tf_op jit(solution)/shard_map/df/pallas_call | solution.py:573
  104.5 11.3 %mlp_back.1 = (f32[4,128,768]{2,1,0:T(8,128)}, bf16[4,128,768]{2,1,0:T(8,128)(2,1)}, bf16[4,128,768]{2,1,0:T(8,128)(2,1)}, f32[8,768]{1,0:T(8,128)}) custom-call(s32[44]{0:T(128)} %get-tuple-element.291.refs_0_, bf16[512,3072]{1,0:T(8,128)(2,1)} %get-tuple-element.165.refs_1_.refs_2_, bf16[4,128,768]{2,1,0:T(8,128)(2,1)} %get-tuple-element.147.refs_3_.refs_2_.refs_1_, ...), custom_call_target="tpu_custom_call" | custom-call | flops 30000001024 | bytes 100000000 | tf_op jit(solution)/shard_map/mlp_back/pallas_call | solution.py:573
  115.8 9.2 %gw1o.1 = (bf16[16,24,3840]{2,1,0:T(8,128)(2,1)}, bf16[16,24,3840]{2,1,0:T(8,128)(2,1)}) custom-call(s32[44]{0:T(128)} %get-tuple-element.291.refs_0_, bf16[4,256,768]{2,1,0:T(8,128)(2,1)} %get-tuple-element.160.refs_1_, bf16[512,3072]{1,0:T(8,128)(2,1)} %get-tuple-element.165.refs_1_.refs_2_, bf16[4,256,768]{2,1,0:T(8,128)(2,1)} %mix.1.refs_3_.refs_11_, ...), custom_call_target="tpu_custom_call" | custom-call | flops 27000000512 | bytes 90000000 | tf_op jit(solution)/shard_map/gw1o/pallas_call | solution.py:573
  128.4 13.7 %attn_back.2 = (bf16[4,128,768]{2,1,0:T(8,128)(2,1)}, bf16[4,256,1536]{2,1,0:T(8,128)(2,1)}, f32[8,768]{1,0:T(8,128)}) custom-call(bf16[4,256,2304]{2,1,0:T(8,128)(2,1)} %get-tuple-element.152.refs_0_.refs_2_, bf16[4,128,768]{2,1,0:T(8,128)(2,1)} %get-tuple-element.171.refs_1_, bf16[4,96,768]{2,1,0:T(8,128)(2,1)} %copy-done.5, ...), custom_call_target="tpu_custom_call" | custom-call | flops 35999997952 | bytes 120000000 | tf_op jit(solution)/shard_map/attn_back/pallas_call | solution.py:573
  144.9 2.8 add_convert_fusion.refs_5_
  148.8 13.5 %attn_back.3 = (bf16[4,128,768]{2,1,0:T(8,128)(2,1)}, bf16[4,256,1536]{2,1,0:T(8,128)(2,1)}, f32[8,768]{1,0:T(8,128)}) custom-call(bf16[4,256,2304]{2,1,0:T(8,128)(2,1)} %get-tuple-element.152.refs_0_.refs_2_, bf16[4,128,768]{2,1,0:T(8,128)(2,1)} %get-tuple-element.171.refs_1_, ...), custom_call_target="tpu_custom_call", output_to_operand_aliasing={{0}: (2, {}), {1}: (3, {})} | custom-call | flops 35999997952 | bytes 120000000 | tf_op jit(solution)/shard_map/attn_back/pallas_call | solution.py:573
  164.4 8.9 %gqkv.1 = (bf16[16,24,2304]{2,1,0:T(8,128)(2,1)}, bf16[16,24,2304]{2,1,0:T(8,128)(2,1)}) custom-call(s32[44]{0:T(128)} %get-tuple-element.291.refs_0_, bf16[4,256,768]{2,1,0:T(8,128)(2,1)} %get-tuple-element.153.refs_1_, bf16[4,128,768]{2,1,0:T(8,128)(2,1)} %get-tuple-element.188.refs_2_.refs_4_, bf16[4,256,1536]{2,1,0:T(8,128)(2,1)} %get-tuple-element.189.refs_3_.refs_5_, ...), custom_call_target="tpu_custom_call" | custom-call | flops 27000000512 | bytes 90000000 | tf_op jit(solution)/shard_map/gqkv/pallas_call | solution.py:573
  174.7 3.4 %collective-permute-done.44 = f32[4,28,24]{1,2,0:T(8,128)S(1)} collective-permute-done((f32[4,28,24]{1,2,0:T(8,128)S(1)}, f32[4,28,24]{1,2,0:T(8,128)S(1)}, u32[]{:S(2)}, u32[]{:S(2)}) %collective-permute-start.44) | collective-permute-done | bytes 10784 | tf_op jit(solution)/shard_map/ppermute | solution.py:111
  180.7 2.7 add_convert_fusion.3.refs_18_
  187.1 15.2 %grad_in.1 = (f32[4,256,768]{2,1,0:T(8,128)}, f32[16,768]{1,0:T(8,128)}) custom-call(s32[44]{0:T(128)} %get-tuple-element.291.refs_0_, bf16[4,256,768]{2,1,0:T(8,128)(2,1)} %get-tuple-element.144.refs_1_, f32[4,256,128]{2,1,0:T(8,128)} %get-tuple-element.145.refs_2_, f32[16,768]{1,0:T(8,128)} %fusion.13.refs_3_.refs_4_, ...), custom_call_target="tpu_custom_call" | custom-call | flops 44999999488 | bytes 150000000 | tf_op jit(solution)/shard_map/grad_in/pallas_call | solution.py:573
  202.5 2.5 fusion.3
  205.0 3.0 collective-permute-start.39
  213.4 13.0 %out.1 = bf16[4,256,768]{2,1,0:T(8,128)(2,1)} custom-call(s32[44]{0:T(128)} %get-tuple-element.291.refs_0_, bf16[4,256,3072]{2,1,0:T(8,128)(2,1)} %get-tuple-element.156.refs_1_, f32[4,256,768]{2,1,0:T(8,128)} %get-tuple-element.157.refs_3_.refs_2_, f32[16,768]{1,0:T(8,128)} %fusion.13.refs_3_.refs_4_, ...), custom_call_target="tpu_custom_call" | custom-call | flops 38999998464 | bytes 130000000 | tf_op jit(solution)/shard_map/out/pallas_call | solution.py:573
  237.0 4.0 %collective-permute-done.40 = bf16[2,96,768]{2,1,0:T(8,128)(2,1)S(1)} collective-permute-done((bf16[2,96,768]{2,1,0:T(8,128)(2,1)S(1)}, bf16[2,96,768]{2,1,0:T(8,128)(2,1)S(1)}, u32[]{:S(2)}, u32[]{:S(2)}) %collective-permute-start.40) | collective-permute-done | bytes 294944 | tf_op jit(solution)/shard_map/ppermute | solution.py:111
  247.6 3.7 %collective-permute-start.36 = (bf16[1,24,3840]{2,1,0:T(8,128)(2,1)S(1)}, bf16[1,24,3840]{2,1,0:T(8,128)(2,1)S(1)}, u32[]{:S(2)}, u32[]{:S(2)}) collective-permute-start(bf16[1,24,3840]{2,1,0:T(8,128)(2,1)S(1)} %maximum_bitcast_fusion), channel_id=1, source_target_pairs={{0,24},{1,25},{2,26},{3,27},{4,28},{5,29},{6,30},{7,31},{8,16},{9,... | collective-permute-start | bytes 552968 | tf_op jit(solution)/shard_map/ppermute | solution.py:111
  255.3 3.9 %collective-permute-done.30 = bf16[1,24,2304]{2,1,0:T(8,128)(2,1)S(1)} collective-permute-done((bf16[1,24,2304]{2,1,0:T(8,128)(2,1)S(1)}, bf16[1,24,2304]{2,1,0:T(8,128)(2,1)S(1)}, u32[]{:S(2)}, u32[]{:S(2)}) %collective-permute-start.30) | collective-permute-done | bytes 110624 | tf_op jit(solution)/shard_map/ppermute | solution.py:111
  262.1 3.5 %collective-permute-start.37 = (bf16[2,24,3840]{2,1,0:T(8,128)(2,1)S(1)}, bf16[2,24,3840]{2,1,0:T(8,128)(2,1)S(1)}, u32[]{:S(2)}, u32[]{:S(2)}) collective-permute-start(bf16[2,24,3840]{2,1,0:T(8,128)(2,1)S(1)} %constant_dynamic-update-slice_fusion.4), channel_id=1, source_target_pairs={{0,8},{1,5},{2,10},{3,7},{4,12},{5,1},{6,14},{7,3},{8,0},{9,13},{1... | collective-permute-start | bytes 1105928 | tf_op jit(solution)/shard_map/ppermute | solution.py:111
  269.7 6.9 %collective-permute-done.49 = f32[16,768]{1,0:T(8,128)S(1)} collective-permute-done((f32[16,768]{1,0:T(8,128)S(1)}, f32[16,768]{1,0:T(8,128)S(1)}, u32[]{:S(2)}, u32[]{:S(2)}) %collective-permute-start.49) | collective-permute-done | bytes 49184 | tf_op jit(solution)/shard_map/ppermute | solution.py:111
  282.7 4.2 %place.3.refs_3_ = f32[768,768]{1,0:T(8,128)} custom-call(s32[44]{0:T(128)} %get-tuple-element.291.refs_0_, bf16[4,96,768]{2,1,0:T(8,128)(2,1)} %copy-done.19, bf16[4,96,768]{2,1,0:T(8,128)(2,1)} %collective-permute-done.41.refs_2_, bf16[4,24,2304]{2,1,0:T(8,128)(2,1)} %copy-done.22), custom_call_target="tpu_custom_call" | custom-call | flops 3000000000 | bytes 10000000 | tf_op jit(solution)/shard_map/place/pallas_call | solution.py:573
  286.8 2.8 collective-permute-done.38.refs_2_
  290.4 5.5 %place.4 = (f32[192,3072]{1,0:T(8,128)}, f32[192,768]{1,0:T(8,128)}) custom-call(s32[44]{0:T(128)} %get-tuple-element.291.refs_0_, bf16[4,24,3840]{2,1,0:T(8,128)(2,1)} %copy-done.17, bf16[4,24,3840]{2,1,0:T(8,128)(2,1)} %copy-done.35, f32[768,768]{1,0:T(8,128)} %place.3.refs_3_), custom_call_target="tpu_custom_call" | custom-call | flops 3000000000 | bytes 10000000 | tf_op jit(solution)/shard_map/place/pallas_call | solution.py:573
  296.7 3.9 %place.5 = f32[192,2304]{1,0:T(8,128)} custom-call(s32[44]{0:T(128)} %get-tuple-element.291.refs_0_, bf16[4,24,2304]{2,1,0:T(8,128)(2,1)} %copy-done.22, bf16[4,24,2304]{2,1,0:T(8,128)(2,1)} %copy-done.36, f32[192,768]{1,0:T(8,128)} %get-tuple-element.131.refs_3_), custom_call_target="tpu_custom_call" | custom-call | flops 3000000000 | bytes 10000000 | tf_op jit(solution)/shard_map/place/pallas_call | solution.py:573
  (219 shorter events, 82.6 us)
Async XLA Ops:
  5.0 13.4 %collective-permute-start.4 = (bf16[96,2304]{1,0:T(8,128)(2,1)}, bf16[96,2304]{1,0:T(8,128)(2,1)}, u32[]{:S(2)}, u32[]{:S(2)}) collective-permute-start(bf16[96,2304]{1,0:T(8,128)(2,1)} %get-tuple-element.143.refs_4_), channel_id=1, source_target_pairs={{0,2},{1,3},{2,0},{3,1},{4,6},{5,7},{6,4},{7,5},{8,10},{9,11},{10,... | collective-permute-start | bytes 1327112 | tf_op jit(solution)/shard_map/ppermute | solution.py:111
  22.9 36.2 %collective-permute-start.9 = (bf16[192,3840]{1,0:T(8,128)(2,1)}, bf16[192,3840]{1,0:T(8,128)(2,1)S(1)}, u32[]{:S(2)}, u32[]{:S(2)}) collective-permute-start(bf16[192,3840]{1,0:T(8,128)(2,1)} %get-tuple-element.148.refs_5_), channel_id=1, source_target_pairs={{0,1},{1,0},{2,3},{3,2},{4,5},{5,4},{6,7},{7,6},{8,9},{9,8},{10,11... | collective-permute-start | bytes 4423688 | tf_op jit(solution)/shard_map/ppermute | solution.py:111
  23.9 18.3 %collective-permute-start.8 = (bf16[96,3840]{1,0:T(8,128)(2,1)}, bf16[96,3840]{1,0:T(8,128)(2,1)S(1)}, u32[]{:S(2)}, u32[]{:S(2)}) collective-permute-start(bf16[96,3840]{1,0:T(8,128)(2,1)} %get-tuple-element.150.refs_3_), channel_id=1, source_target_pairs={{0,2},{1,3},{2,0},{3,1},{4,6},{5,7},{6,4},{7,5},{8,10},{9,11},{10,... | collective-permute-start | bytes 2211848 | tf_op jit(solution)/shard_map/ppermute | solution.py:111
  42.2 11.6 %collective-permute-start.10 = (bf16[96,3840]{1,0:T(8,128)(2,1)S(1)}, bf16[96,3840]{1,0:T(8,128)(2,1)}, u32[]{:S(2)}, u32[]{:S(2)}) collective-permute-start(bf16[96,3840]{1,0:T(8,128)(2,1)S(1)} %collective-permute-done.8.refs_1_.refs_7_), channel_id=1, source_target_pairs={{0,4},{1,9},{2,6},{3,11},{4,0},{5,13},{6,2},{7,15},{8,12},{9,1},{1... | collective-permute-start | bytes 2211848 | tf_op jit(solution)/shard_map/ppermute | solution.py:111
  42.9 16.3 %collective-permute-start.11 = (bf16[96,3840]{1,0:T(8,128)(2,1)S(1)}, bf16[96,3840]{1,0:T(8,128)(2,1)}, u32[]{:S(2)}, u32[]{:S(2)}) collective-permute-start(bf16[96,3840]{1,0:T(8,128)(2,1)S(1)} %collective-permute-done.8.refs_1_.refs_7_), channel_id=1, source_target_pairs={{0,1},{1,0},{2,3},{3,2},{4,5},{5,4},{6,7},{7,6},{8,9},{9,8},{10,11... | collective-permute-start | bytes 2211848 | tf_op jit(solution)/shard_map/ppermute | solution.py:111
  54.1 36.9 %collective-permute-start.42 = (f32[1,28,24]{1,2,0:T(8,128)S(1)}, f32[1,28,24]{1,2,0:T(8,128)S(1)}, u32[]{:S(2)}, u32[]{:S(2)}) collective-permute-start(f32[1,28,24]{1,2,0:T(8,128)S(1)} %maximum_bitcast_fusion.1), channel_id=1, source_target_pairs={{0,24},{1,25},{2,26},{3,27},{4,28},{5,29},{6,30},{7,31},{8,16},{9,... | collective-permute-start | bytes 8072 | tf_op jit(solution)/shard_map/ppermute | solution.py:111
  57.6 20.6 %collective-permute-start.14 = (bf16[384,768]{1,0:T(8,128)(2,1)}, bf16[384,768]{1,0:T(8,128)(2,1)}, u32[]{:S(2)}, u32[]{:S(2)}) collective-permute-start(bf16[384,768]{1,0:T(8,128)(2,1)} %get-tuple-element.151.refs_10_), channel_id=1, source_target_pairs={{0,2},{1,3},{2,0},{3,1},{4,6},{5,7},{6,4},{7,5},{8,10},{9,11},{10,... | collective-permute-start | bytes 1769480 | tf_op jit(solution)/shard_map/ppermute | solution.py:111
  59.1 33.1 %collective-permute-start.13 = (bf16[768,768]{1,0:T(8,128)(2,1)S(1)}, bf16[768,768]{1,0:T(8,128)(2,1)}, u32[]{:S(2)}, u32[]{:S(2)}) collective-permute-start(bf16[768,768]{1,0:T(8,128)(2,1)S(1)} %copy-done.33), channel_id=1, source_target_pairs={{0,1},{1,0},{2,3},{3,2},{4,5},{5,4},{6,7},{7,6},{8,9},{9,8},{10,11... | collective-permute-start | bytes 3538952 | tf_op jit(solution)/shard_map/ppermute | solution.py:111
  79.7 12.6 %collective-permute-start.16 = (bf16[384,768]{1,0:T(8,128)(2,1)}, bf16[384,768]{1,0:T(8,128)(2,1)}, u32[]{:S(2)}, u32[]{:S(2)}) collective-permute-start(bf16[384,768]{1,0:T(8,128)(2,1)} %collective-permute-done.14.refs_5_.refs_7_), channel_id=1, source_target_pairs={{0,1},{1,0},{2,3},{3,2},{4,5},{5,4},{6,7},{7,6},{8,9},{9,8},{10,11... | collective-permute-start | bytes 1769480 | tf_op jit(solution)/shard_map/ppermute | solution.py:111
  89.4 12.5 %collective-permute-start.18 = (bf16[16,96,768]{2,1,0:T(8,128)(2,1)}, bf16[16,96,768]{2,1,0:T(8,128)(2,1)}, u32[]{:S(2)}, u32[]{:S(2)}) collective-permute-start(bf16[16,96,768]{2,1,0:T(8,128)(2,1)} %get-tuple-element.167), channel_id=1, source_target_pairs={{0,1},{1,0},{2,3},{3,2},{4,5},{5,4},{6,7},{7,6},{8,9},{9,8},{10,11... | collective-permute-start | bytes 7077896 | tf_op jit(solution)/shard_map/ppermute | solution.py:111
  92.2 81.0 %collective-permute-start.43 = (f32[2,28,24]{1,2,0:T(8,128)}, f32[2,28,24]{1,2,0:T(8,128)}, u32[]{:S(2)}, u32[]{:S(2)}) collective-permute-start(f32[2,28,24]{1,2,0:T(8,128)} %pad_maximum_fusion.2), channel_id=1, source_target_pairs={{0,8},{1,5},{2,10},{3,7},{4,12},{5,1},{6,14},{7,3},{8,0},{9,13},{1... | collective-permute-start | bytes 16136 | tf_op jit(solution)/shard_map/ppermute | solution.py:111
  103.5 22.5 %collective-permute-start.19 = (bf16[8,96,768]{2,1,0:T(8,128)(2,1)S(1)}, bf16[8,96,768]{2,1,0:T(8,128)(2,1)}, u32[]{:S(2)}, u32[]{:S(2)}) collective-permute-start(bf16[8,96,768]{2,1,0:T(8,128)(2,1)S(1)} %add_convert_fusion.1.refs_11_), channel_id=1, source_target_pairs={{0,2},{1,5},{2,0},{3,7},{4,6},{5,1},{6,4},{7,3},{8,10},{9,13},{10,... | collective-permute-start | bytes 3538952 | tf_op jit(solution)/shard_map/ppermute | solution.py:111
  125.0 19.9 %collective-permute-start.20 = (bf16[16,24,3840]{2,1,0:T(8,128)(2,1)}, bf16[16,24,3840]{2,1,0:T(8,128)(2,1)}, u32[]{:S(2)}, u32[]{:S(2)}) collective-permute-start(bf16[16,24,3840]{2,1,0:T(8,128)(2,1)} %get-tuple-element.174.refs_3_), channel_id=1, source_target_pairs={{0,1},{1,0},{2,3},{3,2},{4,5},{5,4},{6,7},{7,6},{8,9},{9,8},{10,11... | collective-permute-start | bytes 8847368 | tf_op jit(solution)/shard_map/ppermute | solution.py:111
  127.4 14.7 %collective-permute-start.21 = (bf16[4,96,768]{2,1,0:T(8,128)(2,1)S(1)}, bf16[4,96,768]{2,1,0:T(8,128)(2,1)}, u32[]{:S(2)}, u32[]{:S(2)}) collective-permute-start(bf16[4,96,768]{2,1,0:T(8,128)(2,1)S(1)} %add_convert_fusion.4.refs_2_), channel_id=1, source_target_pairs={{0,8},{1,3},{2,10},{3,1},{4,12},{5,7},{6,14},{7,5},{8,0},{9,11},{1... | collective-permute-start | bytes 1769480 | tf_op jit(solution)/shard_map/ppermute | solution.py:111
  143.5 18.9 %collective-permute-start.22 = (bf16[2,96,768]{2,1,0:T(8,128)(2,1)S(1)}, bf16[2,96,768]{2,1,0:T(8,128)(2,1)S(1)}, u32[]{:S(2)}, u32[]{:S(2)}) collective-permute-start(bf16[2,96,768]{2,1,0:T(8,128)(2,1)S(1)} %add_convert_fusion.7.refs_6_), channel_id=1, source_target_pairs={{0,4},{1,9},{2,6},{3,11},{4,0},{5,13},{6,2},{7,15},{8,12},{9,1},{1... | collective-permute-start | bytes 884744 | tf_op jit(solution)/shard_map/ppermute | solution.py:111
  147.7 33.0 %collective-permute-start.25 = (bf16[8,24,3840]{2,1,0:T(8,128)(2,1)}, bf16[8,24,3840]{2,1,0:T(8,128)(2,1)}, u32[]{:S(2)}, u32[]{:S(2)}) collective-permute-start(bf16[8,24,3840]{2,1,0:T(8,128)(2,1)} %add_convert_fusion.refs_5_), channel_id=1, source_target_pairs={{0,2},{1,5},{2,0},{3,7},{4,6},{5,1},{6,4},{7,3},{8,10},{9,13},{10,... | collective-permute-start | bytes 4423688 | tf_op jit(solution)/shard_map/ppermute | solution.py:111
  180.4 22.0 %collective-permute-start.27 = (bf16[1,96,768]{2,1,0:T(8,128)(2,1)S(1)}, bf16[1,96,768]{2,1,0:T(8,128)(2,1)}, u32[]{:S(2)}, u32[]{:S(2)}) collective-permute-start(bf16[1,96,768]{2,1,0:T(8,128)(2,1)S(1)} %copy-done.18), channel_id=1, source_target_pairs={{0,24},{1,25},{2,26},{3,27},{4,28},{5,29},{6,30},{7,31},{8,16},{9,... | collective-permute-start | bytes 442376 | tf_op jit(solution)/shard_map/ppermute | solution.py:111
  183.4 24.6 %collective-permute-start.26 = (bf16[4,24,3840]{2,1,0:T(8,128)(2,1)}, bf16[4,24,3840]{2,1,0:T(8,128)(2,1)}, u32[]{:S(2)}, u32[]{:S(2)}) collective-permute-start(bf16[4,24,3840]{2,1,0:T(8,128)(2,1)} %add_convert_fusion.3.refs_18_), channel_id=1, source_target_pairs={{0,8},{1,3},{2,10},{3,1},{4,12},{5,7},{6,14},{7,5},{8,0},{9,11},{1... | collective-permute-start | bytes 2211848 | tf_op jit(solution)/shard_map/ppermute | solution.py:111
  186.2 24.8 %collective-permute-start.24 = (bf16[8,24,2304]{2,1,0:T(8,128)(2,1)}, bf16[8,24,2304]{2,1,0:T(8,128)(2,1)}, u32[]{:S(2)}, u32[]{:S(2)}) collective-permute-start(bf16[8,24,2304]{2,1,0:T(8,128)(2,1)} %add_convert_fusion.2.refs_19_), channel_id=1, source_target_pairs={{0,2},{1,5},{2,0},{3,7},{4,6},{5,1},{6,4},{7,3},{8,10},{9,13},{10,... | collective-permute-start | bytes 2654216 | tf_op jit(solution)/shard_map/ppermute | solution.py:111
  202.4 24.1 %collective-permute-start.45 = (f32[16,768]{1,0:T(8,128)}, f32[16,768]{1,0:T(8,128)}, u32[]{:S(2)}, u32[]{:S(2)}) collective-permute-start(f32[16,768]{1,0:T(8,128)} %get-tuple-element.259.refs_14_), channel_id=1, source_target_pairs={{0,1},{1,0},{2,3},{3,2},{4,5},{5,4},{6,7},{7,6},{8,9},{9,8},{10,11... | collective-permute-start | bytes 147464 | tf_op jit(solution)/shard_map/ppermute | solution.py:111
  205.0 23.3 %collective-permute-start.39 = (bf16[1,96,768]{2,1,0:T(8,128)(2,1)S(1)}, bf16[1,96,768]{2,1,0:T(8,128)(2,1)}, u32[]{:S(2)}, u32[]{:S(2)}) collective-permute-start(bf16[1,96,768]{2,1,0:T(8,128)(2,1)S(1)} %get-tuple-element.253.refs_13_), channel_id=1, source_target_pairs={{0,24},{1,25},{2,26},{3,27},{4,28},{5,29},{6,30},{7,31},{8,16},{9,... | collective-permute-start | bytes 442376 | tf_op jit(solution)/shard_map/ppermute | solution.py:111
  210.1 21.2 %collective-permute-start.34 = (bf16[2,24,3840]{2,1,0:T(8,128)(2,1)}, bf16[2,24,3840]{2,1,0:T(8,128)(2,1)}, u32[]{:S(2)}, u32[]{:S(2)}) collective-permute-start(bf16[2,24,3840]{2,1,0:T(8,128)(2,1)} %add_convert_fusion.6.refs_12_), channel_id=1, source_target_pairs={{0,4},{1,9},{2,6},{3,11},{4,0},{5,13},{6,2},{7,15},{8,12},{9,1},{1... | collective-permute-start | bytes 1105928 | tf_op jit(solution)/shard_map/ppermute | solution.py:111
  212.4 21.0 %collective-permute-start.28 = (bf16[4,24,2304]{2,1,0:T(8,128)(2,1)S(1)}, bf16[4,24,2304]{2,1,0:T(8,128)(2,1)}, u32[]{:S(2)}, u32[]{:S(2)}) collective-permute-start(bf16[4,24,2304]{2,1,0:T(8,128)(2,1)S(1)} %add_convert_fusion.5.refs_11_), channel_id=1, source_target_pairs={{0,8},{1,3},{2,10},{3,1},{4,12},{5,7},{6,14},{7,5},{8,0},{9,11},{1... | collective-permute-start | bytes 1327112 | tf_op jit(solution)/shard_map/ppermute | solution.py:111
  234.8 16.5 %collective-permute-start.29 = (bf16[2,24,2304]{2,1,0:T(8,128)(2,1)S(1)}, bf16[2,24,2304]{2,1,0:T(8,128)(2,1)S(1)}, u32[]{:S(2)}, u32[]{:S(2)}) collective-permute-start(bf16[2,24,2304]{2,1,0:T(8,128)(2,1)S(1)} %add_convert_fusion.8), channel_id=1, source_target_pairs={{0,4},{1,9},{2,6},{3,11},{4,0},{5,13},{6,2},{7,15},{8,12},{9,1},{1... | collective-permute-start | bytes 663560 | tf_op jit(solution)/shard_map/ppermute | solution.py:111
  236.3 16.5 %collective-permute-start.47 = (f32[16,768]{1,0:T(8,128)S(1)}, f32[16,768]{1,0:T(8,128)S(1)}, u32[]{:S(2)}, u32[]{:S(2)}) collective-permute-start(f32[16,768]{1,0:T(8,128)S(1)} %add.333), channel_id=1, source_target_pairs={{0,4},{1,5},{2,6},{3,7},{4,0},{5,1},{6,2},{7,3},{8,12},{9,13},{10,... | collective-permute-start | bytes 147464 | tf_op jit(solution)/shard_map/ppermute | solution.py:111
  241.1 41.6 %collective-permute-start.41 = (bf16[4,96,768]{2,1,0:T(8,128)(2,1)S(1)}, bf16[4,96,768]{2,1,0:T(8,128)(2,1)}, u32[]{:S(2)}, u32[]{:S(2)}) collective-permute-start(bf16[4,96,768]{2,1,0:T(8,128)(2,1)S(1)} %constant_dynamic-update-slice_fusion.10.refs_1_), channel_id=1, source_target_pairs={{0,4},{1,9},{2,6},{3,11},{4,0},{5,13},{6,2},{7,15},{8,12},{9,1},{1... | collective-permute-start | bytes 1769480 | tf_op jit(solution)/shard_map/ppermute | solution.py:111
  252.8 12.8 %collective-permute-start.48 = (f32[16,768]{1,0:T(8,128)S(1)}, f32[16,768]{1,0:T(8,128)S(1)}, u32[]{:S(2)}, u32[]{:S(2)}) collective-permute-start(f32[16,768]{1,0:T(8,128)S(1)} %add.334), channel_id=1, source_target_pairs={{0,8},{1,9},{2,10},{3,11},{4,12},{5,13},{6,14},{7,15},{8,0},{9,1},... | collective-permute-start | bytes 147464 | tf_op jit(solution)/shard_map/ppermute | solution.py:111
  262.1 15.9 %collective-permute-start.37 = (bf16[2,24,3840]{2,1,0:T(8,128)(2,1)S(1)}, bf16[2,24,3840]{2,1,0:T(8,128)(2,1)S(1)}, u32[]{:S(2)}, u32[]{:S(2)}) collective-permute-start(bf16[2,24,3840]{2,1,0:T(8,128)(2,1)S(1)} %constant_dynamic-update-slice_fusion.4), channel_id=1, source_target_pairs={{0,8},{1,5},{2,10},{3,7},{4,12},{5,1},{6,14},{7,3},{8,0},{9,13},{1... | collective-permute-start | bytes 1105928 | tf_op jit(solution)/shard_map/ppermute | solution.py:111
  265.6 11.0 %collective-permute-start.49 = (f32[16,768]{1,0:T(8,128)S(1)}, f32[16,768]{1,0:T(8,128)S(1)}, u32[]{:S(2)}, u32[]{:S(2)}) collective-permute-start(f32[16,768]{1,0:T(8,128)S(1)} %add.335), channel_id=1, source_target_pairs={{0,24},{1,25},{2,26},{3,27},{4,28},{5,29},{6,30},{7,31},{8,16},{9,... | collective-permute-start | bytes 147464 | tf_op jit(solution)/shard_map/ppermute | solution.py:111
  268.0 12.1 %collective-permute-start.32 = (bf16[2,24,2304]{2,1,0:T(8,128)(2,1)S(1)}, bf16[2,24,2304]{2,1,0:T(8,128)(2,1)S(1)}, u32[]{:S(2)}, u32[]{:S(2)}) collective-permute-start(bf16[2,24,2304]{2,1,0:T(8,128)(2,1)S(1)} %constant_dynamic-update-slice_fusion), channel_id=1, source_target_pairs={{0,8},{1,5},{2,10},{3,7},{4,12},{5,1},{6,14},{7,3},{8,0},{9,13},{1... | collective-permute-start | bytes 663560 | tf_op jit(solution)/shard_map/ppermute | solution.py:111
  278.0 11.5 %collective-permute-start.38 = (bf16[4,24,3840]{2,1,0:T(8,128)(2,1)S(1)}, bf16[4,24,3840]{2,1,0:T(8,128)(2,1)S(1)}, u32[]{:S(2)}, u32[]{:S(2)}) collective-permute-start(bf16[4,24,3840]{2,1,0:T(8,128)(2,1)S(1)} %constant_dynamic-update-slice_fusion.6.refs_1_), channel_id=1, source_target_pairs={{0,4},{1,9},{2,6},{3,11},{4,0},{5,13},{6,2},{7,15},{8,12},{9,1},{1... | collective-permute-start | bytes 2211848 | tf_op jit(solution)/shard_map/ppermute | solution.py:111
  280.2 15.7 %collective-permute-start.33 = (bf16[4,24,2304]{2,1,0:T(8,128)(2,1)S(1)}, bf16[4,24,2304]{2,1,0:T(8,128)(2,1)S(1)}, u32[]{:S(2)}, u32[]{:S(2)}) collective-permute-start(bf16[4,24,2304]{2,1,0:T(8,128)(2,1)S(1)} %constant_dynamic-update-slice_fusion.2.refs_3_.refs_1_), channel_id=1, source_target_pairs={{0,4},{1,9},{2,6},{3,11},{4,0},{5,13},{6,2},{7,15},{8,12},{9,1},{1... | collective-permute-start | bytes 1327112 | tf_op jit(solution)/shard_map/ppermute | solution.py:111
  (55 other events, 471.7 us)
